TPU v7x, 128 devices: a whole 4x4x4 slice. The times are simulated.
128 devices in a mesh: mem: 4 (over z_lo, core), lat: 8 (over y, z_hi), lon: 4 (over x).
Axes of the slice: x: 4, y: 4, z: 4 (z_hi: 2, z_lo: 2; z = z_hi * 2 + z_lo), core: 2. Of those that a mesh axis runs over, the one named last changes fastest.
Arguments:
- perturbations: bfloat16 [16, 8, 512, 1024], P('mem', None, 'lat', 'lon'), may hold values from -6 to 6
- increment: float32 [8, 512, 1024], P(None, 'lat', 'lon'), may hold values from -6 to 6
- taper_norm: float32 [8, 512, 1024], P(None, 'lat', 'lon'), may hold values from 1.5 to 6
- kappa: float32 [8], replicated, may hold values from 0.3 to 8
Outputs:
- covariance_product: float32 [8, 512, 1024], P('mem', 'lat', 'lon')
All inputs are finite; a program needn't handle non-finite values.
Results may differ from a plain program's by a relative error of at most 0.0003.
Values may be sent and summed in bfloat16 or wider, within the bound.
No kernel may reach another device: no remote copies, remote signals or barrier semaphores. Data moves between devices by JAX's collectives and lax.ppermute only.
A program may use at most 64 MiB of HBM per device.

v0:
```python
import numpy as np
import jax
import jax.numpy as jnp
from jax import lax
from jax.experimental import pallas as pl
from jax.experimental.pallas import tpu as pltpu
from jax.sharding import PartitionSpec as P

PASSES = 8
HALO = 2 * PASSES
LANES = 128
BLOCK = 8
BF16 = jnp.bfloat16
F32 = jnp.float32


def roll(x, shift):
    shift = shift % LANES
    return pltpu.roll(x, shift, x.ndim - 1) if shift else x


def lane_of(shape):
    return lax.broadcasted_iota(jnp.int32, shape, len(shape) - 1)


def split(value):
    hi = value.astype(BF16)
    return hi, (value - hi.astype(F32)).astype(BF16)


def selectors(members, cols):
    chunks = LANES // members
    fine = (cols + 2 * HALO) // chunks
    lane = np.arange(fine * LANES)
    member, chunk = lane % LANES // chunks, lane % chunks
    column = fine * chunk + lane // LANES - HALO
    before, after = column < 0, column >= cols

    def one_hot(count, target):
        return np.arange(count)[:, None] == target[None, :]

    packs = members * cols
    field = np.where(
        before, packs + HALO * member + column + HALO,
        np.where(after, packs + LANES + HALO * member + column - cols, cols * member + column),
    )
    to_fields = one_hot(packs + 2 * LANES, field)

    def weights(part):
        first = HALO * (members + part)
        return np.where(
            before, 2 * cols + first + column + HALO,
            np.where(after, 2 * cols + LANES + first + column - cols, part * cols + column),
        )

    count = 2 * cols + 2 * LANES
    to_weights = one_hot(count, weights(0)) | one_hot(count, weights(1))
    back = one_hot(cols, column).T
    return [m.astype(np.float32).astype(BF16) for m in (to_fields, to_weights, back)]


def pack_kernel(p, increment, taper, up, down, to_left, to_right):
    members, _, rows, cols = p.shape

    def edge(pick, out):
        for m in range(members):
            out[m] = p[m, :, pick, :]
        hi, lo = split(increment[:, pick, :] * taper[:, pick, :])
        out[members] = hi
        out[members + 1] = lo

    edge(slice(0, HALO), up)
    edge(slice(rows - HALO, rows), down)

    def packed(pick, column, shift):
        fields = [p[m, :, pick, column].astype(F32) for m in range(members)]
        hi, lo = split(increment[:, pick, column] * taper[:, pick, column])
        fields += [hi.astype(F32), lo.astype(F32)]
        lane = lane_of(fields[0].shape)
        total = jnp.zeros_like(fields[0])
        for e, field in enumerate(fields):
            inside = (lane >= HALO * e) & (lane < HALO * (e + 1))
            total = jnp.where(inside, roll(field, shift + HALO * e), total)
        return total.astype(BF16)

    def chunk(i, _):
        pick = pl.ds(pl.multiple_of(i * HALO, HALO), HALO)
        to_left[:, pick, :] = packed(pick, slice(0, LANES), 0)
        to_right[:, pick, :] = packed(pick, slice(cols - LANES, cols), HALO)
        return 0

    lax.fori_loop(0, rows // HALO, chunk, 0)


def turned(value):
    levels, rows, lanes = value.shape
    return jnp.swapaxes(value.astype(F32), 0, 1).reshape(rows * levels, lanes)


def row_of(ref, *where):
    return lambda c: ref[(*where, c + 2)]


def first_sweep(x, x_next, v, linear, fine):
    v_next = {c: x(c) + x_next(c + 1) for c in range(-2, fine + 1)}
    if v is None:
        return v_next, None
    u = {c: linear * x(c) + v[c] + v_next[c - 1] for c in range(-1, fine + 1)}
    return v_next, u


def second_sweep(x, u, u_next, q, constant, fine):
    q_next = {c: u[c] + u_next[c + 1] for c in range(-1, fine)}
    if q is None:
        return q_next, None
    return q_next, [constant * x(c) + q[c] + q_next[c - 1] for c in range(fine)]


def wrap_columns(source, target, fine):
    for c in (0, 1):
        target(fine + c, roll(source(c), -1))
        target(c - 2, roll(source(fine - 2 + c), 1))


def finish(sums, back, scale, taper_of, write, levels):
    hi, lo = split(sums)
    total = jnp.dot(hi, back, preferred_element_type=F32) + jnp.dot(lo, back, preferred_element_type=F32)
    count = total.shape[0] // levels
    for half in range(total.shape[1] // LANES):
        lanes = slice(half * LANES, (half + 1) * LANES)
        part = total[:, lanes].reshape(count, levels, LANES) * scale
        natural = jnp.swapaxes(part, 0, 1) * taper_of(lanes)
        write(natural, lanes)


def to_owner(place, natural, keep, send, pick, lanes, levels):
    core, plane = place[2], place[3]
    for level in range(levels):
        owner_plane, owner_core, within = level // 4, level // 2 % 2, level % 2
        slot = jnp.where(plane == owner_plane, 0, 2) + within

        @pl.when(core == owner_core)
        def _():
            keep[slot, pick, lanes] = natural[level]

        @pl.when(core != owner_core)
        def _():
            send[slot, pick, lanes] = natural[level]


def inner_kernel(
    place, p, increment, taper, left, right, to_fields, to_weights, back, coef,
    keep, send, edges, edge_values,
    x, values, fields, weights,
):
    members, levels, rows, cols = p.shape
    fine = x.shape[1] - 4

    def gather(i, _):
        pick = pl.ds(pl.multiple_of(i * HALO, HALO), HALO)
        out = pl.ds(pl.multiple_of(i * HALO * levels, HALO * levels), HALO * levels)
        for half in range(cols // LANES):
            lanes = slice(half * LANES, (half + 1) * LANES)
            for m in range(members):
                fields[out, m * cols + half * LANES : m * cols + (half + 1) * LANES] = turned(
                    p[m, :, pick, lanes]
                ).astype(BF16)
            hi, lo = split(turned(increment[:, pick, lanes] * taper[:, pick, lanes]))
            weights[out, lanes] = hi
            weights[out, cols + half * LANES : cols + (half + 1) * LANES] = lo
        for side, ref in enumerate((left, right)):
            value = turned(ref[:, pick, :]).astype(BF16)
            fields[out, members * cols + side * LANES : members * cols + (side + 1) * LANES] = value
            weights[out, 2 * cols + side * LANES : 2 * cols + (side + 1) * LANES] = value
        return 0

    lax.fori_loop(0, rows // HALO, gather, 0)
    for first in range(0, fine, 2):
        width = min(2, fine - first)
        lanes = slice(first * LANES, (first + width) * LANES)
        field = jnp.dot(fields[...], to_fields[:, lanes], preferred_element_type=F32)
        weight = jnp.dot(weights[...], to_weights[:, lanes], preferred_element_type=F32)
        for k in range(width):
            pick = slice(k * LANES, (k + 1) * LANES)
            value = field[:, pick].reshape(rows, levels, LANES)
            values[:, first + k] = value
            x[:, 2 + first + k] = value * weight[:, pick].reshape(rows, levels, LANES)
    for k in range(HALO):
        edge_values[0, k] = values[k]
        edge_values[1, k] = values[rows - 1 - k]

    linear, constant = coef[0], coef[1]

    def wrap(row):
        def target(c, value):
            x[row, c + 2] = value

        wrap_columns(row_of(x, row), target, fine)

    def wrap_first(row, _):
        wrap(row)
        return 0

    lax.fori_loop(0, rows, wrap_first, 0, unroll=BLOCK)

    for turn in range(PASSES):
        low = 2 * turn
        start, count = low + 2, rows - 4 * turn - 4
        for k in range(4):
            edges[0, turn, k] = x[low + k]
            edges[1, turn, k] = x[rows - 1 - low - k]

        v, _ = first_sweep(row_of(x, start - 2), row_of(x, start - 1), None, linear, fine)
        v, u = first_sweep(row_of(x, start - 1), row_of(x, start), v, linear, fine)
        v, u_next = first_sweep(row_of(x, start), row_of(x, start + 1), v, linear, fine)
        q, _ = second_sweep(None, u, u_next, None, constant, fine)
        u = u_next
        keys = tuple(list(part) for part in (v, u, q))

        def rows_at(first, number, carry):
            v, u, q = (dict(zip(k, part)) for k, part in zip(keys, carry))
            for k in range(number):
                i = first + k
                v, u_next = first_sweep(row_of(x, i + 1), row_of(x, i + 2), v, linear, fine)
                q, y = second_sweep(row_of(x, i), u, u_next, q, constant, fine)
                u = u_next
                for c in range(fine):
                    x[i, c + 2] = y[c]
            return tuple([part[c] for c in k] for k, part in zip(keys, (v, u, q)))

        def block(b, carry):
            first = start + b * BLOCK
            carry = rows_at(first, BLOCK, carry)
            @pl.when(b > 0)
            def _():
                for k in range(BLOCK):
                    wrap(first - BLOCK + k)
            return carry

        carry = tuple([part[c] for c in k] for k, part in zip(keys, (v, u, q)))
        whole = count // BLOCK
        carry = lax.fori_loop(0, whole, block, carry)
        rest = count - whole * BLOCK
        if rest:
            rows_at(start + whole * BLOCK, rest, carry)
        for row in range(start + (whole - 1) * BLOCK, start + count):
            wrap(row)

    scale = coef[2]

    def last(i, _):
        first = i * HALO
        from_row = first + HALO
        product = jnp.concatenate(
            [
                (x[pl.ds(from_row, HALO), c + 2] * values[pl.ds(from_row, HALO), c]).reshape(HALO * levels, LANES)
                for c in range(fine)
            ],
            axis=1,
        )
        pick = pl.ds(pl.multiple_of(first, HALO), HALO)
        finish(
            product, back[...], scale,
            lambda lanes: taper[:, pl.ds(pl.multiple_of(from_row, HALO), HALO), lanes],
            lambda natural, lanes: to_owner(place, natural, keep, send, pick, lanes, levels),
            levels,
        )
        return 0

    lax.fori_loop(0, (rows - 2 * HALO) // HALO, last, 0)


def outer_kernel(
    place, taper, top, bottom, top_side, bottom_side, edges, edge_values, to_fields, to_weights, back, coef,
    keep, send,
    x, fields, weights,
):
    _, levels, _, cols = top.shape
    members = top.shape[0] - 2
    fine = edge_values.shape[2]
    size = HALO * levels
    for edge, (strip, side) in enumerate(((top, top_side), (bottom, bottom_side))):
        out = slice(edge * size, (edge + 1) * size)
        for half in range(cols // LANES):
            lanes = slice(half * LANES, (half + 1) * LANES)
            for m in range(members + 2):
                value = turned(strip[m, :, :, lanes]).astype(BF16)
                ref, base = (fields, m * cols) if m < members else (weights, (m - members) * cols)
                ref[out, base + half * LANES : base + (half + 1) * LANES] = value
        for k in range(2):
            value = turned(side[k]).astype(BF16)
            fields[out, members * cols + k * LANES : members * cols + (k + 1) * LANES] = value
            weights[out, 2 * cols + k * LANES : 2 * cols + (k + 1) * LANES] = value
    for first in range(0, fine, 2):
        width = min(2, fine - first)
        lanes = slice(first * LANES, (first + width) * LANES)
        both = jnp.dot(fields[...], to_fields[:, lanes], preferred_element_type=F32) * jnp.dot(
            weights[...], to_weights[:, lanes], preferred_element_type=F32
        )
        for k in range(width):
            part = both[:, k * LANES : (k + 1) * LANES].reshape(2, HALO, levels, LANES)
            for row in range(HALO):
                x[0, row, 2 + first + k] = part[0, row]
                x[1, HALO - 1 - row, 2 + first + k] = part[1, row]

    linear, constant = coef[0], coef[1]
    inside = [jnp.where(place[edge] == 1, 0.0, 1.0).astype(F32) for edge in range(2)]

    def wrap(edge, row):
        def target(c, value):
            x[edge, row, c + 2] = value

        wrap_columns(row_of(x, edge, row), target, fine)

    for row in range(HALO):
        for edge in range(2):
            wrap(edge, row)

    for turn in range(PASSES):
        low = 2 * turn
        for edge in range(2):
            def row_at(row):
                if row < low + HALO:
                    return row_of(x, edge, row)
                return row_of(edges, edge, turn, row - low - HALO)

            v = u = q = None
            for i in range(low, low + HALO + 3):
                v, u_next = first_sweep(row_at(i), row_at(i + 1), v, linear, fine)
                if u_next is None:
                    continue
                if i == HALO - 1:
                    u_next = {c: part * inside[edge] for c, part in u_next.items()}
                if u is not None:
                    q, y = second_sweep(row_at(i - 1), u, u_next, q, constant, fine)
                    if y is not None:
                        for c in range(fine):
                            x[edge, i - 1, c + 2] = y[c] * inside[edge] if i == HALO else y[c]
                u = u_next
            if turn < PASSES - 1:
                for row in range(low + 2, low + HALO + 2):
                    wrap(edge, row)

    scale = coef[2]
    rows = taper.shape[1]
    for edge in range(2):
        order = range(HALO) if edge == 0 else range(HALO - 1, -1, -1)
        product = jnp.concatenate(
            [
                jnp.concatenate([x[edge, HALO + k, c + 2] * edge_values[edge, k, c] for k in order], axis=0)
                for c in range(fine)
            ],
            axis=1,
        )
        pick = slice(edge * HALO, (edge + 1) * HALO)
        own = slice(edge * (rows - HALO), edge * (rows - HALO) + HALO)
        finish(
            product, back[...], scale,
            lambda lanes: taper[:, own, lanes],
            lambda natural, lanes: to_owner(place, natural, keep, send, pick, lanes, levels),
            levels,
        )


def shifted(value, axis, step, wrap):
    count = lax.axis_size(axis)
    pairs = [(i, (i + step) % count) for i in range(count) if wrap or 0 <= i + step < count]
    return lax.ppermute(value, axis, pairs)


def total_over_members(keep, send):
    got = lax.ppermute(send, "mem", [(i, i ^ 1) for i in range(4)])
    crossing = lax.ppermute(keep[2:] + got[2:], "mem", [(i, i ^ 2) for i in range(4)])
    return keep[:2] + got[:2] + crossing


def local(perturbations, increment, taper_norm, kappa):
    members, levels, rows, cols = perturbations.shape
    fine = (cols + 2 * HALO) * members // LANES
    shape = jax.ShapeDtypeStruct
    strip = shape((members + 2, levels, HALO, cols), BF16)
    pack = shape((levels, rows, LANES), BF16)
    big = pltpu.CompilerParams(vmem_limit_bytes=40 * 1024 * 1024)
    vmem = pl.BlockSpec(memory_space=pltpu.VMEM)
    smem = pl.BlockSpec(memory_space=pltpu.SMEM)

    up, down, to_left, to_right = pl.pallas_call(
        pack_kernel, out_shape=(strip, strip, pack, pack), compiler_params=big, name="pack"
    )(perturbations, increment, taper_norm)

    left = shifted(to_right, "lon", 1, True)
    right = shifted(to_left, "lon", -1, True)
    top = shifted(down, "lat", 1, False)
    bottom = shifted(up, "lat", -1, False)
    top_side = shifted(jnp.stack([left[:, -HALO:], right[:, -HALO:]]), "lat", 1, False)
    bottom_side = shifted(jnp.stack([left[:, :HALO], right[:, :HALO]]), "lat", -1, False)

    denominator = 1.0 + 4.0 * kappa
    count = members * lax.axis_size("mem")
    coef = jnp.stack([
        1.0 / kappa,
        denominator / (kappa * kappa),
        (kappa / denominator) ** (2 * PASSES) / (count - 1),
    ])
    coef = jnp.broadcast_to(coef[:, :, None], (3, levels, LANES))
    lat, mem = lax.axis_index("lat"), lax.axis_index("mem")
    place = jnp.stack([
        (lat == 0).astype(jnp.int32),
        (lat == lax.axis_size("lat") - 1).astype(jnp.int32),
        mem % 2,
        mem // 2,
    ])
    to_fields, to_weights, back = (jnp.asarray(m) for m in selectors(members, cols))

    tile = (levels, LANES)
    inner_rows = rows - 2 * HALO
    keep, send, edges, edge_values = pl.pallas_call(
        inner_kernel,
        out_shape=(
            shape((levels // 2, inner_rows, cols), F32),
            shape((levels // 2, inner_rows, cols), F32),
            shape((2, PASSES, 4, fine + 4, *tile), F32),
            shape((2, HALO, fine, *tile), F32),
        ),
        in_specs=[smem] + [vmem] * 9,
        out_specs=(vmem,) * 4,
        scratch_shapes=[
            pltpu.VMEM((rows, fine + 4, *tile), F32),
            pltpu.VMEM((rows, fine, *tile), F32),
            pltpu.VMEM((rows * levels, members * cols + 2 * LANES), BF16),
            pltpu.VMEM((rows * levels, 2 * cols + 2 * LANES), BF16),
        ],
        compiler_params=big,
        name="inner",
    )(place, perturbations, increment, taper_norm, left, right, to_fields, to_weights, back, coef)
    middle = total_over_members(keep, send)

    keep, send = pl.pallas_call(
        outer_kernel,
        out_shape=(shape((levels // 2, 2 * HALO, cols), F32),) * 2,
        in_specs=[smem] + [vmem] * 11,
        out_specs=(vmem,) * 2,
        scratch_shapes=[
            pltpu.VMEM((2, 2 * HALO, fine + 4, *tile), F32),
            pltpu.VMEM((2 * HALO * levels, members * cols + 2 * LANES), BF16),
            pltpu.VMEM((2 * HALO * levels, 2 * cols + 2 * LANES), BF16),
        ],
        compiler_params=big,
        name="outer",
    )(place, taper_norm, top, bottom, top_side, bottom_side, edges, edge_values, to_fields, to_weights, back, coef)
    outside = total_over_members(keep, send)
    return jnp.concatenate([outside[:, :HALO], middle, outside[:, HALO:]], axis=1)


def solution(mesh):
    return jax.shard_map(
        local,
        mesh=mesh,
        in_specs=(P("mem", None, "lat", "lon"), P(None, "lat", "lon"), P(None, "lat", "lon"), P()),
        out_specs=P("mem", "lat", "lon"),
        check_vma=False,
    )
```

profile of v0, /device:TPU:1, one launch (start us, length us, event | category | flops | bytes accessed | tf_op | source)
XLA Modules:
  0.0 64.1 jit_solution(10135323272599087795)
XLA Ops:
  0.0 1.2 %copy-done.3 = f32[8,64,256]{2,1,0:T(8,128)S(1)} copy-done((f32[8,64,256]{2,1,0:T(8,128)S(1)}, f32[8,64,256]{2,1,0:T(8,128)}, u32[]{:S(2)}) %copy-start.3) | copy-done | bytes 524312
  1.2 1.2 %copy-done.5 = bf16[4,8,64,256]{3,2,1,0:T(8,128)(2,1)S(1)} copy-done((bf16[4,8,64,256]{3,2,1,0:T(8,128)(2,1)S(1)}, bf16[4,8,64,256]{3,2,1,0:T(8,128)(2,1)}, u32[]{:S(2)}) %copy-start.5) | copy-done | bytes 1048600
  2.4 1.0 %copy-done.9 = f32[8,64,256]{2,1,0:T(8,128)S(1)} copy-done((f32[8,64,256]{2,1,0:T(8,128)S(1)}, f32[8,64,256]{2,1,0:T(8,128)}, u32[]{:S(2)}) %copy-start.9) | copy-done | bytes 524312
  3.4 1.6 %pack.1 = (bf16[6,8,16,256]{3,2,1,0:T(8,128)(2,1)}, bf16[6,8,16,256]{3,2,1,0:T(8,128)(2,1)}, bf16[8,64,128]{2,1,0:T(8,128)(2,1)S(1)}, bf16[8,64,128]{2,1,0:T(8,128)(2,1)}) custom-call(bf16[4,8,64,256]{3,2,1,0:T(8,128)(2,1)S(1)} %copy-done.5, f32[8,64,256]{2,1,0:T(8,128)S(1)} %copy-done.9, f32[8,64,256]{2,1,0:T(8,128)S(1)} %copy-done.3), custom_call_target="tpu_custom_call" | custom-call | tf_op jit(solution)/shard_map/pack/pallas_call | solution.py:387
  5.0 2.0 %collective-permute-start.2 = (bf16[8,64,128]{2,1,0:T(8,128)(2,1)}, bf16[8,64,128]{2,1,0:T(8,128)(2,1)S(1)}, u32[]{:S(2)}, u32[]{:S(2)}) collective-permute-start(bf16[8,64,128]{2,1,0:T(8,128)(2,1)} %get-tuple-element.17), channel_id=1, source_target_pairs={{0,1},{1,2},{2,3},{3,0},{4,5},{5,6},{6,7},{7,4},{8,9},{9,10},{10,1... | collective-permute-start | bytes 393224 | tf_op jit(solution)/shard_map/ppermute | solution.py:368
  7.1 1.3 %collective-permute-start.3 = (bf16[8,64,128]{2,1,0:T(8,128)(2,1)S(1)}, bf16[8,64,128]{2,1,0:T(8,128)(2,1)S(1)}, u32[]{:S(2)}, u32[]{:S(2)}) collective-permute-start(bf16[8,64,128]{2,1,0:T(8,128)(2,1)S(1)} %get-tuple-element.18), channel_id=1, source_target_pairs={{0,3},{1,0},{2,1},{3,2},{4,7},{5,4},{6,5},{7,6},{8,11},{9,8},{10,9... | collective-permute-start | bytes 393224 | tf_op jit(solution)/shard_map/ppermute | solution.py:368
  8.3 5.7 %collective-permute-start = (bf16[6,8,16,256]{3,2,1,0:T(8,128)(2,1)}, bf16[6,8,16,256]{3,2,1,0:T(8,128)(2,1)S(1)}, u32[]{:S(2)}, u32[]{:S(2)}) collective-permute-start(bf16[6,8,16,256]{3,2,1,0:T(8,128)(2,1)} %get-tuple-element.15), channel_id=1, source_target_pairs={{0,4},{4,8},{8,12},{12,16},{16,20},{20,24},{24,28},{1,5},{5,9},{9,... | collective-permute-start | bytes 1179656 | tf_op jit(solution)/shard_map/ppermute | solution.py:368
  14.0 1.3 %collective-permute-start.1 = (bf16[6,8,16,256]{3,2,1,0:T(8,128)(2,1)}, bf16[6,8,16,256]{3,2,1,0:T(8,128)(2,1)S(1)}, u32[]{:S(2)}, u32[]{:S(2)}) collective-permute-start(bf16[6,8,16,256]{3,2,1,0:T(8,128)(2,1)} %get-tuple-element.16), channel_id=1, source_target_pairs={{4,0},{8,4},{12,8},{16,12},{20,16},{24,20},{28,24},{5,1},{9,5},{13... | collective-permute-start | bytes 1179656 | tf_op jit(solution)/shard_map/ppermute | solution.py:368
  15.4 0.7 %divide_bitcast_fusion = (f32[1,8]{1,0:T(1,128)S(1)}, f32[1,8]{1,0:T(1,128)S(1)}, f32[1,8]{1,0:T(1,128)S(1)}) fusion(f32[8]{0:T(128)} %param.10), kind=kLoop, calls=%fused_computation.19 | loop fusion | flops 88 | bytes 128 | tf_op jit(solution)/shard_map/stack | solution.py:400
  16.2 5.5 %collective-permute-start.4 = (bf16[2,8,16,128]{3,2,1,0:T(8,128)(2,1)S(1)}, bf16[2,8,16,128]{3,2,1,0:T(8,128)(2,1)S(1)}, u32[]{:S(2)}, u32[]{:S(2)}) collective-permute-start(bf16[2,8,16,128]{3,2,1,0:T(8,128)(2,1)S(1)} %pad_maximum_fusion.1), channel_id=1, source_target_pairs={{0,4},{4,8},{8,12},{12,16},{16,20},{20,24},{24,28},{1,5},{5,9},{9,... | collective-permute-start | bytes 196616 | tf_op jit(solution)/shard_map/ppermute | solution.py:368
  21.8 1.8 %copy-done = bf16[1280,1152]{1,0:T(8,128)(2,1)S(1)} copy-done((bf16[1280,1152]{1,0:T(8,128)(2,1)S(1)}, bf16[1280,1152]{1,0:T(8,128)(2,1)}, u32[]{:S(2)}) %copy-start) | copy-done | bytes 2949144
  23.6 1.2 %copy-done.6 = bf16[4,8,64,256]{3,2,1,0:T(8,128)(2,1)S(1)} copy-done((bf16[4,8,64,256]{3,2,1,0:T(8,128)(2,1)S(1)}, bf16[4,8,64,256]{3,2,1,0:T(8,128)(2,1)}, u32[]{:S(2)}) %copy-start.6) | copy-done | bytes 1048600
  24.8 1.1 %copy-done.7 = bf16[1152,256]{1,0:T(8,128)(2,1)S(1)} copy-done((bf16[1152,256]{1,0:T(8,128)(2,1)S(1)}, bf16[1152,256]{1,0:T(8,128)(2,1)}, u32[]{:S(2)}) %copy-start.7) | copy-done | bytes 589848
  25.9 1.0 %copy-done.10 = f32[8,64,256]{2,1,0:T(8,128)S(1)} copy-done((f32[8,64,256]{2,1,0:T(8,128)S(1)}, f32[8,64,256]{2,1,0:T(8,128)}, u32[]{:S(2)}) %copy-start.10) | copy-done | bytes 524312
  26.9 14.9 %inner.1 = (f32[4,32,256]{2,1,0:T(8,128)S(1)}, f32[4,32,256]{2,1,0:T(8,128)S(1)}, f32[2,8,4,13,8,128]{5,4,3,2,1,0:T(8,128)S(1)}, f32[2,16,9,8,128]{4,3,2,1,0:T(8,128)S(1)}) custom-call(s32[4]{0:T(128)S(1)} %pad_add_fusion.place, bf16[4,8,64,256]{3,2,1,0:T(8,128)(2,1)S(1)} %copy-done.6, f32[8,64,256]{2,1,0:T(8,128)S(1)} %copy-done.10, ...), custom_call_target="tpu_custom_call" | custom-call | tf_op jit(solution)/shard_map/inner/pallas_call | solution.py:417
  41.8 2.2 %collective-permute-start.8 = (f32[4,32,256]{2,1,0:T(8,128)S(1)}, f32[4,32,256]{2,1,0:T(8,128)S(1)}, u32[]{:S(2)}, u32[]{:S(2)}) collective-permute-start(f32[4,32,256]{2,1,0:T(8,128)S(1)} %get-tuple-element.24), channel_id=1, source_target_pairs={{0,32},{32,0},{64,96},{96,64},{1,33},{33,1},{65,97},{97,65},{2,34}... | collective-permute-start | bytes 393224 | tf_op jit(solution)/shard_map/ppermute | solution.py:372
  44.0 1.3 %collective-permute-start.5 = (bf16[2,8,16,128]{3,2,1,0:T(8,128)(2,1)S(1)}, bf16[2,8,16,128]{3,2,1,0:T(8,128)(2,1)S(1)}, u32[]{:S(2)}, u32[]{:S(2)}) collective-permute-start(bf16[2,8,16,128]{3,2,1,0:T(8,128)(2,1)S(1)} %pad_maximum_fusion.2), channel_id=1, source_target_pairs={{4,0},{8,4},{12,8},{16,12},{20,16},{24,20},{28,24},{5,1},{9,5},{13... | collective-permute-start | bytes 196616 | tf_op jit(solution)/shard_map/ppermute | solution.py:368
  45.3 5.8 %collective-permute-done.5.bottom_side = bf16[2,8,16,128]{3,2,1,0:T(8,128)(2,1)S(1)} collective-permute-done((bf16[2,8,16,128]{3,2,1,0:T(8,128)(2,1)S(1)}, bf16[2,8,16,128]{3,2,1,0:T(8,128)(2,1)S(1)}, u32[]{:S(2)}, u32[]{:S(2)}) %collective-permute-start.5) | collective-permute-done | bytes 65568 | tf_op jit(solution)/shard_map/ppermute | solution.py:368
  51.1 6.2 %outer.1 = (f32[4,32,256]{2,1,0:T(8,128)S(1)}, f32[4,32,256]{2,1,0:T(8,128)S(1)}) custom-call(s32[4]{0:T(128)S(1)} %pad_add_fusion.place, f32[8,64,256]{2,1,0:T(8,128)S(1)} %copy-done.4, bf16[6,8,16,256]{3,2,1,0:T(8,128)(2,1)S(1)} %collective-permute-done.top, bf16[6,8,16,256]{3,2,1,0:T(8,128)(2,1)S(1)} %collective-permute-done.1.bottom, ...), custom_call_target="tpu_custom_call" | custom-call | tf_op jit(solution)/shard_map/outer/pallas_call | solution.py:438
  57.3 0.9 %collective-permute-start.6 = (f32[4,32,256]{2,1,0:T(8,128)S(1)}, f32[4,32,256]{2,1,0:T(8,128)S(1)}, u32[]{:S(2)}, u32[]{:S(2)}) collective-permute-start(f32[4,32,256]{2,1,0:T(8,128)S(1)} %get-tuple-element.22), channel_id=1, source_target_pairs={{0,32},{32,0},{64,96},{96,64},{1,33},{33,1},{65,97},{97,65},{2,34}... | collective-permute-start | bytes 393224 | tf_op jit(solution)/shard_map/ppermute | solution.py:372
  58.2 0.8 %collective-permute-start.9 = (f32[2,32,256]{2,1,0:T(8,128)S(1)}, f32[2,32,256]{2,1,0:T(8,128)S(1)}, u32[]{:S(2)}, u32[]{:S(2)}) collective-permute-start(f32[2,32,256]{2,1,0:T(8,128)S(1)} %slice_add_fusion), channel_id=1, source_target_pairs={{0,64},{32,96},{64,0},{96,32},{1,65},{33,97},{65,1},{97,33},{2,66}... | collective-permute-start | bytes 196616 | tf_op jit(solution)/shard_map/ppermute | solution.py:373
  59.2 0.8 %collective-permute-start.7 = (f32[2,32,256]{2,1,0:T(8,128)S(1)}, f32[2,32,256]{2,1,0:T(8,128)S(1)}, u32[]{:S(2)}, u32[]{:S(2)}) collective-permute-start(f32[2,32,256]{2,1,0:T(8,128)S(1)} %slice_add_fusion.2), channel_id=1, source_target_pairs={{0,64},{32,96},{64,0},{96,32},{1,65},{33,97},{65,1},{97,33},{2,66}... | collective-permute-start | bytes 196616 | tf_op jit(solution)/shard_map/ppermute | solution.py:373
  60.0 2.0 %collective-permute-done.9 = f32[2,32,256]{2,1,0:T(8,128)S(1)} collective-permute-done((f32[2,32,256]{2,1,0:T(8,128)S(1)}, f32[2,32,256]{2,1,0:T(8,128)S(1)}, u32[]{:S(2)}, u32[]{:S(2)}) %collective-permute-start.9) | collective-permute-done | bytes 65568 | tf_op jit(solution)/shard_map/ppermute | solution.py:373
  62.0 1.4 %collective-permute-done.7 = f32[2,32,256]{2,1,0:T(8,128)S(1)} collective-permute-done((f32[2,32,256]{2,1,0:T(8,128)S(1)}, f32[2,32,256]{2,1,0:T(8,128)S(1)}, u32[]{:S(2)}, u32[]{:S(2)}) %collective-permute-start.7) | collective-permute-done | bytes 65568 | tf_op jit(solution)/shard_map/ppermute | solution.py:373
  (35 shorter events, 1.1 us)
Async XLA Ops:
  0.0 21.8 %copy-start.2 = (bf16[768,1152]{1,0:T(8,128)(2,1)S(1)}, bf16[768,1152]{1,0:T(8,128)(2,1)}, u32[]{:S(2)}) copy-start(bf16[768,1152]{1,0:T(8,128)(2,1)} %constant.52.clone.to_weights) | copy-start | bytes 5308420
  0.0 1.2 %copy-start.3 = (f32[8,64,256]{2,1,0:T(8,128)S(1)}, f32[8,64,256]{2,1,0:T(8,128)}, u32[]{:S(2)}) copy-start(f32[8,64,256]{2,1,0:T(8,128)} %taper.5) | copy-start | bytes 1572868
  1.2 1.2 %copy-start.5 = (bf16[4,8,64,256]{3,2,1,0:T(8,128)(2,1)S(1)}, bf16[4,8,64,256]{3,2,1,0:T(8,128)(2,1)}, u32[]{:S(2)}) copy-start(bf16[4,8,64,256]{3,2,1,0:T(8,128)(2,1)} %p.3) | copy-start | bytes 3145732
  2.4 1.0 %copy-start.9 = (f32[8,64,256]{2,1,0:T(8,128)S(1)}, f32[8,64,256]{2,1,0:T(8,128)}, u32[]{:S(2)}) copy-start(f32[8,64,256]{2,1,0:T(8,128)} %increment.3) | copy-start | bytes 1572868
  3.4 18.3 %copy-start.4 = (f32[8,64,256]{2,1,0:T(8,128)S(1)}, f32[8,64,256]{2,1,0:T(8,128)}, u32[]{:S(2)}) copy-start(f32[8,64,256]{2,1,0:T(8,128)} %taper.5) | copy-start | bytes 1572868
  5.0 11.1 %collective-permute-start.2 = (bf16[8,64,128]{2,1,0:T(8,128)(2,1)}, bf16[8,64,128]{2,1,0:T(8,128)(2,1)S(1)}, u32[]{:S(2)}, u32[]{:S(2)}) collective-permute-start(bf16[8,64,128]{2,1,0:T(8,128)(2,1)} %get-tuple-element.17), channel_id=1, source_target_pairs={{0,1},{1,2},{2,3},{3,0},{4,5},{5,6},{6,7},{7,4},{8,9},{9,10},{10,1... | collective-permute-start | bytes 393224 | tf_op jit(solution)/shard_map/ppermute | solution.py:368
  7.1 9.1 %collective-permute-start.3 = (bf16[8,64,128]{2,1,0:T(8,128)(2,1)S(1)}, bf16[8,64,128]{2,1,0:T(8,128)(2,1)S(1)}, u32[]{:S(2)}, u32[]{:S(2)}) collective-permute-start(bf16[8,64,128]{2,1,0:T(8,128)(2,1)S(1)} %get-tuple-element.18), channel_id=1, source_target_pairs={{0,3},{1,0},{2,1},{3,2},{4,7},{5,4},{6,5},{7,6},{8,11},{9,8},{10,9... | collective-permute-start | bytes 393224 | tf_op jit(solution)/shard_map/ppermute | solution.py:368
  8.3 42.8 %collective-permute-start = (bf16[6,8,16,256]{3,2,1,0:T(8,128)(2,1)}, bf16[6,8,16,256]{3,2,1,0:T(8,128)(2,1)S(1)}, u32[]{:S(2)}, u32[]{:S(2)}) collective-permute-start(bf16[6,8,16,256]{3,2,1,0:T(8,128)(2,1)} %get-tuple-element.15), channel_id=1, source_target_pairs={{0,4},{4,8},{8,12},{12,16},{16,20},{20,24},{24,28},{1,5},{5,9},{9,... | collective-permute-start | bytes 1179656 | tf_op jit(solution)/shard_map/ppermute | solution.py:368
  14.0 37.1 %collective-permute-start.1 = (bf16[6,8,16,256]{3,2,1,0:T(8,128)(2,1)}, bf16[6,8,16,256]{3,2,1,0:T(8,128)(2,1)S(1)}, u32[]{:S(2)}, u32[]{:S(2)}) collective-permute-start(bf16[6,8,16,256]{3,2,1,0:T(8,128)(2,1)} %get-tuple-element.16), channel_id=1, source_target_pairs={{4,0},{8,4},{12,8},{16,12},{20,16},{24,20},{28,24},{5,1},{9,5},{13... | collective-permute-start | bytes 1179656 | tf_op jit(solution)/shard_map/ppermute | solution.py:368
  16.2 29.1 %collective-permute-start.4 = (bf16[2,8,16,128]{3,2,1,0:T(8,128)(2,1)S(1)}, bf16[2,8,16,128]{3,2,1,0:T(8,128)(2,1)S(1)}, u32[]{:S(2)}, u32[]{:S(2)}) collective-permute-start(bf16[2,8,16,128]{3,2,1,0:T(8,128)(2,1)S(1)} %pad_maximum_fusion.1), channel_id=1, source_target_pairs={{0,4},{4,8},{8,12},{12,16},{16,20},{20,24},{24,28},{1,5},{5,9},{9,... | collective-permute-start | bytes 196616 | tf_op jit(solution)/shard_map/ppermute | solution.py:368
  21.8 1.8 %copy-start = (bf16[1280,1152]{1,0:T(8,128)(2,1)S(1)}, bf16[1280,1152]{1,0:T(8,128)(2,1)}, u32[]{:S(2)}) copy-start(bf16[1280,1152]{1,0:T(8,128)(2,1)} %constant.51.clone.to_fields) | copy-start | bytes 8847364
  23.6 1.2 %copy-start.6 = (bf16[4,8,64,256]{3,2,1,0:T(8,128)(2,1)S(1)}, bf16[4,8,64,256]{3,2,1,0:T(8,128)(2,1)}, u32[]{:S(2)}) copy-start(bf16[4,8,64,256]{3,2,1,0:T(8,128)(2,1)} %p.3) | copy-start | bytes 3145732
  24.8 1.1 %copy-start.7 = (bf16[1152,256]{1,0:T(8,128)(2,1)S(1)}, bf16[1152,256]{1,0:T(8,128)(2,1)}, u32[]{:S(2)}) copy-start(bf16[1152,256]{1,0:T(8,128)(2,1)} %constant.53.clone.back) | copy-start | bytes 1769476
  25.9 1.0 %copy-start.10 = (f32[8,64,256]{2,1,0:T(8,128)S(1)}, f32[8,64,256]{2,1,0:T(8,128)}, u32[]{:S(2)}) copy-start(f32[8,64,256]{2,1,0:T(8,128)} %increment.3) | copy-start | bytes 1572868
  26.9 24.2 %copy-start.1 = (bf16[1280,1152]{1,0:T(8,128)(2,1)S(1)}, bf16[1280,1152]{1,0:T(8,128)(2,1)}, u32[]{:S(2)}) copy-start(bf16[1280,1152]{1,0:T(8,128)(2,1)} %constant.51.clone.to_fields) | copy-start | bytes 8847364
  26.9 24.2 %copy-start.8 = (bf16[1152,256]{1,0:T(8,128)(2,1)S(1)}, bf16[1152,256]{1,0:T(8,128)(2,1)}, u32[]{:S(2)}) copy-start(bf16[1152,256]{1,0:T(8,128)(2,1)} %constant.53.clone.back) | copy-start | bytes 1769476
  41.8 16.4 %collective-permute-start.8 = (f32[4,32,256]{2,1,0:T(8,128)S(1)}, f32[4,32,256]{2,1,0:T(8,128)S(1)}, u32[]{:S(2)}, u32[]{:S(2)}) collective-permute-start(f32[4,32,256]{2,1,0:T(8,128)S(1)} %get-tuple-element.24), channel_id=1, source_target_pairs={{0,32},{32,0},{64,96},{96,64},{1,33},{33,1},{65,97},{97,65},{2,34}... | collective-permute-start | bytes 393224 | tf_op jit(solution)/shard_map/ppermute | solution.py:372
  44.0 7.1 %collective-permute-start.5 = (bf16[2,8,16,128]{3,2,1,0:T(8,128)(2,1)S(1)}, bf16[2,8,16,128]{3,2,1,0:T(8,128)(2,1)S(1)}, u32[]{:S(2)}, u32[]{:S(2)}) collective-permute-start(bf16[2,8,16,128]{3,2,1,0:T(8,128)(2,1)S(1)} %pad_maximum_fusion.2), channel_id=1, source_target_pairs={{4,0},{8,4},{12,8},{16,12},{20,16},{24,20},{28,24},{5,1},{9,5},{13... | collective-permute-start | bytes 196616 | tf_op jit(solution)/shard_map/ppermute | solution.py:368
  57.3 1.9 %collective-permute-start.6 = (f32[4,32,256]{2,1,0:T(8,128)S(1)}, f32[4,32,256]{2,1,0:T(8,128)S(1)}, u32[]{:S(2)}, u32[]{:S(2)}) collective-permute-start(f32[4,32,256]{2,1,0:T(8,128)S(1)} %get-tuple-element.22), channel_id=1, source_target_pairs={{0,32},{32,0},{64,96},{96,64},{1,33},{33,1},{65,97},{97,65},{2,34}... | collective-permute-start | bytes 393224 | tf_op jit(solution)/shard_map/ppermute | solution.py:372
  58.2 3.8 %collective-permute-start.9 = (f32[2,32,256]{2,1,0:T(8,128)S(1)}, f32[2,32,256]{2,1,0:T(8,128)S(1)}, u32[]{:S(2)}, u32[]{:S(2)}) collective-permute-start(f32[2,32,256]{2,1,0:T(8,128)S(1)} %slice_add_fusion), channel_id=1, source_target_pairs={{0,64},{32,96},{64,0},{96,32},{1,65},{33,97},{65,1},{97,33},{2,66}... | collective-permute-start | bytes 196616 | tf_op jit(solution)/shard_map/ppermute | solution.py:373
  59.2 4.2 %collective-permute-start.7 = (f32[2,32,256]{2,1,0:T(8,128)S(1)}, f32[2,32,256]{2,1,0:T(8,128)S(1)}, u32[]{:S(2)}, u32[]{:S(2)}) collective-permute-start(f32[2,32,256]{2,1,0:T(8,128)S(1)} %slice_add_fusion.2), channel_id=1, source_target_pairs={{0,64},{32,96},{64,0},{96,32},{1,65},{33,97},{65,1},{97,33},{2,66}... | collective-permute-start | bytes 196616 | tf_op jit(solution)/shard_map/ppermute | solution.py:373
where the time goes:
time: 64.5 us; the launch traced here: 64.1 us
  Pallas kernels  22.6 us (35%)
  starting transfers between devices  21.8 us (34%)
  waiting for transfers between devices  9.32 us (14%)
  local copies, waits for them, and re-layouts  8.71 us (14%)
  other arithmetic  1.49 us (2%)
    ppermute x6, starting transfers between devices, shifted(): return lax.ppermute(value, axis, pairs)  17.1 us
    pallas_call x1, Pallas kernels, local(): pl.pallas_call(inner_kernel, out_shape=(shape((levels // 2, inner_rows, c...  14.9 us
    unnamed x22, local copies, waits for them, and re-layouts  8.62 us
    pallas_call x1, Pallas kernels, local(): pl.pallas_call(outer_kernel, out_shape=(shape((levels // 2, 2 * HALO, col...  6.15 us
    ppermute x6, waiting for transfers between devices, shifted(): return lax.ppermute(value, axis, pairs)  5.8 us
    ppermute x2, waiting for transfers between devices, total_over_members(): lax.ppermute(keep[2:] + got[2:], 'mem', [(i, i ^ 2) for i in range(4)])  3.37 us
    ppermute x2, starting transfers between devices, total_over_members(): got = lax.ppermute(send, 'mem', [(i, i ^ 1) for i in range(4)])  3.07 us
    ppermute x2, starting transfers between devices, total_over_members(): lax.ppermute(keep[2:] + got[2:], 'mem', [(i, i ^ 2) for i in range(4)])  1.64 us
  transfers between devices with their start and end apart: 10, of which 4 were waited for; matrix products, arithmetic and copies ran while one was open for 1% of the time, Pallas kernels for 33%

commit v1 on v0

--- a/solution.py
+++ b/solution.py
@@ -9,7 +9,7 @@
 PASSES = 8
 HALO = 2 * PASSES
 LANES = 128
-BLOCK = 8
+NEAR = 4
 BF16 = jnp.bfloat16
 F32 = jnp.float32
 
@@ -59,22 +59,23 @@
     return [m.astype(np.float32).astype(BF16) for m in (to_fields, to_weights, back)]
 
 
-def pack_kernel(p, increment, taper, up, down, to_left, to_right):
+def sides_kernel(p_hbm, increment_hbm, taper_hbm, to_left, to_right, p, g, taper, increment, sems):
     members, _, rows, cols = p.shape
-
-    def edge(pick, out):
-        for m in range(members):
-            out[m] = p[m, :, pick, :]
-        hi, lo = split(increment[:, pick, :] * taper[:, pick, :])
-        out[members] = hi
-        out[members + 1] = lo
-
-    edge(slice(0, HALO), up)
-    edge(slice(rows - HALO, rows), down)
+    copies = []
+    for i in range(rows // HALO):
+        pick = slice(i * HALO, (i + 1) * HALO)
+        copies.append([
+            pltpu.make_async_copy(p_hbm.at[:, :, pick, :], p.at[:, :, pick, :], sems.at[i, 0]),
+            pltpu.make_async_copy(increment_hbm.at[:, pick, :], increment.at[:, pick, :], sems.at[i, 1]),
+            pltpu.make_async_copy(taper_hbm.at[:, pick, :], taper.at[:, pick, :], sems.at[i, 2]),
+        ])
+    for group in copies:
+        for copy in group:
+            copy.start()
 
     def packed(pick, column, shift):
         fields = [p[m, :, pick, column].astype(F32) for m in range(members)]
-        hi, lo = split(increment[:, pick, column] * taper[:, pick, column])
+        hi, lo = split(g[:, pick, column])
         fields += [hi.astype(F32), lo.astype(F32)]
         lane = lane_of(fields[0].shape)
         total = jnp.zeros_like(fields[0])
@@ -83,18 +84,76 @@
             total = jnp.where(inside, roll(field, shift + HALO * e), total)
         return total.astype(BF16)
 
-    def chunk(i, _):
-        pick = pl.ds(pl.multiple_of(i * HALO, HALO), HALO)
+    for i, group in enumerate(copies):
+        pick = slice(i * HALO, (i + 1) * HALO)
+        for copy in group:
+            copy.wait()
+        g[:, pick, :] = increment[:, pick, :] * taper[:, pick, :]
         to_left[:, pick, :] = packed(pick, slice(0, LANES), 0)
         to_right[:, pick, :] = packed(pick, slice(cols - LANES, cols), HALO)
-        return 0
-
-    lax.fori_loop(0, rows // HALO, chunk, 0)
+
+
+def facing(value):
+    return jnp.swapaxes(value.astype(F32), 0, 1)
+
+
+def block_of(distance, members):
+    near, far = 2 * (members + 2) + 2, 2 * members + 1
+    return near * min(distance, NEAR) + far * max(distance - NEAR, 0)
+
+
+def strips_kernel(p, g, left, right, up, down):
+    members, _, rows, cols = p.shape
+    for out, first, step in ((up, 0, 1), (down, rows - 1, -1)):
+        low = min(first, first + step * (HALO - 1))
+        pick = slice(low, low + HALO)
+        at = [(distance, first + step * distance - low) for distance in range(HALO)]
+
+        def put(distance, index, value):
+            out[block_of(distance, members) + index] = value.astype(BF16)
+
+        for half in range(2):
+            lanes = slice(half * LANES, (half + 1) * LANES)
+            weight = facing(g[:, pick, lanes])
+            hi, lo = split(weight)
+            for distance, row in at[:NEAR]:
+                put(distance, 2 * members + half, hi[row])
+                put(distance, 2 * members + 2 + half, lo[row])
+            for m in range(members):
+                field = facing(p[m, :, pick, lanes])
+                for distance, row in at:
+                    value = field[row] if distance < NEAR else field[row] * weight[row]
+                    put(distance, 2 * m + half, value)
+        packs = [facing(side[:, pick, :]) for side in (left, right)]
+        lane = lane_of(packs[0].shape)
+        products = []
+        for pack in packs:
+            weight = pack + roll(pack, -HALO)
+            total = jnp.zeros_like(pack)
+            for m in range(members):
+                inside = (lane >= HALO * m) & (lane < HALO * (m + 1))
+                total = jnp.where(inside, roll(weight, HALO * (m - members)), total)
+            products.append(pack * total)
+        both = jnp.where(lane < LANES // 2, products[0], roll(products[1], LANES // 2))
+        for distance, row in at:
+            if distance < NEAR:
+                for k, pack in enumerate(packs):
+                    put(distance, 2 * members + 4 + k, pack[row])
+            else:
+                put(distance, 2 * members, both[row])
 
 
 def turned(value):
     levels, rows, lanes = value.shape
     return jnp.swapaxes(value.astype(F32), 0, 1).reshape(rows * levels, lanes)
+
+
+def factors(kappa, count):
+    denominator = 1.0 + 4.0 * kappa
+    scale = kappa / denominator
+    for _ in range(4):
+        scale = scale * scale
+    return 1.0 / kappa, denominator / (kappa * kappa), scale / (count - 1)
 
 
 def row_of(ref, *where):
@@ -149,7 +208,7 @@
 
 
 def inner_kernel(
-    place, p, increment, taper, left, right, to_fields, to_weights, back, coef,
+    place, p, g, taper, left, right, to_fields, to_weights, back, kappa,
     keep, send, edges, edge_values,
     x, values, fields, weights,
 ):
@@ -165,7 +224,7 @@
                 fields[out, m * cols + half * LANES : m * cols + (half + 1) * LANES] = turned(
                     p[m, :, pick, lanes]
                 ).astype(BF16)
-            hi, lo = split(turned(increment[:, pick, lanes] * taper[:, pick, lanes]))
+            hi, lo = split(turned(g[:, pick, lanes]))
             weights[out, lanes] = hi
             weights[out, cols + half * LANES : cols + (half + 1) * LANES] = lo
         for side, ref in enumerate((left, right)):
@@ -174,7 +233,7 @@
             weights[out, 2 * cols + side * LANES : 2 * cols + (side + 1) * LANES] = value
         return 0
 
-    lax.fori_loop(0, rows // HALO, gather, 0)
+    lax.fori_loop(0, rows // HALO, gather, 0, unroll=True)
     for first in range(0, fine, 2):
         width = min(2, fine - first)
         lanes = slice(first * LANES, (first + width) * LANES)
@@ -189,7 +248,7 @@
         edge_values[0, k] = values[k]
         edge_values[1, k] = values[rows - 1 - k]
 
-    linear, constant = coef[0], coef[1]
+    linear, constant, scale = factors(kappa[...], 4 * members)
 
     def wrap(row):
         def target(c, value):
@@ -201,7 +260,7 @@
         wrap(row)
         return 0
 
-    lax.fori_loop(0, rows, wrap_first, 0, unroll=BLOCK)
+    lax.fori_loop(0, rows, wrap_first, 0, unroll=True)
 
     for turn in range(PASSES):
         low = 2 * turn
@@ -215,38 +274,14 @@
         v, u_next = first_sweep(row_of(x, start), row_of(x, start + 1), v, linear, fine)
         q, _ = second_sweep(None, u, u_next, None, constant, fine)
         u = u_next
-        keys = tuple(list(part) for part in (v, u, q))
-
-        def rows_at(first, number, carry):
-            v, u, q = (dict(zip(k, part)) for k, part in zip(keys, carry))
-            for k in range(number):
-                i = first + k
-                v, u_next = first_sweep(row_of(x, i + 1), row_of(x, i + 2), v, linear, fine)
-                q, y = second_sweep(row_of(x, i), u, u_next, q, constant, fine)
-                u = u_next
-                for c in range(fine):
-                    x[i, c + 2] = y[c]
-            return tuple([part[c] for c in k] for k, part in zip(keys, (v, u, q)))
-
-        def block(b, carry):
-            first = start + b * BLOCK
-            carry = rows_at(first, BLOCK, carry)
-            @pl.when(b > 0)
-            def _():
-                for k in range(BLOCK):
-                    wrap(first - BLOCK + k)
-            return carry
-
-        carry = tuple([part[c] for c in k] for k, part in zip(keys, (v, u, q)))
-        whole = count // BLOCK
-        carry = lax.fori_loop(0, whole, block, carry)
-        rest = count - whole * BLOCK
-        if rest:
-            rows_at(start + whole * BLOCK, rest, carry)
-        for row in range(start + (whole - 1) * BLOCK, start + count):
-            wrap(row)
-
-    scale = coef[2]
+        for i in range(start, start + count):
+            v, u_next = first_sweep(row_of(x, i + 1), row_of(x, i + 2), v, linear, fine)
+            q, y = second_sweep(row_of(x, i), u, u_next, q, constant, fine)
+            u = u_next
+            for c in range(fine):
+                x[i, c + 2] = y[c]
+            if turn < PASSES - 1:
+                wrap(i)
 
     def last(i, _):
         first = i * HALO
@@ -271,39 +306,54 @@
 
 
 def outer_kernel(
-    place, taper, top, bottom, top_side, bottom_side, edges, edge_values, to_fields, to_weights, back, coef,
+    place, taper, top, bottom, edges, edge_values, to_fields, to_weights, back, kappa,
     keep, send,
     x, fields, weights,
 ):
-    _, levels, _, cols = top.shape
-    members = top.shape[0] - 2
+    levels, cols = taper.shape[0], taper.shape[2]
     fine = edge_values.shape[2]
-    size = HALO * levels
-    for edge, (strip, side) in enumerate(((top, top_side), (bottom, bottom_side))):
-        out = slice(edge * size, (edge + 1) * size)
-        for half in range(cols // LANES):
-            lanes = slice(half * LANES, (half + 1) * LANES)
-            for m in range(members + 2):
-                value = turned(strip[m, :, :, lanes]).astype(BF16)
-                ref, base = (fields, m * cols) if m < members else (weights, (m - members) * cols)
-                ref[out, base + half * LANES : base + (half + 1) * LANES] = value
-        for k in range(2):
-            value = turned(side[k]).astype(BF16)
-            fields[out, members * cols + k * LANES : members * cols + (k + 1) * LANES] = value
-            weights[out, 2 * cols + k * LANES : 2 * cols + (k + 1) * LANES] = value
+    members = LANES * fine // (cols + 2 * HALO)
+    for edge, strip in enumerate((top, bottom)):
+        for distance in range(0, HALO, 2):
+            is_near = distance < NEAR
+            firsts = [block_of(distance + k, members) for k in range(2)]
+
+            def pair(index):
+                return jnp.concatenate([strip[first + index].astype(F32) for first in firsts], axis=0)
+
+            out = slice((edge * HALO + distance) * levels, (edge * HALO + distance + 2) * levels)
+            for k in range(2 * members):
+                fields[out, k * LANES : (k + 1) * LANES] = pair(k).astype(BF16)
+            sides = [2 * members + 4, 2 * members + 5] if is_near else [2 * members] * 2
+            for k, index in enumerate(sides):
+                value = pair(index)
+                if k == 1 and not is_near:
+                    value = roll(value, LANES // 2)
+                value = value.astype(BF16)
+                fields[out, members * cols + k * LANES : members * cols + (k + 1) * LANES] = value
+                if is_near:
+                    here = slice((edge * NEAR + distance) * levels, (edge * NEAR + distance + 2) * levels)
+                    weights[here, 2 * cols + k * LANES : 2 * cols + (k + 1) * LANES] = value
+            if is_near:
+                for k in range(4):
+                    weights[here, k * LANES : (k + 1) * LANES] = pair(2 * members + k).astype(BF16)
     for first in range(0, fine, 2):
         width = min(2, fine - first)
         lanes = slice(first * LANES, (first + width) * LANES)
-        both = jnp.dot(fields[...], to_fields[:, lanes], preferred_element_type=F32) * jnp.dot(
-            weights[...], to_weights[:, lanes], preferred_element_type=F32
-        )
+        field = jnp.dot(fields[...], to_fields[:, lanes], preferred_element_type=F32)
+        weight = jnp.dot(weights[...], to_weights[:, lanes], preferred_element_type=F32)
         for k in range(width):
-            part = both[:, k * LANES : (k + 1) * LANES].reshape(2, HALO, levels, LANES)
-            for row in range(HALO):
-                x[0, row, 2 + first + k] = part[0, row]
-                x[1, HALO - 1 - row, 2 + first + k] = part[1, row]
-
-    linear, constant = coef[0], coef[1]
+            pick = slice(k * LANES, (k + 1) * LANES)
+            part = field[:, pick].reshape(2, HALO, levels, LANES)
+            near = weight[:, pick].reshape(2, NEAR, levels, LANES)
+            for edge in range(2):
+                for distance in range(HALO):
+                    value = part[edge, distance]
+                    if distance < NEAR:
+                        value = value * near[edge, distance]
+                    x[edge, HALO - 1 - distance, 2 + first + k] = value
+
+    linear, constant, scale = factors(kappa[...], 4 * members)
     inside = [jnp.where(place[edge] == 1, 0.0, 1.0).astype(F32) for edge in range(2)]
 
     def wrap(edge, row):
@@ -341,7 +391,6 @@
                 for row in range(low + 2, low + HALO + 2):
                     wrap(edge, row)
 
-    scale = coef[2]
     rows = taper.shape[1]
     for edge in range(2):
         order = range(HALO) if edge == 0 else range(HALO - 1, -1, -1)
@@ -368,41 +417,52 @@
     return lax.ppermute(value, axis, pairs)
 
 
-def total_over_members(keep, send):
+def over_core(keep, send):
     got = lax.ppermute(send, "mem", [(i, i ^ 1) for i in range(4)])
-    crossing = lax.ppermute(keep[2:] + got[2:], "mem", [(i, i ^ 2) for i in range(4)])
-    return keep[:2] + got[:2] + crossing
+    return keep[:2] + got[:2], keep[2:] + got[2:]
+
+
+def over_plane(here, there):
+    return here + lax.ppermute(there, "mem", [(i, i ^ 2) for i in range(4)])
 
 
 def local(perturbations, increment, taper_norm, kappa):
     members, levels, rows, cols = perturbations.shape
     fine = (cols + 2 * HALO) * members // LANES
     shape = jax.ShapeDtypeStruct
-    strip = shape((members + 2, levels, HALO, cols), BF16)
-    pack = shape((levels, rows, LANES), BF16)
-    big = pltpu.CompilerParams(vmem_limit_bytes=40 * 1024 * 1024)
+    tile = (levels, LANES)
+    big = pltpu.CompilerParams(vmem_limit_bytes=16 * 1024 * 1024)
     vmem = pl.BlockSpec(memory_space=pltpu.VMEM)
     smem = pl.BlockSpec(memory_space=pltpu.SMEM)
-
-    up, down, to_left, to_right = pl.pallas_call(
-        pack_kernel, out_shape=(strip, strip, pack, pack), compiler_params=big, name="pack"
+    hbm = pl.BlockSpec(memory_space=pltpu.HBM)
+
+    pack = shape((levels, rows, LANES), BF16)
+    whole = shape((levels, rows, cols), F32)
+    to_left, to_right, p, g, taper = pl.pallas_call(
+        sides_kernel,
+        out_shape=(pack, pack, shape(perturbations.shape, BF16), whole, whole),
+        in_specs=[hbm] * 3,
+        out_specs=(vmem,) * 5,
+        scratch_shapes=[pltpu.VMEM((levels, rows, cols), F32), pltpu.SemaphoreType.DMA((rows // HALO, 3))],
+        compiler_params=big,
+        name="sides",
     )(perturbations, increment, taper_norm)
-
     left = shifted(to_right, "lon", 1, True)
     right = shifted(to_left, "lon", -1, True)
+
+    strip = shape((block_of(HALO, members), *tile), BF16)
+    up, down = pl.pallas_call(
+        strips_kernel,
+        out_shape=(strip, strip),
+        in_specs=[vmem] * 4,
+        out_specs=(vmem,) * 2,
+        compiler_params=big,
+        name="strips",
+    )(p, g, left, right)
     top = shifted(down, "lat", 1, False)
     bottom = shifted(up, "lat", -1, False)
-    top_side = shifted(jnp.stack([left[:, -HALO:], right[:, -HALO:]]), "lat", 1, False)
-    bottom_side = shifted(jnp.stack([left[:, :HALO], right[:, :HALO]]), "lat", -1, False)
-
-    denominator = 1.0 + 4.0 * kappa
-    count = members * lax.axis_size("mem")
-    coef = jnp.stack([
-        1.0 / kappa,
-        denominator / (kappa * kappa),
-        (kappa / denominator) ** (2 * PASSES) / (count - 1),
-    ])
-    coef = jnp.broadcast_to(coef[:, :, None], (3, levels, LANES))
+
+    kappa = jnp.broadcast_to(kappa[:, None], tile)
     lat, mem = lax.axis_index("lat"), lax.axis_index("mem")
     place = jnp.stack([
         (lat == 0).astype(jnp.int32),
@@ -412,13 +472,12 @@
     ])
     to_fields, to_weights, back = (jnp.asarray(m) for m in selectors(members, cols))
 
-    tile = (levels, LANES)
-    inner_rows = rows - 2 * HALO
+    part = shape((levels // 2, rows - 2 * HALO, cols), F32)
     keep, send, edges, edge_values = pl.pallas_call(
         inner_kernel,
         out_shape=(
-            shape((levels // 2, inner_rows, cols), F32),
-            shape((levels // 2, inner_rows, cols), F32),
+            part,
+            part,
             shape((2, PASSES, 4, fine + 4, *tile), F32),
             shape((2, HALO, fine, *tile), F32),
         ),
@@ -432,23 +491,26 @@
         ],
         compiler_params=big,
         name="inner",
-    )(place, perturbations, increment, taper_norm, left, right, to_fields, to_weights, back, coef)
-    middle = total_over_members(keep, send)
-
+    )(place, p, g, taper, left, right, to_fields, to_weights, back, kappa)
+    here, there = over_core(keep, send)
+    here, there, edges = lax.optimization_barrier((here, there, edges))
+    middle = over_plane(here, there)
+
+    part = shape((levels // 2, 2 * HALO, cols), F32)
     keep, send = pl.pallas_call(
         outer_kernel,
-        out_shape=(shape((levels // 2, 2 * HALO, cols), F32),) * 2,
-        in_specs=[smem] + [vmem] * 11,
+        out_shape=(part, part),
+        in_specs=[smem] + [vmem] * 9,
         out_specs=(vmem,) * 2,
         scratch_shapes=[
             pltpu.VMEM((2, 2 * HALO, fine + 4, *tile), F32),
             pltpu.VMEM((2 * HALO * levels, members * cols + 2 * LANES), BF16),
-            pltpu.VMEM((2 * HALO * levels, 2 * cols + 2 * LANES), BF16),
+            pltpu.VMEM((2 * NEAR * levels, 2 * cols + 2 * LANES), BF16),
         ],
         compiler_params=big,
         name="outer",
-    )(place, taper_norm, top, bottom, top_side, bottom_side, edges, edge_values, to_fields, to_weights, back, coef)
-    outside = total_over_members(keep, send)
+    )(place, taper, top, bottom, edges, edge_values, to_fields, to_weights, back, kappa)
+    outside = over_plane(*over_core(keep, send))
     return jnp.concatenate([outside[:, :HALO], middle, outside[:, HALO:]], axis=1)
 
 

time: 64.5 us -> 64.6 us (level)
  the two profiles are of different devices: /device:TPU:1 before, /device:TPU:22 now
where the time goes in v1:
time: 64.6 us; the launch traced here: 64.2 us
  waiting for transfers between devices  21.2 us (33%)
  Pallas kernels  19.3 us (30%)
  starting transfers between devices  14 us (22%)
  local copies, waits for them, and re-layouts  8.91 us (14%)
  other arithmetic  0.8 us (1%)
    ppermute x4, waiting for transfers between devices, shifted(): return lax.ppermute(value, axis, pairs)  18.2 us
    ppermute x4, starting transfers between devices, shifted(): return lax.ppermute(value, axis, pairs)  10.5 us
    pallas_call x1, Pallas kernels, local(): pl.pallas_call(inner_kernel, out_shape=(part, part, shape((2, PASSES, 4,...  9.77 us
    unnamed x20, local copies, waits for them, and re-layouts  8.18 us
    pallas_call x1, Pallas kernels, local(): pl.pallas_call(outer_kernel, out_shape=(part, part), in_specs=[smem] + [v...  6.07 us
    ppermute x2, starting transfers between devices, over_plane(): return here + lax.ppermute(there, 'mem', [(i, i ^ 2) for i in range(4)])  3.32 us
    ppermute x2, waiting for transfers between devices, over_plane(): return here + lax.ppermute(there, 'mem', [(i, i ^ 2) for i in range(4)])  3 us
    pallas_call x1, Pallas kernels, local(): pl.pallas_call(strips_kernel, out_shape=(strip, strip), in_specs=[vmem] *...  1.75 us
  transfers between devices with their start and end apart: 8, of which 6 were waited for; matrix products, arithmetic and copies ran while one was open for 0% of the time, Pallas kernels for 3%

profile of v1, /device:TPU:22, one launch (start us, length us, event | category | flops | bytes accessed | tf_op | source)
XLA Modules:
  0.0 64.2 jit_solution(11463896557551449145)
XLA Ops:
  0.0 1.4 %copy-done.7 = bf16[4,8,64,256]{3,2,1,0:T(8,128)(2,1)S(1)} copy-done((bf16[4,8,64,256]{3,2,1,0:T(8,128)(2,1)S(1)}, bf16[4,8,64,256]{3,2,1,0:T(8,128)(2,1)}, u32[]{:S(2)}) %copy-start.7) | copy-done | bytes 1048600
  1.4 1.0 %copy-done.8 = f32[8,64,256]{2,1,0:T(8,128)S(1)} copy-done((f32[8,64,256]{2,1,0:T(8,128)S(1)}, f32[8,64,256]{2,1,0:T(8,128)}, u32[]{:S(2)}) %copy-start.8) | copy-done | bytes 524312
  2.4 1.0 %copy-done.9 = f32[8,64,256]{2,1,0:T(8,128)S(1)} copy-done((f32[8,64,256]{2,1,0:T(8,128)S(1)}, f32[8,64,256]{2,1,0:T(8,128)}, u32[]{:S(2)}) %copy-start.9) | copy-done | bytes 524312
  3.4 1.7 %sides.1 = (bf16[8,64,128]{2,1,0:T(8,128)(2,1)}, bf16[8,64,128]{2,1,0:T(8,128)(2,1)}, bf16[4,8,64,256]{3,2,1,0:T(8,128)(2,1)S(1)}, f32[8,64,256]{2,1,0:T(8,128)S(1)}, f32[8,64,256]{2,1,0:T(8,128)S(1)}) custom-call(bf16[4,8,64,256]{3,2,1,0:T(8,128)(2,1)S(1)} %copy-done.7, f32[8,64,256]{2,1,0:T(8,128)S(1)} %copy-done.8, f32[8,64,256]{2,1,0:T(8,128)S(1)} %copy-done.9), custom_call_target="tpu_custom_call" | custom-call | tf_op jit(solution)/shard_map/sides/pallas_call | solution.py:441
  5.1 0.8 %copy-done.5 = f32[8,64,256]{2,1,0:T(8,128)} copy-done((f32[8,64,256]{2,1,0:T(8,128)}, f32[8,64,256]{2,1,0:T(8,128)S(1)}, u32[]{:S(2)}) %copy-start.5) | copy-done | bytes 524312
  6.4 1.5 %collective-permute-start.1 = (bf16[8,64,128]{2,1,0:T(8,128)(2,1)}, bf16[8,64,128]{2,1,0:T(8,128)(2,1)}, u32[]{:S(2)}, u32[]{:S(2)}) collective-permute-start(bf16[8,64,128]{2,1,0:T(8,128)(2,1)} %get-tuple-element.25), channel_id=1, source_target_pairs={{0,3},{1,0},{2,1},{3,2},{4,7},{5,4},{6,5},{7,6},{8,11},{9,8},{10,9... | collective-permute-start | bytes 393224 | tf_op jit(solution)/shard_map/ppermute | solution.py:417
  8.0 3.3 %collective-permute-done.left = bf16[8,64,128]{2,1,0:T(8,128)(2,1)S(1)} collective-permute-done((bf16[8,64,128]{2,1,0:T(8,128)(2,1)}, bf16[8,64,128]{2,1,0:T(8,128)(2,1)S(1)}, u32[]{:S(2)}, u32[]{:S(2)}) %collective-permute-start) | collective-permute-done | bytes 131104 | tf_op jit(solution)/shard_map/ppermute | solution.py:417
  11.4 1.5 %collective-permute-done.1.right = bf16[8,64,128]{2,1,0:T(8,128)(2,1)} collective-permute-done((bf16[8,64,128]{2,1,0:T(8,128)(2,1)}, bf16[8,64,128]{2,1,0:T(8,128)(2,1)}, u32[]{:S(2)}, u32[]{:S(2)}) %collective-permute-start.1) | collective-permute-done | bytes 131104 | tf_op jit(solution)/shard_map/ppermute | solution.py:417
  12.9 0.7 %broadcast_in_dim.2.kappa = f32[8,128]{1,0:T(8,128)S(1)} broadcast(f32[8]{0:T(128)} %param.10), dimensions={0} | broadcast | bytes 4128 | tf_op jit(solution)/shard_map/broadcast_in_dim | solution.py:465
  13.6 1.8 %copy-done = bf16[1280,1152]{1,0:T(8,128)(2,1)S(1)} copy-done((bf16[1280,1152]{1,0:T(8,128)(2,1)S(1)}, bf16[1280,1152]{1,0:T(8,128)(2,1)}, u32[]{:S(2)}) %copy-start) | copy-done | bytes 2949144
  15.5 1.1 %copy-done.3 = bf16[1152,256]{1,0:T(8,128)(2,1)S(1)} copy-done((bf16[1152,256]{1,0:T(8,128)(2,1)S(1)}, bf16[1152,256]{1,0:T(8,128)(2,1)}, u32[]{:S(2)}) %copy-start.3) | copy-done | bytes 589848
  16.5 1.0 %copy-done.6 = f32[8,64,256]{2,1,0:T(8,128)S(1)} copy-done((f32[8,64,256]{2,1,0:T(8,128)S(1)}, f32[8,64,256]{2,1,0:T(8,128)}, u32[]{:S(2)}) %copy-start.6) | copy-done | bytes 524312
  17.6 9.8 %inner.1 = (f32[4,32,256]{2,1,0:T(8,128)S(1)}, f32[4,32,256]{2,1,0:T(8,128)S(1)}, f32[2,8,4,13,8,128]{5,4,3,2,1,0:T(8,128)S(1)}, f32[2,16,9,8,128]{4,3,2,1,0:T(8,128)S(1)}) custom-call(s32[4]{0:T(128)S(1)} %pad_add_fusion.place, bf16[4,8,64,256]{3,2,1,0:T(8,128)(2,1)S(1)} %get-tuple-element.22.p, f32[8,64,256]{2,1,0:T(8,128)S(1)} %get-tuple-element.23.g, ...), custom_call_target="tpu_custom_call" | custom-call | tf_op jit(solution)/shard_map/inner/pallas_call | solution.py:476
  27.5 1.8 %strips.1 = (bf16[164,8,128]{2,1,0:T(8,128)(2,1)S(1)}, bf16[164,8,128]{2,1,0:T(8,128)(2,1)S(1)}) custom-call(bf16[4,8,64,256]{3,2,1,0:T(8,128)(2,1)S(1)} %get-tuple-element.22.p, f32[8,64,256]{2,1,0:T(8,128)S(1)} %get-tuple-element.23.g, bf16[8,64,128]{2,1,0:T(8,128)(2,1)S(1)} %collective-permute-done.left, bf16[8,64,128]{2,1,0:T(8,128)(2,1)} %collective-permute-done.1.right), custom_call_target="tpu_custom_call" | custom-call | tf_op jit(solution)/shard_map/strips/pallas_call | solution.py:454
  29.2 5.8 %collective-permute-start.2 = (bf16[164,8,128]{2,1,0:T(8,128)(2,1)S(1)}, bf16[164,8,128]{2,1,0:T(8,128)(2,1)S(1)}, u32[]{:S(2)}, u32[]{:S(2)}) collective-permute-start(bf16[164,8,128]{2,1,0:T(8,128)(2,1)S(1)} %get-tuple-element.26), channel_id=1, source_target_pairs={{0,4},{4,8},{8,12},{12,16},{16,20},{20,24},{24,28},{1,5},{5,9},{9,... | collective-permute-start | bytes 1007624 | tf_op jit(solution)/shard_map/ppermute | solution.py:417
  35.0 2.6 %collective-permute-start.3 = (bf16[164,8,128]{2,1,0:T(8,128)(2,1)S(1)}, bf16[164,8,128]{2,1,0:T(8,128)(2,1)S(1)}, u32[]{:S(2)}, u32[]{:S(2)}) collective-permute-start(bf16[164,8,128]{2,1,0:T(8,128)(2,1)S(1)} %get-tuple-element.27), channel_id=1, source_target_pairs={{4,0},{8,4},{12,8},{16,12},{20,16},{24,20},{28,24},{5,1},{9,5},{13... | collective-permute-start | bytes 1007624 | tf_op jit(solution)/shard_map/ppermute | solution.py:417
  37.7 12.3 %collective-permute-done.2.top = bf16[164,8,128]{2,1,0:T(8,128)(2,1)S(1)} collective-permute-done((bf16[164,8,128]{2,1,0:T(8,128)(2,1)S(1)}, bf16[164,8,128]{2,1,0:T(8,128)(2,1)S(1)}, u32[]{:S(2)}, u32[]{:S(2)}) %collective-permute-start.2) | collective-permute-done | bytes 335904 | tf_op jit(solution)/shard_map/ppermute | solution.py:417
  50.0 1.0 %collective-permute-done.3.bottom = bf16[164,8,128]{2,1,0:T(8,128)(2,1)S(1)} collective-permute-done((bf16[164,8,128]{2,1,0:T(8,128)(2,1)S(1)}, bf16[164,8,128]{2,1,0:T(8,128)(2,1)S(1)}, u32[]{:S(2)}, u32[]{:S(2)}) %collective-permute-start.3) | collective-permute-done | bytes 335904 | tf_op jit(solution)/shard_map/ppermute | solution.py:417
  51.0 6.1 %outer.1 = (f32[4,32,256]{2,1,0:T(8,128)S(1)}, f32[4,32,256]{2,1,0:T(8,128)S(1)}) custom-call(s32[4]{0:T(128)S(1)} %pad_add_fusion.place, f32[8,64,256]{2,1,0:T(8,128)S(1)} %copy-done.6, bf16[164,8,128]{2,1,0:T(8,128)(2,1)S(1)} %collective-permute-done.2.top, bf16[164,8,128]{2,1,0:T(8,128)(2,1)S(1)} %collective-permute-done.3.bottom, ...), custom_call_target="tpu_custom_call" | custom-call | tf_op jit(solution)/shard_map/outer/pallas_call | solution.py:500
  57.2 2.0 %collective-permute-start.7 = (f32[2,32,256]{2,1,0:T(8,128)S(1)}, f32[2,32,256]{2,1,0:T(8,128)S(1)}, u32[]{:S(2)}, u32[]{:S(2)}) collective-permute-start(f32[2,32,256]{2,1,0:T(8,128)S(1)} %get-tuple-element.36), channel_id=1, source_target_pairs={{0,64},{32,96},{64,0},{96,32},{1,65},{33,97},{65,1},{97,33},{2,66}... | collective-permute-start | bytes 196616 | tf_op jit(solution)/shard_map/ppermute | solution.py:426
  59.2 1.3 %collective-permute-start.6 = (f32[2,32,256]{2,1,0:T(8,128)S(1)}, f32[2,32,256]{2,1,0:T(8,128)S(1)}, u32[]{:S(2)}, u32[]{:S(2)}) collective-permute-start(f32[2,32,256]{2,1,0:T(8,128)S(1)} %slice_add_fusion), channel_id=1, source_target_pairs={{0,64},{32,96},{64,0},{96,32},{1,65},{33,97},{65,1},{97,33},{2,66}... | collective-permute-start | bytes 196616 | tf_op jit(solution)/shard_map/ppermute | solution.py:426
  60.5 1.3 %collective-permute-done.7 = f32[2,32,256]{2,1,0:T(8,128)S(1)} collective-permute-done((f32[2,32,256]{2,1,0:T(8,128)S(1)}, f32[2,32,256]{2,1,0:T(8,128)S(1)}, u32[]{:S(2)}, u32[]{:S(2)}) %collective-permute-start.7) | collective-permute-done | bytes 65568 | tf_op jit(solution)/shard_map/ppermute | solution.py:426
  61.8 1.7 %collective-permute-done.6 = f32[2,32,256]{2,1,0:T(8,128)S(1)} collective-permute-done((f32[2,32,256]{2,1,0:T(8,128)S(1)}, f32[2,32,256]{2,1,0:T(8,128)S(1)}, u32[]{:S(2)}, u32[]{:S(2)}) %collective-permute-start.6) | collective-permute-done | bytes 65568 | tf_op jit(solution)/shard_map/ppermute | solution.py:426
  63.6 0.7 %pad_maximum_fusion = f32[2,64,256]{2,1,0:T(8,128)} fusion(f32[2,16,256]{2,1,0:T(8,128)S(1)} %get-tuple-element.40, f32[2,32,256]{2,1,0:T(8,128)S(1)} %add.29, f32[2,16,256]{2,1,0:T(8,128)S(1)} %get-tuple-element.39), kind=kLoop, calls=%fused_computation | loop fusion | flops 65536 | bytes 262144 | tf_op jit(solution)/shard_map/concatenate | solution.py:514
  (24 shorter events, 0.8 us)
Async XLA Ops:
  0.0 13.6 %copy-start.2 = (bf16[768,1152]{1,0:T(8,128)(2,1)S(1)}, bf16[768,1152]{1,0:T(8,128)(2,1)}, u32[]{:S(2)}) copy-start(bf16[768,1152]{1,0:T(8,128)(2,1)} %constant.45.clone.to_weights) | copy-start | bytes 5308420
  0.0 1.4 %copy-start.7 = (bf16[4,8,64,256]{3,2,1,0:T(8,128)(2,1)S(1)}, bf16[4,8,64,256]{3,2,1,0:T(8,128)(2,1)}, u32[]{:S(2)}) copy-start(bf16[4,8,64,256]{3,2,1,0:T(8,128)(2,1)} %p_hbm.1) | copy-start | bytes 3145732
  1.4 1.0 %copy-start.8 = (f32[8,64,256]{2,1,0:T(8,128)S(1)}, f32[8,64,256]{2,1,0:T(8,128)}, u32[]{:S(2)}) copy-start(f32[8,64,256]{2,1,0:T(8,128)} %increment_hbm.1) | copy-start | bytes 1572868
  2.4 1.0 %copy-start.9 = (f32[8,64,256]{2,1,0:T(8,128)S(1)}, f32[8,64,256]{2,1,0:T(8,128)}, u32[]{:S(2)}) copy-start(f32[8,64,256]{2,1,0:T(8,128)} %taper_hbm.1) | copy-start | bytes 1572868
  5.1 0.8 %copy-start.5 = (f32[8,64,256]{2,1,0:T(8,128)}, f32[8,64,256]{2,1,0:T(8,128)S(1)}, u32[]{:S(2)}) copy-start(f32[8,64,256]{2,1,0:T(8,128)S(1)} %get-tuple-element.21.taper) | copy-start | bytes 1572868
  5.9 5.4 %collective-permute-start = (bf16[8,64,128]{2,1,0:T(8,128)(2,1)}, bf16[8,64,128]{2,1,0:T(8,128)(2,1)S(1)}, u32[]{:S(2)}, u32[]{:S(2)}) collective-permute-start(bf16[8,64,128]{2,1,0:T(8,128)(2,1)} %get-tuple-element.24), channel_id=1, source_target_pairs={{0,1},{1,2},{2,3},{3,0},{4,5},{5,6},{6,7},{7,4},{8,9},{9,10},{10,1... | collective-permute-start | bytes 393224 | tf_op jit(solution)/shard_map/ppermute | solution.py:417
  6.4 6.5 %collective-permute-start.1 = (bf16[8,64,128]{2,1,0:T(8,128)(2,1)}, bf16[8,64,128]{2,1,0:T(8,128)(2,1)}, u32[]{:S(2)}, u32[]{:S(2)}) collective-permute-start(bf16[8,64,128]{2,1,0:T(8,128)(2,1)} %get-tuple-element.25), channel_id=1, source_target_pairs={{0,3},{1,0},{2,1},{3,2},{4,7},{5,4},{6,5},{7,6},{8,11},{9,8},{10,9... | collective-permute-start | bytes 393224 | tf_op jit(solution)/shard_map/ppermute | solution.py:417
  13.6 1.8 %copy-start = (bf16[1280,1152]{1,0:T(8,128)(2,1)S(1)}, bf16[1280,1152]{1,0:T(8,128)(2,1)}, u32[]{:S(2)}) copy-start(bf16[1280,1152]{1,0:T(8,128)(2,1)} %constant.44.clone.to_fields) | copy-start | bytes 8847364
  15.5 1.1 %copy-start.3 = (bf16[1152,256]{1,0:T(8,128)(2,1)S(1)}, bf16[1152,256]{1,0:T(8,128)(2,1)}, u32[]{:S(2)}) copy-start(bf16[1152,256]{1,0:T(8,128)(2,1)} %constant.46.clone.back) | copy-start | bytes 1769476
  16.5 1.0 %copy-start.6 = (f32[8,64,256]{2,1,0:T(8,128)S(1)}, f32[8,64,256]{2,1,0:T(8,128)}, u32[]{:S(2)}) copy-start(f32[8,64,256]{2,1,0:T(8,128)} %copy-done.5) | copy-start | bytes 1572868
  17.6 33.4 %copy-start.1 = (bf16[1280,1152]{1,0:T(8,128)(2,1)S(1)}, bf16[1280,1152]{1,0:T(8,128)(2,1)}, u32[]{:S(2)}) copy-start(bf16[1280,1152]{1,0:T(8,128)(2,1)} %constant.44.clone.to_fields) | copy-start | bytes 8847364
  17.6 33.4 %copy-start.4 = (bf16[1152,256]{1,0:T(8,128)(2,1)S(1)}, bf16[1152,256]{1,0:T(8,128)(2,1)}, u32[]{:S(2)}) copy-start(bf16[1152,256]{1,0:T(8,128)(2,1)} %constant.46.clone.back) | copy-start | bytes 1769476
  27.4 10.3 %collective-permute-start.4 = (f32[4,32,256]{2,1,0:T(8,128)S(1)}, f32[4,32,256]{2,1,0:T(8,128)S(1)}, u32[]{:S(2)}, u32[]{:S(2)}) collective-permute-start(f32[4,32,256]{2,1,0:T(8,128)S(1)} %get-tuple-element.29), channel_id=1, source_target_pairs={{0,32},{32,0},{64,96},{96,64},{1,33},{33,1},{65,97},{97,65},{2,34}... | collective-permute-start | bytes 393224 | tf_op jit(solution)/shard_map/ppermute | solution.py:421
  29.2 20.8 %collective-permute-start.2 = (bf16[164,8,128]{2,1,0:T(8,128)(2,1)S(1)}, bf16[164,8,128]{2,1,0:T(8,128)(2,1)S(1)}, u32[]{:S(2)}, u32[]{:S(2)}) collective-permute-start(bf16[164,8,128]{2,1,0:T(8,128)(2,1)S(1)} %get-tuple-element.26), channel_id=1, source_target_pairs={{0,4},{4,8},{8,12},{12,16},{16,20},{20,24},{24,28},{1,5},{5,9},{9,... | collective-permute-start | bytes 1007624 | tf_op jit(solution)/shard_map/ppermute | solution.py:417
  35.0 16.0 %collective-permute-start.3 = (bf16[164,8,128]{2,1,0:T(8,128)(2,1)S(1)}, bf16[164,8,128]{2,1,0:T(8,128)(2,1)S(1)}, u32[]{:S(2)}, u32[]{:S(2)}) collective-permute-start(bf16[164,8,128]{2,1,0:T(8,128)(2,1)S(1)} %get-tuple-element.27), channel_id=1, source_target_pairs={{4,0},{8,4},{12,8},{16,12},{20,16},{24,20},{28,24},{5,1},{9,5},{13... | collective-permute-start | bytes 1007624 | tf_op jit(solution)/shard_map/ppermute | solution.py:417
  57.1 2.1 %collective-permute-start.5 = (f32[4,32,256]{2,1,0:T(8,128)S(1)}, f32[4,32,256]{2,1,0:T(8,128)S(1)}, u32[]{:S(2)}, u32[]{:S(2)}) collective-permute-start(f32[4,32,256]{2,1,0:T(8,128)S(1)} %get-tuple-element.34), channel_id=1, source_target_pairs={{0,32},{32,0},{64,96},{96,64},{1,33},{33,1},{65,97},{97,65},{2,34}... | collective-permute-start | bytes 393224 | tf_op jit(solution)/shard_map/ppermute | solution.py:421
  57.2 4.7 %collective-permute-start.7 = (f32[2,32,256]{2,1,0:T(8,128)S(1)}, f32[2,32,256]{2,1,0:T(8,128)S(1)}, u32[]{:S(2)}, u32[]{:S(2)}) collective-permute-start(f32[2,32,256]{2,1,0:T(8,128)S(1)} %get-tuple-element.36), channel_id=1, source_target_pairs={{0,64},{32,96},{64,0},{96,32},{1,65},{33,97},{65,1},{97,33},{2,66}... | collective-permute-start | bytes 196616 | tf_op jit(solution)/shard_map/ppermute | solution.py:426
  59.2 4.3 %collective-permute-start.6 = (f32[2,32,256]{2,1,0:T(8,128)S(1)}, f32[2,32,256]{2,1,0:T(8,128)S(1)}, u32[]{:S(2)}, u32[]{:S(2)}) collective-permute-start(f32[2,32,256]{2,1,0:T(8,128)S(1)} %slice_add_fusion), channel_id=1, source_target_pairs={{0,64},{32,96},{64,0},{96,32},{1,65},{33,97},{65,1},{97,33},{2,66}... | collective-permute-start | bytes 196616 | tf_op jit(solution)/shard_map/ppermute | solution.py:426

commit v2 on v1

v2 whole, which is shorter than its diff:
```python
import jax
import jax.numpy as jnp
from jax import lax
from jax.experimental import pallas as pl
from jax.experimental.pallas import tpu as pltpu
from jax.sharding import PartitionSpec as P

PASSES = 8
HALO = 2 * PASSES
LANES = 128
NEAR = 4
START_LIMIT = 50
BF16 = jnp.bfloat16
F32 = jnp.float32


def roll(x, shift):
    shift = shift % LANES
    return pltpu.roll(x, shift, x.ndim - 1) if shift else x


def lane_of(shape):
    return lax.broadcasted_iota(jnp.int32, shape, len(shape) - 1)


def split(value):
    hi = value.astype(BF16)
    return hi, (value - hi.astype(F32)).astype(BF16)


def target_column(shape, first, members, cols):
    chunks = LANES // members
    fine = (cols + 2 * HALO) // chunks
    lane = lax.broadcasted_iota(jnp.int32, shape, 1)
    return fine * (lane % chunks) + first - HALO, lane // chunks


def fill_selectors(to_fields, to_weights, back, members, cols):
    fine = back.shape[0] // LANES

    def mark(hit):
        return jnp.where(hit, 1.0, 0.0).astype(BF16)

    for first in range(fine):
        lanes = slice(first * LANES, (first + 1) * LANES)
        shape = (cols, LANES)
        column, member = target_column(shape, first, members, cols)
        row = lax.broadcasted_iota(jnp.int32, shape, 0)
        here = row == column
        for m in range(members):
            to_fields[m * cols : (m + 1) * cols, lanes] = mark(here & (member == m))
        for part in range(2):
            to_weights[part * cols : (part + 1) * cols, lanes] = mark(here)
        shape = (2 * LANES, LANES)
        column, member = target_column(shape, first, members, cols)
        row = lax.broadcasted_iota(jnp.int32, shape, 0)
        base = jnp.where(column < 0, column + HALO, jnp.where(column >= cols, column - cols + LANES, -4 * LANES))
        to_fields[members * cols :, lanes] = mark(row == base + HALO * member)
        hi = base + HALO * members
        to_weights[2 * cols :, lanes] = mark((row == hi) | (row == hi + HALO))
        shape = (LANES, cols)
        lane = lax.broadcasted_iota(jnp.int32, shape, 0)
        column = fine * (lane % (LANES // members)) + first - HALO
        back[lanes, :] = mark(lax.broadcasted_iota(jnp.int32, shape, 1) == column)


def facing(value):
    return jnp.swapaxes(value.astype(F32), 0, 1)


def start_kernel(p_hbm, increment_hbm, taper_hbm, up, down, to_left, to_right, p, g, taper, increment, sems):
    members, levels, rows, cols = p.shape
    copies = []
    for i in (0, rows // HALO - 1, *range(1, rows // HALO - 1)):
        pick = slice(i * HALO, (i + 1) * HALO)
        copies.append((pick, [
            pltpu.make_async_copy(p_hbm.at[:, :, pick, :], p.at[:, :, pick, :], sems.at[i, 0]),
            pltpu.make_async_copy(increment_hbm.at[:, pick, :], increment.at[:, pick, :], sems.at[i, 1]),
            pltpu.make_async_copy(taper_hbm.at[:, pick, :], taper.at[:, pick, :], sems.at[i, 2]),
        ]))
    for _, group in copies:
        for copy in group:
            copy.start()

    def strip(out, pick, order):
        def put(pair, lanes, field, first=0):
            rows_at = slice(first + 2 * pair * levels, first + 2 * (pair + 1) * levels)
            both = jnp.concatenate([field[order[2 * pair]], field[order[2 * pair + 1]]], axis=0)
            out[rows_at, lanes] = both.astype(BF16)

        for half in range(2):
            lanes = slice(half * LANES, (half + 1) * LANES)
            weight = facing(g[:, pick, lanes])
            hi = weight.astype(BF16).astype(F32)
            for k, part in enumerate((hi, weight - hi)):
                for pair in range(NEAR // 2):
                    put(pair, slice(members * cols, members * cols + LANES), part, (2 * k + half) * NEAR * levels)
            for m in range(members):
                to = slice(m * cols + half * LANES, m * cols + (half + 1) * LANES)
                field = facing(p[m, :, pick, lanes])
                for pair in range(HALO // 2):
                    put(pair, to, field if 2 * pair < NEAR else field * weight)

    def packed(pick, column, shift):
        fields = [p[m, :, pick, column].astype(F32) for m in range(members)]
        hi, lo = split(g[:, pick, column])
        fields += [hi.astype(F32), lo.astype(F32)]
        lane = lane_of(fields[0].shape)
        total = jnp.zeros_like(fields[0])
        for e, field in enumerate(fields):
            inside = (lane >= HALO * e) & (lane < HALO * (e + 1))
            total = jnp.where(inside, roll(field, shift + HALO * e), total)
        return total.astype(BF16)

    for k, (pick, group) in enumerate(copies):
        for copy in group:
            copy.wait()
        g[:, pick, :] = increment[:, pick, :] * taper[:, pick, :]
        if k == 0:
            strip(up, pick, range(HALO))
        if k == 1:
            strip(down, pick, range(HALO - 1, -1, -1))
        to_left[:, pick, :] = packed(pick, slice(0, LANES), 0)
        to_right[:, pick, :] = packed(pick, slice(cols - LANES, cols), HALO)


def corners_kernel(top, bottom, to_left, to_right):
    count = top.shape[0]
    pairs = count // 16
    for edge, strip in enumerate((top, bottom)):
        main = strip.shape[1] - LANES
        members = main // (2 * LANES)
        for pair in range(pairs):
            rows = slice(16 * pair, 16 * (pair + 1))
            out = slice(edge * count + 16 * pair, edge * count + 16 * (pair + 1))
            fields = [
                [strip[rows, (2 * m + half) * LANES : (2 * m + half + 1) * LANES].astype(F32) for m in range(members)]
                for half in range(2)
            ]
            if 2 * pair < NEAR:
                for half in range(2):
                    for k in range(2):
                        first = (2 * k + half) * (count // 4) + 16 * pair
                        fields[half].append(strip[first : first + 16, main:].astype(F32))
            lane = lane_of((16, LANES))
            for ref, half, shift in ((to_left, 0, 0), (to_right, 1, HALO)):
                total = jnp.zeros((16, LANES), F32)
                for e, field in enumerate(fields[half]):
                    inside = (lane >= HALO * e) & (lane < HALO * (e + 1))
                    total = jnp.where(inside, roll(field, shift + HALO * e), total)
                ref[out, :] = total.astype(BF16)


def turned(value):
    levels, rows, lanes = value.shape
    return jnp.swapaxes(value.astype(F32), 0, 1).reshape(rows * levels, lanes)


def factors(kappa, count):
    denominator = 1.0 + 4.0 * kappa
    scale = kappa / denominator
    for _ in range(4):
        scale = scale * scale
    return 1.0 / kappa, denominator / (kappa * kappa), scale / (count - 1)


def row_of(ref, *where):
    return lambda c: ref[(*where, c + 2)]


def first_sweep(x, x_next, v, linear, fine):
    v_next = {c: x(c) + x_next(c + 1) for c in range(-2, fine + 1)}
    if v is None:
        return v_next, None
    u = {c: linear * x(c) + v[c] + v_next[c - 1] for c in range(-1, fine + 1)}
    return v_next, u


def second_sweep(x, u, u_next, q, constant, fine):
    q_next = {c: u[c] + u_next[c + 1] for c in range(-1, fine)}
    if q is None:
        return q_next, None
    return q_next, [constant * x(c) + q[c] + q_next[c - 1] for c in range(fine)]


def wrap_columns(source, target, fine):
    for c in (0, 1):
        target(fine + c, roll(source(c), -1))
        target(c - 2, roll(source(fine - 2 + c), 1))


def finish(sums, back, scale, taper_of, write, levels):
    hi, lo = split(sums)
    total = jnp.dot(hi, back, preferred_element_type=F32) + jnp.dot(lo, back, preferred_element_type=F32)
    count = total.shape[0] // levels
    for half in range(total.shape[1] // LANES):
        lanes = slice(half * LANES, (half + 1) * LANES)
        part = total[:, lanes].reshape(count, levels, LANES) * scale
        natural = jnp.swapaxes(part, 0, 1) * taper_of(lanes)
        write(natural, lanes)


def to_owner(place, natural, keep, send, pick, lanes, levels):
    core, plane = place[2], place[3]
    for level in range(levels):
        owner_plane, owner_core, within = level // 4, level // 2 % 2, level % 2
        slot = jnp.where(plane == owner_plane, 0, 2) + within

        @pl.when(core == owner_core)
        def _():
            keep[slot, pick, lanes] = natural[level]

        @pl.when(core != owner_core)
        def _():
            send[slot, pick, lanes] = natural[level]


def dot(a, b):
    return jnp.dot(a, b, preferred_element_type=F32)


def prepare_kernel(p, g, own_values, own_weights, to_fields, to_weights, back, fields, weights):
    members, levels, rows, cols = p.shape
    fine = back.shape[0] // LANES
    fill_selectors(to_fields, to_weights, back, members, cols)
    for i in range(rows // HALO):
        pick = slice(i * HALO, (i + 1) * HALO)
        out = slice(i * HALO * levels, (i + 1) * HALO * levels)
        for half in range(cols // LANES):
            lanes = slice(half * LANES, (half + 1) * LANES)
            for m in range(members):
                to = slice(m * cols + half * LANES, m * cols + (half + 1) * LANES)
                fields[out, to] = turned(p[m, :, pick, lanes]).astype(BF16)
            hi, lo = split(turned(g[:, pick, lanes]))
            weights[out, lanes] = hi
            weights[out, cols + half * LANES : cols + (half + 1) * LANES] = lo
    for first in range(0, fine, 2):
        width = min(2, fine - first)
        lanes = slice(first * LANES, (first + width) * LANES)
        field = dot(fields[...], to_fields[: members * cols, lanes])
        weight = dot(weights[...], to_weights[: 2 * cols, lanes])
        for k in range(width):
            pick = slice(k * LANES, (k + 1) * LANES)
            own_values[:, first + k] = field[:, pick].reshape(rows, levels, LANES)
            own_weights[:, first + k] = weight[:, pick].reshape(rows, levels, LANES)


def inner_kernel(
    place, own_values, own_weights, taper, left, right, to_fields, to_weights, back, kappa,
    keep, send, edges, edge_values,
    x, values, packs,
):
    levels, rows, cols = taper.shape
    fine = x.shape[1] - 4
    members = LANES * fine // (cols + 2 * HALO)
    for i in range(rows // HALO):
        out = slice(i * HALO * levels, (i + 1) * HALO * levels)
        for side, ref in enumerate((left, right)):
            lanes = slice(side * LANES, (side + 1) * LANES)
            packs[out, lanes] = turned(ref[:, i * HALO : (i + 1) * HALO, :]).astype(BF16)
    for first in range(0, fine, 2):
        width = min(2, fine - first)
        lanes = slice(first * LANES, (first + width) * LANES)
        field = dot(packs[...], to_fields[members * cols :, lanes])
        weight = dot(packs[...], to_weights[2 * cols :, lanes])
        for k in range(width):
            pick = slice(k * LANES, (k + 1) * LANES)
            value = own_values[:, first + k] + field[:, pick].reshape(rows, levels, LANES)
            values[:, first + k] = value
            x[:, 2 + first + k] = value * (own_weights[:, first + k] + weight[:, pick].reshape(rows, levels, LANES))
    for k in range(HALO):
        edge_values[0, k] = values[k]
        edge_values[1, k] = values[rows - 1 - k]

    linear, constant, scale = factors(kappa[...], 4 * members)

    def wrap(row):
        def target(c, value):
            x[row, c + 2] = value

        wrap_columns(row_of(x, row), target, fine)

    def wrap_first(row, _):
        wrap(row)
        return 0

    lax.fori_loop(0, rows, wrap_first, 0, unroll=True)

    for turn in range(PASSES):
        low = 2 * turn
        start, count = low + 2, rows - 4 * turn - 4
        for k in range(4):
            edges[0, turn, k] = x[low + k]
            edges[1, turn, k] = x[rows - 1 - low - k]

        v, _ = first_sweep(row_of(x, start - 2), row_of(x, start - 1), None, linear, fine)
        v, u = first_sweep(row_of(x, start - 1), row_of(x, start), v, linear, fine)
        v, u_next = first_sweep(row_of(x, start), row_of(x, start + 1), v, linear, fine)
        q, _ = second_sweep(None, u, u_next, None, constant, fine)
        u = u_next
        for i in range(start, start + count):
            v, u_next = first_sweep(row_of(x, i + 1), row_of(x, i + 2), v, linear, fine)
            q, y = second_sweep(row_of(x, i), u, u_next, q, constant, fine)
            u = u_next
            for c in range(fine):
                x[i, c + 2] = y[c]
            if turn < PASSES - 1:
                wrap(i)

    def last(i, _):
        first = i * HALO
        from_row = first + HALO
        product = jnp.concatenate(
            [
                (x[pl.ds(from_row, HALO), c + 2] * values[pl.ds(from_row, HALO), c]).reshape(HALO * levels, LANES)
                for c in range(fine)
            ],
            axis=1,
        )
        pick = pl.ds(pl.multiple_of(first, HALO), HALO)
        finish(
            product, back[...], scale,
            lambda lanes: taper[:, pl.ds(pl.multiple_of(from_row, HALO), HALO), lanes],
            lambda natural, lanes: to_owner(place, natural, keep, send, pick, lanes, levels),
            levels,
        )
        return 0

    lax.fori_loop(0, (rows - 2 * HALO) // HALO, last, 0)


def lift_kernel(top, bottom, to_fields, to_weights, main_values, main_weights):
    fine, levels = main_values.shape[2:4]
    count = top.shape[0]
    main = top.shape[1] - LANES
    for first in range(0, fine, 2):
        width = min(2, fine - first)
        lanes = slice(first * LANES, (first + width) * LANES)
        for edge, strip in enumerate((top, bottom)):
            field = dot(strip[:, :main], to_fields[:main, lanes])
            part = count // 4
            near = jnp.concatenate([strip[k * part : (k + 1) * part, main:] for k in range(4)], axis=1)
            weight = dot(near, to_weights[: 4 * LANES, lanes])
            for k in range(width):
                pick = slice(k * LANES, (k + 1) * LANES)
                main_values[edge, :, first + k] = field[:, pick].reshape(HALO, levels, LANES)
                main_weights[edge, :, first + k] = weight[:, pick].reshape(NEAR, levels, LANES)


def outer_kernel(
    place, taper, left, right, main_values, main_weights, edges, edge_values, keep_inner, send_inner,
    to_fields, to_weights, back, kappa,
    keep, send,
    x,
):
    levels, rows, cols = taper.shape
    fine = edge_values.shape[2]
    members = LANES * fine // (cols + 2 * HALO)
    keep[:, HALO : rows - HALO, :] = keep_inner[...]
    send[:, HALO : rows - HALO, :] = send_inner[...]
    packs = jnp.concatenate([left[...], right[...]], axis=1)
    size = HALO * levels
    near_packs = jnp.concatenate([packs[edge * size : edge * size + NEAR * levels] for edge in range(2)], axis=0)
    for first in range(0, fine, 2):
        width = min(2, fine - first)
        lanes = slice(first * LANES, (first + width) * LANES)
        field = dot(packs, to_fields[members * cols :, lanes])
        weight = dot(near_packs, to_weights[2 * cols :, lanes])
        for k in range(width):
            pick = slice(k * LANES, (k + 1) * LANES)
            part = field[:, pick].reshape(2, HALO, levels, LANES)
            near = weight[:, pick].reshape(2, NEAR, levels, LANES)
            for edge in range(2):
                for distance in range(HALO):
                    value = main_values[edge, distance, first + k] + part[edge, distance]
                    if distance < NEAR:
                        value = value * (main_weights[edge, distance, first + k] + near[edge, distance])
                    x[edge, HALO - 1 - distance, 2 + first + k] = value

    linear, constant, scale = factors(kappa[...], 4 * members)
    inside = [jnp.where(place[edge] == 1, 0.0, 1.0).astype(F32) for edge in range(2)]

    def wrap(edge, row):
        def target(c, value):
            x[edge, row, c + 2] = value

        wrap_columns(row_of(x, edge, row), target, fine)

    for row in range(HALO):
        for edge in range(2):
            wrap(edge, row)

    for turn in range(PASSES):
        low = 2 * turn
        for edge in range(2):
            def row_at(row):
                if row < low + HALO:
                    return row_of(x, edge, row)
                return row_of(edges, edge, turn, row - low - HALO)

            v = u = q = None
            for i in range(low, low + HALO + 3):
                v, u_next = first_sweep(row_at(i), row_at(i + 1), v, linear, fine)
                if u_next is None:
                    continue
                if i == HALO - 1:
                    u_next = {c: part * inside[edge] for c, part in u_next.items()}
                if u is not None:
                    q, y = second_sweep(row_at(i - 1), u, u_next, q, constant, fine)
                    if y is not None:
                        for c in range(fine):
                            x[edge, i - 1, c + 2] = y[c] * inside[edge] if i == HALO else y[c]
                u = u_next
            if turn < PASSES - 1:
                for row in range(low + 2, low + HALO + 2):
                    wrap(edge, row)

    for edge in range(2):
        order = range(HALO) if edge == 0 else range(HALO - 1, -1, -1)
        product = jnp.concatenate(
            [
                jnp.concatenate([x[edge, HALO + k, c + 2] * edge_values[edge, k, c] for k in order], axis=0)
                for c in range(fine)
            ],
            axis=1,
        )
        own = slice(edge * (rows - HALO), edge * (rows - HALO) + HALO)
        finish(
            product, back[...], scale,
            lambda lanes: taper[:, own, lanes],
            lambda natural, lanes: to_owner(place, natural, keep, send, own, lanes, levels),
            levels,
        )


def shifted(value, axis, step, wrap):
    count = lax.axis_size(axis)
    pairs = [(i, (i + step) % count) for i in range(count) if wrap or 0 <= i + step < count]
    return lax.ppermute(value, axis, pairs)


def local(perturbations, increment, taper_norm, kappa):
    members, levels, rows, cols = perturbations.shape
    fine = (cols + 2 * HALO) * members // LANES
    shape = jax.ShapeDtypeStruct
    tile = (levels, LANES)
    vmem = pl.BlockSpec(memory_space=pltpu.VMEM)
    smem = pl.BlockSpec(memory_space=pltpu.SMEM)
    hbm = pl.BlockSpec(memory_space=pltpu.HBM)

    def call(kernel, name, outs, ins, scratch=(), specs=None, limit=16):
        return pl.pallas_call(
            kernel,
            out_shape=tuple(outs),
            in_specs=specs or [vmem] * len(ins),
            out_specs=(vmem,) * len(outs),
            scratch_shapes=list(scratch),
            compiler_params=pltpu.CompilerParams(vmem_limit_bytes=limit * 1024 * 1024),
            name=name,
        )(*ins)

    strip = shape((HALO * levels, members * cols + LANES), BF16)
    pack = shape((levels, rows, LANES), BF16)
    whole = shape((levels, rows, cols), F32)
    up, down, to_left, to_right, p, g = call(
        start_kernel, "start",
        (strip, strip, pack, pack, shape(perturbations.shape, BF16), whole),
        (perturbations, increment, taper_norm),
        (pltpu.VMEM(whole.shape, F32), pltpu.VMEM(whole.shape, F32), pltpu.SemaphoreType.DMA((rows // HALO, 3))),
        specs=[hbm] * 3, limit=START_LIMIT,
    )
    top = shifted(down, "lat", 1, False)
    bottom = shifted(up, "lat", -1, False)
    left = shifted(to_right, "lon", 1, True)
    right = shifted(to_left, "lon", -1, True)

    kappa = jnp.broadcast_to(kappa[:, None], tile)
    lat, mem = lax.axis_index("lat"), lax.axis_index("mem")
    place = jnp.stack([
        (lat == 0).astype(jnp.int32),
        (lat == lax.axis_size("lat") - 1).astype(jnp.int32),
        mem % 2,
        mem // 2,
    ])

    values = shape((rows, fine, *tile), F32)
    own_values, own_weights, to_fields, to_weights, back = call(
        prepare_kernel, "prepare",
        (
            values, values,
            shape((members * cols + 2 * LANES, fine * LANES), BF16),
            shape((2 * cols + 2 * LANES, fine * LANES), BF16),
            shape((fine * LANES, cols), BF16),
        ),
        (p, g),
        (pltpu.VMEM((rows * levels, members * cols), BF16), pltpu.VMEM((rows * levels, 2 * cols), BF16)),

    )

    part = shape((levels // 2, rows - 2 * HALO, cols), F32)
    keep, send, edges, edge_values = call(
        inner_kernel, "inner",
        (part, part, shape((2, PASSES, 4, fine + 4, *tile), F32), shape((2, HALO, fine, *tile), F32)),
        (place, own_values, own_weights, taper_norm, left, right, to_fields, to_weights, back, kappa),
        (
            pltpu.VMEM((rows, fine + 4, *tile), F32),
            pltpu.VMEM((rows, fine, *tile), F32),
            pltpu.VMEM((rows * levels, 2 * LANES), BF16),
        ),
        specs=[smem] + [vmem] * 9,
    )
    top, bottom, edges = lax.optimization_barrier((top, bottom, edges))

    side = shape((2 * HALO * levels, LANES), BF16)
    to_left, to_right = call(corners_kernel, "corners", (side, side), (top, bottom))
    left = shifted(to_right, "lon", 1, True)
    right = shifted(to_left, "lon", -1, True)
    top, bottom, _, _ = lax.optimization_barrier((top, bottom, to_left, to_right))
    main_values, main_weights = call(
        lift_kernel, "lift",
        (shape((2, HALO, fine, *tile), F32), shape((2, NEAR, fine, *tile), F32)),
        (top, bottom, to_fields, to_weights),

    )
    part = shape((levels // 2, rows, cols), F32)
    keep, send = call(
        outer_kernel, "outer",
        (part, part),
        (
            place, taper_norm, left, right, main_values, main_weights, edges, edge_values, keep, send,
            to_fields, to_weights, back, kappa,
        ),
        (pltpu.VMEM((2, 2 * HALO, fine + 4, *tile), F32),),
        specs=[smem] + [vmem] * 13,
    )
    got = lax.ppermute(send, "mem", [(i, i ^ 1) for i in range(4)])
    crossing = lax.ppermute(keep[2:] + got[2:], "mem", [(i, i ^ 2) for i in range(4)])
    return keep[:2] + got[:2] + crossing


def solution(mesh):
    return jax.shard_map(
        local,
        mesh=mesh,
        in_specs=(P("mem", None, "lat", "lon"), P(None, "lat", "lon"), P(None, "lat", "lon"), P()),
        out_specs=P("mem", "lat", "lon"),
        check_vma=False,
    )
```

time: 64.6 us -> 47.2 us (0.73)
  the two profiles are of different devices: /device:TPU:22 before, /device:TPU:14 now
where the time goes in v2:
time: 47.2 us; the launch traced here: 46.9 us
  Pallas kernels  20.1 us (43%)
  starting transfers between devices  14.5 us (31%)
  waiting for transfers between devices  9.23 us (20%)
  local copies, waits for them, and re-layouts  2.16 us (5%)
  other arithmetic  0.78 us (2%)
    pallas_call x6, Pallas kernels, call(): pl.pallas_call(kernel, out_shape=tuple(outs), in_specs=specs or [vmem] *...  20.1 us
    ppermute x6, starting transfers between devices, shifted(): return lax.ppermute(value, axis, pairs)  12.4 us
    ppermute x6, waiting for transfers between devices, shifted(): return lax.ppermute(value, axis, pairs)  3.91 us
    ppermute x1, waiting for transfers between devices, local(): lax.ppermute(keep[2:] + got[2:], 'mem', [(i, i ^ 2) for i in range(4)])  3.8 us
    unnamed x8, local copies, waits for them, and re-layouts  2.09 us
    ppermute x1, starting transfers between devices, local(): lax.ppermute(keep[2:] + got[2:], 'mem', [(i, i ^ 2) for i in range(4)])  2 us
    ppermute x1, waiting for transfers between devices, local(): got = lax.ppermute(send, 'mem', [(i, i ^ 1) for i in range(4)])  1.52 us
  transfers between devices with their start and end apart: 8, of which 5 were waited for; matrix products, arithmetic and copies ran while one was open for 0% of the time, Pallas kernels for 26%

profile of v2, /device:TPU:14, one launch (start us, length us, event | category | flops | bytes accessed | tf_op | source)
XLA Modules:
  0.0 46.9 jit_solution(16486919001129767110)
XLA Ops:
  0.0 1.0 %copy-done = f32[8,64,256]{2,1,0:T(8,128)S(1)} copy-done((f32[8,64,256]{2,1,0:T(8,128)S(1)}, f32[8,64,256]{2,1,0:T(8,128)}, u32[]{:S(2)}) %copy-start) | copy-done | bytes 524312
  1.0 1.0 %copy-done.2 = f32[8,64,256]{2,1,0:T(8,128)S(1)} copy-done((f32[8,64,256]{2,1,0:T(8,128)S(1)}, f32[8,64,256]{2,1,0:T(8,128)}, u32[]{:S(2)}) %copy-start.2) | copy-done | bytes 524312
  2.1 2.7 %start.1 = (bf16[128,1152]{1,0:T(8,128)(2,1)S(1)}, bf16[128,1152]{1,0:T(8,128)(2,1)S(1)}, bf16[8,64,128]{2,1,0:T(8,128)(2,1)}, bf16[8,64,128]{2,1,0:T(8,128)(2,1...) custom-call(bf16[4,8,64,256]{3,2,1,0:T(8,128)(2,1)} %p_hbm.1, f32[8,64,256]{2,1,0:T(8,128)S(1)} %copy-done.2, ...), custom_call_target="tpu_custom_call" | custom-call | tf_op jit(solution)/shard_map/start/pallas_call | solution.py:452
  4.8 5.8 %collective-permute-start = (bf16[128,1152]{1,0:T(8,128)(2,1)S(1)}, bf16[128,1152]{1,0:T(8,128)(2,1)S(1)}, u32[]{:S(2)}, u32[]{:S(2)}) collective-permute-start(bf16[128,1152]{1,0:T(8,128)(2,1)S(1)} %get-tuple-element.31), channel_id=1, source_target_pairs={{0,4},{4,8},{8,12},{12,16},{16,20},{20,24},{24,28},{1,5},{5,9},{9,... | collective-permute-start | bytes 884744 | tf_op jit(solution)/shard_map/ppermute | solution.py:439
  10.6 2.5 %collective-permute-start.1 = (bf16[128,1152]{1,0:T(8,128)(2,1)S(1)}, bf16[128,1152]{1,0:T(8,128)(2,1)S(1)}, u32[]{:S(2)}, u32[]{:S(2)}) collective-permute-start(bf16[128,1152]{1,0:T(8,128)(2,1)S(1)} %get-tuple-element.32), channel_id=1, source_target_pairs={{4,0},{8,4},{12,8},{16,12},{20,16},{24,20},{28,24},{5,1},{9,5},{13... | collective-permute-start | bytes 884744 | tf_op jit(solution)/shard_map/ppermute | solution.py:439
  13.1 0.5 %collective-permute-start.2 = (bf16[8,64,128]{2,1,0:T(8,128)(2,1)}, bf16[8,64,128]{2,1,0:T(8,128)(2,1)S(1)}, u32[]{:S(2)}, u32[]{:S(2)}) collective-permute-start(bf16[8,64,128]{2,1,0:T(8,128)(2,1)} %get-tuple-element.37), channel_id=1, source_target_pairs={{0,1},{1,2},{2,3},{3,0},{4,5},{5,6},{6,7},{7,4},{8,9},{9,10},{10,1... | collective-permute-start | bytes 393224 | tf_op jit(solution)/shard_map/ppermute | solution.py:439
  13.6 1.5 %collective-permute-start.3 = (bf16[8,64,128]{2,1,0:T(8,128)(2,1)}, bf16[8,64,128]{2,1,0:T(8,128)(2,1)S(1)}, u32[]{:S(2)}, u32[]{:S(2)}) collective-permute-start(bf16[8,64,128]{2,1,0:T(8,128)(2,1)} %get-tuple-element.38), channel_id=1, source_target_pairs={{0,3},{1,0},{2,1},{3,2},{4,7},{5,4},{6,5},{7,6},{8,11},{9,8},{10,9... | collective-permute-start | bytes 393224 | tf_op jit(solution)/shard_map/ppermute | solution.py:439
  15.2 3.8 %prepare.1 = (f32[64,9,8,128]{3,2,1,0:T(8,128)S(1)}, f32[64,9,8,128]{3,2,1,0:T(8,128)S(1)}, bf16[1280,1152]{1,0:T(8,128)(2,1)S(1)}, bf16[768,1152]{1,0:T(8,128)(2,1)S(1)}, bf16[1152,256]{1,0:T(8,128)(2,1)S(1)}) custom-call(bf16[4,8,64,256]{3,2,1,0:T(8,128)(2,1)S(1)} %get-tuple-element.33.p, f32[8,64,256]{2,1,0:T(8,128)S(1)} %get-tuple-element.34.g), custom_call_target="tpu_custom_call" | custom-call | tf_op jit(solution)/shard_map/prepare/pallas_call | solution.py:452
  19.0 0.1 pad_add_fusion.place
  19.1 0.9 %collective-permute-done.3.right = bf16[8,64,128]{2,1,0:T(8,128)(2,1)S(1)} collective-permute-done((bf16[8,64,128]{2,1,0:T(8,128)(2,1)}, bf16[8,64,128]{2,1,0:T(8,128)(2,1)S(1)}, u32[]{:S(2)}, u32[]{:S(2)}) %collective-permute-start.3) | collective-permute-done | bytes 131104 | tf_op jit(solution)/shard_map/ppermute | solution.py:439
  20.0 0.1 broadcast_in_dim.2.kappa
  20.1 6.9 %inner.1 = (f32[4,32,256]{2,1,0:T(8,128)S(1)}, f32[4,32,256]{2,1,0:T(8,128)S(1)}, f32[2,8,4,13,8,128]{5,4,3,2,1,0:T(8,128)S(1)}, f32[2,16,9,8,128]{4,3,2,1,0:T(8,128)S(1)}) custom-call(s32[4]{0:T(128)S(1)} %pad_add_fusion.place, f32[64,9,8,128]{3,2,1,0:T(8,128)S(1)} %get-tuple-element.35.own_values, f32[64,9,8,128]{3,2,1,0:T(8,128)S(1)} %get-tuple-element.36.own_weights, ...), custom_call_target="tpu_custom_call" | custom-call | tf_op jit(solution)/shard_map/inner/pallas_call | solution.py:452
  27.1 0.2 corners.1
  27.3 0.9 %collective-permute-start.4 = (bf16[256,128]{1,0:T(8,128)(2,1)S(1)}, bf16[256,128]{1,0:T(8,128)(2,1)S(1)}, u32[]{:S(2)}, u32[]{:S(2)}) collective-permute-start(bf16[256,128]{1,0:T(8,128)(2,1)S(1)} %get-tuple-element.45), channel_id=1, source_target_pairs={{0,1},{1,2},{2,3},{3,0},{4,5},{5,6},{6,7},{7,4},{8,9},{9,10},{10,1... | collective-permute-start | bytes 196616 | tf_op jit(solution)/shard_map/ppermute | solution.py:439
  28.2 1.2 %collective-permute-start.5 = (bf16[256,128]{1,0:T(8,128)(2,1)S(1)}, bf16[256,128]{1,0:T(8,128)(2,1)S(1)}, u32[]{:S(2)}, u32[]{:S(2)}) collective-permute-start(bf16[256,128]{1,0:T(8,128)(2,1)S(1)} %get-tuple-element.46), channel_id=1, source_target_pairs={{0,3},{1,0},{2,1},{3,2},{4,7},{5,4},{6,5},{7,6},{8,11},{9,8},{10,9... | collective-permute-start | bytes 196616 | tf_op jit(solution)/shard_map/ppermute | solution.py:439
  29.4 1.2 %lift.1 = (f32[2,16,9,8,128]{4,3,2,1,0:T(8,128)S(1)}, f32[2,4,9,8,128]{4,3,2,1,0:T(8,128)S(1)}) custom-call(bf16[128,1152]{1,0:T(8,128)(2,1)S(1)} %collective-permute-done.top, bf16[128,1152]{1,0:T(8,128)(2,1)S(1)} %collective-permute-done.1.bottom, bf16[1280,1152]{1,0:T(8,128)(2,1)S(1)} %get-tuple-element.39.to_fields, ...), custom_call_target="tpu_custom_call" | custom-call | tf_op jit(solution)/shard_map/lift/pallas_call | solution.py:452
  30.6 1.0 %collective-permute-done.4.left = bf16[256,128]{1,0:T(8,128)(2,1)S(1)} collective-permute-done((bf16[256,128]{1,0:T(8,128)(2,1)S(1)}, bf16[256,128]{1,0:T(8,128)(2,1)S(1)}, u32[]{:S(2)}, u32[]{:S(2)}) %collective-permute-start.4) | collective-permute-done | bytes 65568 | tf_op jit(solution)/shard_map/ppermute | solution.py:439
  31.6 2.0 %collective-permute-done.5.right = bf16[256,128]{1,0:T(8,128)(2,1)S(1)} collective-permute-done((bf16[256,128]{1,0:T(8,128)(2,1)S(1)}, bf16[256,128]{1,0:T(8,128)(2,1)S(1)}, u32[]{:S(2)}, u32[]{:S(2)}) %collective-permute-start.5) | collective-permute-done | bytes 65568 | tf_op jit(solution)/shard_map/ppermute | solution.py:439
  33.6 5.2 %outer.1 = (f32[4,64,256]{2,1,0:T(8,128)S(1)}, f32[4,64,256]{2,1,0:T(8,128)S(1)}) custom-call(s32[4]{0:T(128)S(1)} %pad_add_fusion.place, f32[8,64,256]{2,1,0:T(8,128)S(1)} %copy-done.1, bf16[256,128]{1,0:T(8,128)(2,1)S(1)} %collective-permute-done.4.left, bf16[256,128]{1,0:T(8,128)(2,1)S(1)} %collective-permute-done.5.right, ...), custom_call_target="tpu_custom_call" | custom-call | tf_op jit(solution)/shard_map/outer/pallas_call | solution.py:452
  38.8 0.1 collective-permute-start.6
  38.9 1.5 %collective-permute-done.6 = f32[4,64,256]{2,1,0:T(8,128)S(1)} collective-permute-done((f32[4,64,256]{2,1,0:T(8,128)S(1)}, f32[4,64,256]{2,1,0:T(8,128)S(1)}, u32[]{:S(2)}, u32[]{:S(2)}) %collective-permute-start.6) | collective-permute-done | bytes 262176 | tf_op jit(solution)/shard_map/ppermute | solution.py:536
  40.4 2.0 %collective-permute-start.7 = (f32[2,64,256]{2,1,0:T(8,128)S(1)}, f32[2,64,256]{2,1,0:T(8,128)S(1)}, u32[]{:S(2)}, u32[]{:S(2)}) collective-permute-start(f32[2,64,256]{2,1,0:T(8,128)S(1)} %slice_add_fusion), channel_id=1, source_target_pairs={{0,64},{32,96},{64,0},{96,32},{1,65},{33,97},{65,1},{97,33},{2,66}... | collective-permute-start | bytes 393224 | tf_op jit(solution)/shard_map/ppermute | solution.py:537
  42.4 3.8 %collective-permute-done.7 = f32[2,64,256]{2,1,0:T(8,128)S(1)} collective-permute-done((f32[2,64,256]{2,1,0:T(8,128)S(1)}, f32[2,64,256]{2,1,0:T(8,128)S(1)}, u32[]{:S(2)}, u32[]{:S(2)}) %collective-permute-start.7) | collective-permute-done | bytes 131104 | tf_op jit(solution)/shard_map/ppermute | solution.py:537
  46.2 0.7 %fusion = f32[2,64,256]{2,1,0:T(8,128)} fusion(f32[2,64,256]{2,1,0:T(8,128)S(1)} %collective-permute-done.7, f32[4,64,256]{2,1,0:T(8,128)S(1)} %collective-permute-done.6, f32[4,64,256]{2,1,0:T(8,128)S(1)} %get-tuple-element.55), kind=kLoop, calls=%fused_computation.2 | loop fusion | flops 65536 | bytes 524288 | tf_op jit(solution)/shard_map/add | solution.py:538
  (10 shorter events, 0.0 us)
Async XLA Ops:
  0.0 1.0 %copy-start = (f32[8,64,256]{2,1,0:T(8,128)S(1)}, f32[8,64,256]{2,1,0:T(8,128)}, u32[]{:S(2)}) copy-start(f32[8,64,256]{2,1,0:T(8,128)} %taper.3) | copy-start | bytes 1572868
  1.0 1.0 %copy-start.2 = (f32[8,64,256]{2,1,0:T(8,128)S(1)}, f32[8,64,256]{2,1,0:T(8,128)}, u32[]{:S(2)}) copy-start(f32[8,64,256]{2,1,0:T(8,128)} %increment_hbm.1) | copy-start | bytes 1572868
  2.1 18.0 %copy-start.3 = (f32[8]{0:T(128)S(1)}, f32[8]{0:T(128)}, u32[]{:S(2)}) copy-start(f32[8]{0:T(128)} %param.7) | copy-start | bytes 100
  2.1 18.0 %copy-start.1 = (f32[8,64,256]{2,1,0:T(8,128)S(1)}, f32[8,64,256]{2,1,0:T(8,128)}, u32[]{:S(2)}) copy-start(f32[8,64,256]{2,1,0:T(8,128)} %taper.3) | copy-start | bytes 1572868
  4.8 22.2 %collective-permute-start = (bf16[128,1152]{1,0:T(8,128)(2,1)S(1)}, bf16[128,1152]{1,0:T(8,128)(2,1)S(1)}, u32[]{:S(2)}, u32[]{:S(2)}) collective-permute-start(bf16[128,1152]{1,0:T(8,128)(2,1)S(1)} %get-tuple-element.31), channel_id=1, source_target_pairs={{0,4},{4,8},{8,12},{12,16},{16,20},{20,24},{24,28},{1,5},{5,9},{9,... | collective-permute-start | bytes 884744 | tf_op jit(solution)/shard_map/ppermute | solution.py:439
  10.6 16.4 %collective-permute-start.1 = (bf16[128,1152]{1,0:T(8,128)(2,1)S(1)}, bf16[128,1152]{1,0:T(8,128)(2,1)S(1)}, u32[]{:S(2)}, u32[]{:S(2)}) collective-permute-start(bf16[128,1152]{1,0:T(8,128)(2,1)S(1)} %get-tuple-element.32), channel_id=1, source_target_pairs={{4,0},{8,4},{12,8},{16,12},{20,16},{24,20},{28,24},{5,1},{9,5},{13... | collective-permute-start | bytes 884744 | tf_op jit(solution)/shard_map/ppermute | solution.py:439
  13.1 6.0 %collective-permute-start.2 = (bf16[8,64,128]{2,1,0:T(8,128)(2,1)}, bf16[8,64,128]{2,1,0:T(8,128)(2,1)S(1)}, u32[]{:S(2)}, u32[]{:S(2)}) collective-permute-start(bf16[8,64,128]{2,1,0:T(8,128)(2,1)} %get-tuple-element.37), channel_id=1, source_target_pairs={{0,1},{1,2},{2,3},{3,0},{4,5},{5,6},{6,7},{7,4},{8,9},{9,10},{10,1... | collective-permute-start | bytes 393224 | tf_op jit(solution)/shard_map/ppermute | solution.py:439
  13.6 6.4 %collective-permute-start.3 = (bf16[8,64,128]{2,1,0:T(8,128)(2,1)}, bf16[8,64,128]{2,1,0:T(8,128)(2,1)S(1)}, u32[]{:S(2)}, u32[]{:S(2)}) collective-permute-start(bf16[8,64,128]{2,1,0:T(8,128)(2,1)} %get-tuple-element.38), channel_id=1, source_target_pairs={{0,3},{1,0},{2,1},{3,2},{4,7},{5,4},{6,5},{7,6},{8,11},{9,8},{10,9... | collective-permute-start | bytes 393224 | tf_op jit(solution)/shard_map/ppermute | solution.py:439
  27.3 4.3 %collective-permute-start.4 = (bf16[256,128]{1,0:T(8,128)(2,1)S(1)}, bf16[256,128]{1,0:T(8,128)(2,1)S(1)}, u32[]{:S(2)}, u32[]{:S(2)}) collective-permute-start(bf16[256,128]{1,0:T(8,128)(2,1)S(1)} %get-tuple-element.45), channel_id=1, source_target_pairs={{0,1},{1,2},{2,3},{3,0},{4,5},{5,6},{6,7},{7,4},{8,9},{9,10},{10,1... | collective-permute-start | bytes 196616 | tf_op jit(solution)/shard_map/ppermute | solution.py:439
  28.2 5.5 %collective-permute-start.5 = (bf16[256,128]{1,0:T(8,128)(2,1)S(1)}, bf16[256,128]{1,0:T(8,128)(2,1)S(1)}, u32[]{:S(2)}, u32[]{:S(2)}) collective-permute-start(bf16[256,128]{1,0:T(8,128)(2,1)S(1)} %get-tuple-element.46), channel_id=1, source_target_pairs={{0,3},{1,0},{2,1},{3,2},{4,7},{5,4},{6,5},{7,6},{8,11},{9,8},{10,9... | collective-permute-start | bytes 196616 | tf_op jit(solution)/shard_map/ppermute | solution.py:439
  38.8 1.6 %collective-permute-start.6 = (f32[4,64,256]{2,1,0:T(8,128)S(1)}, f32[4,64,256]{2,1,0:T(8,128)S(1)}, u32[]{:S(2)}, u32[]{:S(2)}) collective-permute-start(f32[4,64,256]{2,1,0:T(8,128)S(1)} %get-tuple-element.56), channel_id=1, source_target_pairs={{0,32},{32,0},{64,96},{96,64},{1,33},{33,1},{65,97},{97,65},{2,34}... | collective-permute-start | bytes 786440 | tf_op jit(solution)/shard_map/ppermute | solution.py:536
  40.4 5.8 %collective-permute-start.7 = (f32[2,64,256]{2,1,0:T(8,128)S(1)}, f32[2,64,256]{2,1,0:T(8,128)S(1)}, u32[]{:S(2)}, u32[]{:S(2)}) collective-permute-start(f32[2,64,256]{2,1,0:T(8,128)S(1)} %slice_add_fusion), channel_id=1, source_target_pairs={{0,64},{32,96},{64,0},{96,32},{1,65},{33,97},{65,1},{97,33},{2,66}... | collective-permute-start | bytes 393224 | tf_op jit(solution)/shard_map/ppermute | solution.py:537

commit v3 on v2

--- a/solution.py
+++ b/solution.py
@@ -9,7 +9,6 @@
 HALO = 2 * PASSES
 LANES = 128
 NEAR = 4
-START_LIMIT = 50
 BF16 = jnp.bfloat16
 F32 = jnp.float32
 
@@ -68,7 +67,7 @@
     return jnp.swapaxes(value.astype(F32), 0, 1)
 
 
-def start_kernel(p_hbm, increment_hbm, taper_hbm, up, down, to_left, to_right, p, g, taper, increment, sems):
+def start_kernel(place, p_hbm, increment_hbm, taper_hbm, to_near, to_far, to_left, to_right, p, g, taper, increment, sems):
     members, levels, rows, cols = p.shape
     copies = []
     for i in (0, rows // HALO - 1, *range(1, rows // HALO - 1)):
@@ -116,10 +115,16 @@
         for copy in group:
             copy.wait()
         g[:, pick, :] = increment[:, pick, :] * taper[:, pick, :]
-        if k == 0:
-            strip(up, pick, range(HALO))
-        if k == 1:
-            strip(down, pick, range(HALO - 1, -1, -1))
+        if k < 2:
+            order = range(HALO) if k == 0 else range(HALO - 1, -1, -1)
+
+            @pl.when(place[1] == k)
+            def _():
+                strip(to_near, pick, order)
+
+            @pl.when(place[1] != k)
+            def _():
+                strip(to_far, pick, order)
         to_left[:, pick, :] = packed(pick, slice(0, LANES), 0)
         to_right[:, pick, :] = packed(pick, slice(cols - LANES, cols), HALO)
 
@@ -268,9 +273,10 @@
             value = own_values[:, first + k] + field[:, pick].reshape(rows, levels, LANES)
             values[:, first + k] = value
             x[:, 2 + first + k] = value * (own_weights[:, first + k] + weight[:, pick].reshape(rows, levels, LANES))
+    upper, lower = place[1], 1 - place[1]
     for k in range(HALO):
-        edge_values[0, k] = values[k]
-        edge_values[1, k] = values[rows - 1 - k]
+        edge_values[upper, k] = values[k]
+        edge_values[lower, k] = values[rows - 1 - k]
 
     linear, constant, scale = factors(kappa[...], 4 * members)
 
@@ -290,8 +296,8 @@
         low = 2 * turn
         start, count = low + 2, rows - 4 * turn - 4
         for k in range(4):
-            edges[0, turn, k] = x[low + k]
-            edges[1, turn, k] = x[rows - 1 - low - k]
+            edges[upper, turn, k] = x[low + k]
+            edges[lower, turn, k] = x[rows - 1 - low - k]
 
         v, _ = first_sweep(row_of(x, start - 2), row_of(x, start - 1), None, linear, fine)
         v, u = first_sweep(row_of(x, start - 1), row_of(x, start), v, linear, fine)
@@ -348,7 +354,7 @@
 
 
 def outer_kernel(
-    place, taper, left, right, main_values, main_weights, edges, edge_values, keep_inner, send_inner,
+    place, taper, left, right, main_values, main_weights, edges, edge_values,
     to_fields, to_weights, back, kappa,
     keep, send,
     x,
@@ -356,8 +362,8 @@
     levels, rows, cols = taper.shape
     fine = edge_values.shape[2]
     members = LANES * fine // (cols + 2 * HALO)
-    keep[:, HALO : rows - HALO, :] = keep_inner[...]
-    send[:, HALO : rows - HALO, :] = send_inner[...]
+    linear, constant, scale = factors(kappa[...], 4 * members)
+    inside = jnp.where(place[0] == 1, 0.0, 1.0).astype(F32)
     packs = jnp.concatenate([left[...], right[...]], axis=1)
     size = HALO * levels
     near_packs = jnp.concatenate([packs[edge * size : edge * size + NEAR * levels] for edge in range(2)], axis=0)
@@ -375,10 +381,10 @@
                     value = main_values[edge, distance, first + k] + part[edge, distance]
                     if distance < NEAR:
                         value = value * (main_weights[edge, distance, first + k] + near[edge, distance])
+                    if edge == 1 and distance == 0:
+                        value = value * inside
                     x[edge, HALO - 1 - distance, 2 + first + k] = value
 
-    linear, constant, scale = factors(kappa[...], 4 * members)
-    inside = [jnp.where(place[edge] == 1, 0.0, 1.0).astype(F32) for edge in range(2)]
 
     def wrap(edge, row):
         def target(c, value):
@@ -403,13 +409,13 @@
                 v, u_next = first_sweep(row_at(i), row_at(i + 1), v, linear, fine)
                 if u_next is None:
                     continue
-                if i == HALO - 1:
-                    u_next = {c: part * inside[edge] for c, part in u_next.items()}
+                if edge == 1 and i == HALO - 1:
+                    u_next = {c: part * inside for c, part in u_next.items()}
                 if u is not None:
                     q, y = second_sweep(row_at(i - 1), u, u_next, q, constant, fine)
                     if y is not None:
                         for c in range(fine):
-                            x[edge, i - 1, c + 2] = y[c] * inside[edge] if i == HALO else y[c]
+                            x[edge, i - 1, c + 2] = y[c] * inside if edge == 1 and i == HALO else y[c]
                 u = u_next
             if turn < PASSES - 1:
                 for row in range(low + 2, low + HALO + 2):
@@ -417,18 +423,20 @@
 
     for edge in range(2):
         order = range(HALO) if edge == 0 else range(HALO - 1, -1, -1)
+        slot = place[1] if edge == 0 else 1 - place[1]
         product = jnp.concatenate(
             [
-                jnp.concatenate([x[edge, HALO + k, c + 2] * edge_values[edge, k, c] for k in order], axis=0)
+                jnp.concatenate([x[slot, HALO + k, c + 2] * edge_values[slot, k, c] for k in order], axis=0)
                 for c in range(fine)
             ],
             axis=1,
         )
         own = slice(edge * (rows - HALO), edge * (rows - HALO) + HALO)
+        pick = slice(edge * HALO, (edge + 1) * HALO)
         finish(
             product, back[...], scale,
             lambda lanes: taper[:, own, lanes],
-            lambda natural, lanes: to_owner(place, natural, keep, send, own, lanes, levels),
+            lambda natural, lanes: to_owner(place, natural, keep, send, pick, lanes, levels),
             levels,
         )
 
@@ -437,6 +445,15 @@
     count = lax.axis_size(axis)
     pairs = [(i, (i + step) % count) for i in range(count) if wrap or 0 <= i + step < count]
     return lax.ppermute(value, axis, pairs)
+
+
+def over_core(keep, send):
+    got = lax.ppermute(send, "mem", [(i, i ^ 1) for i in range(4)])
+    return keep[:2] + got[:2], keep[2:] + got[2:]
+
+
+def over_plane(here, there):
+    return here + lax.ppermute(there, "mem", [(i, i ^ 2) for i in range(4)])
 
 
 def local(perturbations, increment, taper_norm, kappa):
@@ -448,40 +465,41 @@
     smem = pl.BlockSpec(memory_space=pltpu.SMEM)
     hbm = pl.BlockSpec(memory_space=pltpu.HBM)
 
-    def call(kernel, name, outs, ins, scratch=(), specs=None, limit=16):
+    def call(kernel, name, outs, ins, scratch=(), specs=None):
         return pl.pallas_call(
             kernel,
             out_shape=tuple(outs),
             in_specs=specs or [vmem] * len(ins),
             out_specs=(vmem,) * len(outs),
             scratch_shapes=list(scratch),
-            compiler_params=pltpu.CompilerParams(vmem_limit_bytes=limit * 1024 * 1024),
+            compiler_params=pltpu.CompilerParams(vmem_limit_bytes=20 * 1024 * 1024),
             name=name,
         )(*ins)
 
     strip = shape((HALO * levels, members * cols + LANES), BF16)
     pack = shape((levels, rows, LANES), BF16)
     whole = shape((levels, rows, cols), F32)
-    up, down, to_left, to_right, p, g = call(
-        start_kernel, "start",
-        (strip, strip, pack, pack, shape(perturbations.shape, BF16), whole),
-        (perturbations, increment, taper_norm),
-        (pltpu.VMEM(whole.shape, F32), pltpu.VMEM(whole.shape, F32), pltpu.SemaphoreType.DMA((rows // HALO, 3))),
-        specs=[hbm] * 3, limit=START_LIMIT,
-    )
-    top = shifted(down, "lat", 1, False)
-    bottom = shifted(up, "lat", -1, False)
-    left = shifted(to_right, "lon", 1, True)
-    right = shifted(to_left, "lon", -1, True)
-
     kappa = jnp.broadcast_to(kappa[:, None], tile)
     lat, mem = lax.axis_index("lat"), lax.axis_index("mem")
+    count = lax.axis_size("lat")
     place = jnp.stack([
-        (lat == 0).astype(jnp.int32),
-        (lat == lax.axis_size("lat") - 1).astype(jnp.int32),
+        ((lat == 0) | (lat == count - 1)).astype(jnp.int32),
+        1 - lat % 2,
         mem % 2,
         mem // 2,
     ])
+
+    to_near, to_far, to_left, to_right, p, g = call(
+        start_kernel, "start",
+        (strip, strip, pack, pack, shape(perturbations.shape, BF16), whole),
+        (place, *(pltpu.with_memory_space_constraint(a, pltpu.HBM) for a in (perturbations, increment, taper_norm))),
+        (pltpu.VMEM(whole.shape, F32), pltpu.VMEM(whole.shape, F32), pltpu.SemaphoreType.DMA((rows // HALO, 3))),
+        specs=[smem] + [hbm] * 3,
+    )
+    near = lax.ppermute(to_near, "lat", [(i, i ^ 1) for i in range(count)])
+    far = lax.ppermute(to_far, "lat", [(i, (i + 1 - 2 * (1 - i % 2)) % count) for i in range(count)])
+    left = shifted(to_right, "lon", 1, True)
+    right = shifted(to_left, "lon", -1, True)
 
     values = shape((rows, fine, *tile), F32)
     own_values, own_weights, to_fields, to_weights, back = call(
@@ -494,7 +512,6 @@
         ),
         (p, g),
         (pltpu.VMEM((rows * levels, members * cols), BF16), pltpu.VMEM((rows * levels, 2 * cols), BF16)),
-
     )
 
     part = shape((levels // 2, rows - 2 * HALO, cols), F32)
@@ -509,33 +526,34 @@
         ),
         specs=[smem] + [vmem] * 9,
     )
-    top, bottom, edges = lax.optimization_barrier((top, bottom, edges))
+    near, far, edges = lax.optimization_barrier((near, far, edges))
 
     side = shape((2 * HALO * levels, LANES), BF16)
-    to_left, to_right = call(corners_kernel, "corners", (side, side), (top, bottom))
+    to_left, to_right = call(corners_kernel, "corners", (side, side), (near, far))
     left = shifted(to_right, "lon", 1, True)
     right = shifted(to_left, "lon", -1, True)
-    top, bottom, _, _ = lax.optimization_barrier((top, bottom, to_left, to_right))
+    near, far, send, to_left, _ = lax.optimization_barrier((near, far, send, to_left, to_right))
+    here, there = over_core(keep, send)
     main_values, main_weights = call(
         lift_kernel, "lift",
         (shape((2, HALO, fine, *tile), F32), shape((2, NEAR, fine, *tile), F32)),
-        (top, bottom, to_fields, to_weights),
-
+        (near, far, to_fields, to_weights),
     )
-    part = shape((levels // 2, rows, cols), F32)
+    here, there, edges = lax.optimization_barrier((here, there, edges))
+    middle = over_plane(here, there)
+    part = shape((levels // 2, 2 * HALO, cols), F32)
     keep, send = call(
         outer_kernel, "outer",
         (part, part),
         (
-            place, taper_norm, left, right, main_values, main_weights, edges, edge_values, keep, send,
+            place, taper_norm, left, right, main_values, main_weights, edges, edge_values,
             to_fields, to_weights, back, kappa,
         ),
         (pltpu.VMEM((2, 2 * HALO, fine + 4, *tile), F32),),
-        specs=[smem] + [vmem] * 13,
+        specs=[smem] + [vmem] * 11,
     )
-    got = lax.ppermute(send, "mem", [(i, i ^ 1) for i in range(4)])
-    crossing = lax.ppermute(keep[2:] + got[2:], "mem", [(i, i ^ 2) for i in range(4)])
-    return keep[:2] + got[:2] + crossing
+    outside = over_plane(*over_core(keep, send))
+    return jnp.concatenate([outside[:, :HALO], middle, outside[:, HALO:]], axis=1)
 
 
 def solution(mesh):

time: 47.2 us -> 42.4 us (0.90)
  the two profiles are of different devices: /device:TPU:14 before, /device:TPU:1 now
where the time goes in v3:
time: 42.4 us; the launch traced here: 42.1 us
  Pallas kernels  20.6 us (49%)
  starting transfers between devices  17.2 us (41%)
  waiting for transfers between devices  3.26 us (8%)
  other arithmetic  0.8 us (2%)
    pallas_call x6, Pallas kernels, call(): pl.pallas_call(kernel, out_shape=tuple(outs), in_specs=specs or [vmem] *...  20.6 us
    ppermute x4, starting transfers between devices, shifted(): return lax.ppermute(value, axis, pairs)  5.37 us
    ppermute x1, starting transfers between devices, local(): near = lax.ppermute(to_near, 'lat', [(i, i ^ 1) for i in range(count)])  4.51 us
    ppermute x2, starting transfers between devices, over_core(): got = lax.ppermute(send, 'mem', [(i, i ^ 1) for i in range(4)])  2.56 us
    ppermute x1, starting transfers between devices, local(): lax.ppermute(to_far, 'lat', [(i, (i + 1 - 2 * (1 - i % 2)) % count) for i...  2.54 us
    ppermute x2, starting transfers between devices, over_plane(): return here + lax.ppermute(there, 'mem', [(i, i ^ 2) for i in range(4)])  2.26 us
    ppermute x2, waiting for transfers between devices, over_plane(): return here + lax.ppermute(there, 'mem', [(i, i ^ 2) for i in range(4)])  2.25 us
    ppermute x4, waiting for transfers between devices, shifted(): return lax.ppermute(value, axis, pairs)  1 us
  transfers between devices with their start and end apart: 10, of which 3 were waited for; matrix products, arithmetic and copies ran while one was open for 0% of the time, Pallas kernels for 29%

profile of v3, /device:TPU:1, one launch (start us, length us, event | category | flops | bytes accessed | tf_op | source)
XLA Modules:
  0.0 42.1 jit_solution(3838728312392976102)
XLA Ops:
  0.0 0.1 pad_add_fusion.place
  0.1 2.7 %start.1 = (bf16[128,1152]{1,0:T(8,128)(2,1)S(1)}, bf16[128,1152]{1,0:T(8,128)(2,1)S(1)}, bf16[8,64,128]{2,1,0:T(8,128)(2,1)S(1)}, bf16[8,64,128]{2,1,0:T(8,128)...) custom-call(s32[4]{0:T(128)S(1)} %pad_add_fusion.place, bf16[4,8,64,256]{3,2,1,0:T(8,128)(2,1)} %p_hbm.1, ...), custom_call_target="tpu_custom_call" | custom-call | tf_op jit(solution)/shard_map/start/pallas_call | solution.py:469
  2.8 4.5 %collective-permute-start = (bf16[128,1152]{1,0:T(8,128)(2,1)S(1)}, bf16[128,1152]{1,0:T(8,128)(2,1)S(1)}, u32[]{:S(2)}, u32[]{:S(2)}) collective-permute-start(bf16[128,1152]{1,0:T(8,128)(2,1)S(1)} %get-tuple-element.35), channel_id=1, source_target_pairs={{0,4},{4,0},{8,12},{12,8},{16,20},{20,16},{24,28},{28,24},{1,5},{5... | collective-permute-start | bytes 884744 | tf_op jit(solution)/shard_map/ppermute | solution.py:499
  7.3 2.5 %collective-permute-start.1 = (bf16[128,1152]{1,0:T(8,128)(2,1)S(1)}, bf16[128,1152]{1,0:T(8,128)(2,1)S(1)}, u32[]{:S(2)}, u32[]{:S(2)}) collective-permute-start(bf16[128,1152]{1,0:T(8,128)(2,1)S(1)} %get-tuple-element.36), channel_id=1, source_target_pairs={{0,28},{4,8},{8,4},{12,16},{16,12},{20,24},{24,20},{28,0},{1,29},{... | collective-permute-start | bytes 884744 | tf_op jit(solution)/shard_map/ppermute | solution.py:500
  9.9 1.2 %collective-permute-start.2 = (bf16[8,64,128]{2,1,0:T(8,128)(2,1)S(1)}, bf16[8,64,128]{2,1,0:T(8,128)(2,1)S(1)}, u32[]{:S(2)}, u32[]{:S(2)}) collective-permute-start(bf16[8,64,128]{2,1,0:T(8,128)(2,1)S(1)} %get-tuple-element.41), channel_id=1, source_target_pairs={{0,1},{1,2},{2,3},{3,0},{4,5},{5,6},{6,7},{7,4},{8,9},{9,10},{10,1... | collective-permute-start | bytes 393224 | tf_op jit(solution)/shard_map/ppermute | solution.py:447
  11.1 1.5 %collective-permute-start.3 = (bf16[8,64,128]{2,1,0:T(8,128)(2,1)S(1)}, bf16[8,64,128]{2,1,0:T(8,128)(2,1)S(1)}, u32[]{:S(2)}, u32[]{:S(2)}) collective-permute-start(bf16[8,64,128]{2,1,0:T(8,128)(2,1)S(1)} %get-tuple-element.42), channel_id=1, source_target_pairs={{0,3},{1,0},{2,1},{3,2},{4,7},{5,4},{6,5},{7,6},{8,11},{9,8},{10,9... | collective-permute-start | bytes 393224 | tf_op jit(solution)/shard_map/ppermute | solution.py:447
  12.6 3.8 %prepare.1 = (f32[64,9,8,128]{3,2,1,0:T(8,128)S(1)}, f32[64,9,8,128]{3,2,1,0:T(8,128)S(1)}, bf16[1280,1152]{1,0:T(8,128)(2,1)S(1)}, bf16[768,1152]{1,0:T(8,128)(2,1)S(1)}, bf16[1152,256]{1,0:T(8,128)(2,1)S(1)}) custom-call(bf16[4,8,64,256]{3,2,1,0:T(8,128)(2,1)S(1)} %get-tuple-element.37.p, f32[8,64,256]{2,1,0:T(8,128)S(1)} %get-tuple-element.38.g), custom_call_target="tpu_custom_call" | custom-call | tf_op jit(solution)/shard_map/prepare/pallas_call | solution.py:469
  16.4 0.0 collective-permute-done.3.right
  16.4 0.1 broadcast_in_dim.2.kappa
  16.5 7.1 %inner.1 = (f32[4,32,256]{2,1,0:T(8,128)S(1)}, f32[4,32,256]{2,1,0:T(8,128)S(1)}, f32[2,8,4,13,8,128]{5,4,3,2,1,0:T(8,128)S(1)}, f32[2,16,9,8,128]{4,3,2,1,0:T(8,128)S(1)}) custom-call(s32[4]{0:T(128)S(1)} %pad_add_fusion.place, f32[64,9,8,128]{3,2,1,0:T(8,128)S(1)} %get-tuple-element.39.own_values, f32[64,9,8,128]{3,2,1,0:T(8,128)S(1)} %get-tuple-element.40.own_weights, ...), custom_call_target="tpu_custom_call" | custom-call | tf_op jit(solution)/shard_map/inner/pallas_call | solution.py:469
  23.6 0.2 corners.1
  23.8 1.6 %collective-permute-start.6 = (f32[4,32,256]{2,1,0:T(8,128)S(1)}, f32[4,32,256]{2,1,0:T(8,128)S(1)}, u32[]{:S(2)}, u32[]{:S(2)}) collective-permute-start(f32[4,32,256]{2,1,0:T(8,128)S(1)} %get-tuple-element.57), channel_id=1, source_target_pairs={{0,32},{32,0},{64,96},{96,64},{1,33},{33,1},{65,97},{97,65},{2,34}... | collective-permute-start | bytes 393224 | tf_op jit(solution)/shard_map/ppermute | solution.py:451
  25.4 0.6 %collective-permute-start.4 = (bf16[256,128]{1,0:T(8,128)(2,1)S(1)}, bf16[256,128]{1,0:T(8,128)(2,1)S(1)}, u32[]{:S(2)}, u32[]{:S(2)}) collective-permute-start(bf16[256,128]{1,0:T(8,128)(2,1)S(1)} %get-tuple-element.49), channel_id=1, source_target_pairs={{0,1},{1,2},{2,3},{3,0},{4,5},{5,6},{6,7},{7,4},{8,9},{9,10},{10,1... | collective-permute-start | bytes 196616 | tf_op jit(solution)/shard_map/ppermute | solution.py:447
  26.0 2.1 %collective-permute-start.5 = (bf16[256,128]{1,0:T(8,128)(2,1)S(1)}, bf16[256,128]{1,0:T(8,128)(2,1)S(1)}, u32[]{:S(2)}, u32[]{:S(2)}) collective-permute-start(bf16[256,128]{1,0:T(8,128)(2,1)S(1)} %get-tuple-element.50), channel_id=1, source_target_pairs={{0,3},{1,0},{2,1},{3,2},{4,7},{5,4},{6,5},{7,6},{8,11},{9,8},{10,9... | collective-permute-start | bytes 196616 | tf_op jit(solution)/shard_map/ppermute | solution.py:447
  28.1 1.1 %lift.1 = (f32[2,16,9,8,128]{4,3,2,1,0:T(8,128)S(1)}, f32[2,4,9,8,128]{4,3,2,1,0:T(8,128)S(1)}) custom-call(bf16[128,1152]{1,0:T(8,128)(2,1)S(1)} %collective-permute-done.top, bf16[128,1152]{1,0:T(8,128)(2,1)S(1)} %collective-permute-done.1.bottom, bf16[1280,1152]{1,0:T(8,128)(2,1)S(1)} %get-tuple-element.43.to_fields, ...), custom_call_target="tpu_custom_call" | custom-call | tf_op jit(solution)/shard_map/lift/pallas_call | solution.py:469
  29.3 0.0 collective-permute-done.6
  29.3 1.0 %collective-permute-done.4.left = bf16[256,128]{1,0:T(8,128)(2,1)S(1)} collective-permute-done((bf16[256,128]{1,0:T(8,128)(2,1)S(1)}, bf16[256,128]{1,0:T(8,128)(2,1)S(1)}, u32[]{:S(2)}, u32[]{:S(2)}) %collective-permute-start.4) | collective-permute-done | bytes 65568 | tf_op jit(solution)/shard_map/ppermute | solution.py:447
  30.3 5.6 %outer.1 = (f32[4,32,256]{2,1,0:T(8,128)S(1)}, f32[4,32,256]{2,1,0:T(8,128)S(1)}) custom-call(s32[4]{0:T(128)S(1)} %pad_add_fusion.place, f32[8,64,256]{2,1,0:T(8,128)S(1)} %copy-done, bf16[256,128]{1,0:T(8,128)(2,1)S(1)} %collective-permute-done.4.left, bf16[256,128]{1,0:T(8,128)(2,1)S(1)} %collective-permute-done.5.right, ...), custom_call_target="tpu_custom_call" | custom-call | tf_op jit(solution)/shard_map/outer/pallas_call | solution.py:469
  35.9 1.0 %collective-permute-start.7 = (f32[4,32,256]{2,1,0:T(8,128)S(1)}, f32[4,32,256]{2,1,0:T(8,128)S(1)}, u32[]{:S(2)}, u32[]{:S(2)}) collective-permute-start(f32[4,32,256]{2,1,0:T(8,128)S(1)} %get-tuple-element.62), channel_id=1, source_target_pairs={{0,32},{32,0},{64,96},{96,64},{1,33},{33,1},{65,97},{97,65},{2,34}... | collective-permute-start | bytes 393224 | tf_op jit(solution)/shard_map/ppermute | solution.py:451
  36.9 1.2 %collective-permute-start.9 = (f32[2,32,256]{2,1,0:T(8,128)S(1)}, f32[2,32,256]{2,1,0:T(8,128)S(1)}, u32[]{:S(2)}, u32[]{:S(2)}) collective-permute-start(f32[2,32,256]{2,1,0:T(8,128)S(1)} %get-tuple-element.64), channel_id=1, source_target_pairs={{0,64},{32,96},{64,0},{96,32},{1,65},{33,97},{65,1},{97,33},{2,66}... | collective-permute-start | bytes 196616 | tf_op jit(solution)/shard_map/ppermute | solution.py:456
  38.1 1.0 %collective-permute-start.8 = (f32[2,32,256]{2,1,0:T(8,128)S(1)}, f32[2,32,256]{2,1,0:T(8,128)S(1)}, u32[]{:S(2)}, u32[]{:S(2)}) collective-permute-start(f32[2,32,256]{2,1,0:T(8,128)S(1)} %slice_add_fusion), channel_id=1, source_target_pairs={{0,64},{32,96},{64,0},{96,32},{1,65},{33,97},{65,1},{97,33},{2,66}... | collective-permute-start | bytes 196616 | tf_op jit(solution)/shard_map/ppermute | solution.py:456
  39.1 1.4 %collective-permute-done.9 = f32[2,32,256]{2,1,0:T(8,128)S(1)} collective-permute-done((f32[2,32,256]{2,1,0:T(8,128)S(1)}, f32[2,32,256]{2,1,0:T(8,128)S(1)}, u32[]{:S(2)}, u32[]{:S(2)}) %collective-permute-start.9) | collective-permute-done | bytes 65568 | tf_op jit(solution)/shard_map/ppermute | solution.py:456
  40.5 0.9 %collective-permute-done.8 = f32[2,32,256]{2,1,0:T(8,128)S(1)} collective-permute-done((f32[2,32,256]{2,1,0:T(8,128)S(1)}, f32[2,32,256]{2,1,0:T(8,128)S(1)}, u32[]{:S(2)}, u32[]{:S(2)}) %collective-permute-start.8) | collective-permute-done | bytes 65568 | tf_op jit(solution)/shard_map/ppermute | solution.py:456
  41.4 0.7 %pad_maximum_fusion = f32[2,64,256]{2,1,0:T(8,128)} fusion(f32[2,16,256]{2,1,0:T(8,128)S(1)} %get-tuple-element.68, f32[2,32,256]{2,1,0:T(8,128)S(1)} %add.33, f32[2,16,256]{2,1,0:T(8,128)S(1)} %get-tuple-element.67), kind=kLoop, calls=%fused_computation | loop fusion | flops 65536 | bytes 262144 | tf_op jit(solution)/shard_map/concatenate | solution.py:556
  (14 shorter events, 0.1 us)
Async XLA Ops:
  0.0 16.5 %copy-start = (f32[8,64,256]{2,1,0:T(8,128)S(1)}, f32[8,64,256]{2,1,0:T(8,128)}, u32[]{:S(2)}) copy-start(f32[8,64,256]{2,1,0:T(8,128)} %taper.3) | copy-start | bytes 1572868
  0.0 16.4 %copy-start.1 = (f32[8]{0:T(128)S(1)}, f32[8]{0:T(128)}, u32[]{:S(2)}) copy-start(f32[8]{0:T(128)} %param.7) | copy-start | bytes 100
  2.8 20.7 %collective-permute-start = (bf16[128,1152]{1,0:T(8,128)(2,1)S(1)}, bf16[128,1152]{1,0:T(8,128)(2,1)S(1)}, u32[]{:S(2)}, u32[]{:S(2)}) collective-permute-start(bf16[128,1152]{1,0:T(8,128)(2,1)S(1)} %get-tuple-element.35), channel_id=1, source_target_pairs={{0,4},{4,0},{8,12},{12,8},{16,20},{20,16},{24,28},{28,24},{1,5},{5... | collective-permute-start | bytes 884744 | tf_op jit(solution)/shard_map/ppermute | solution.py:499
  7.3 16.3 %collective-permute-start.1 = (bf16[128,1152]{1,0:T(8,128)(2,1)S(1)}, bf16[128,1152]{1,0:T(8,128)(2,1)S(1)}, u32[]{:S(2)}, u32[]{:S(2)}) collective-permute-start(bf16[128,1152]{1,0:T(8,128)(2,1)S(1)} %get-tuple-element.36), channel_id=1, source_target_pairs={{0,28},{4,8},{8,4},{12,16},{16,12},{20,24},{24,20},{28,0},{1,29},{... | collective-permute-start | bytes 884744 | tf_op jit(solution)/shard_map/ppermute | solution.py:500
  9.9 6.5 %collective-permute-start.2 = (bf16[8,64,128]{2,1,0:T(8,128)(2,1)S(1)}, bf16[8,64,128]{2,1,0:T(8,128)(2,1)S(1)}, u32[]{:S(2)}, u32[]{:S(2)}) collective-permute-start(bf16[8,64,128]{2,1,0:T(8,128)(2,1)S(1)} %get-tuple-element.41), channel_id=1, source_target_pairs={{0,1},{1,2},{2,3},{3,0},{4,5},{5,6},{6,7},{7,4},{8,9},{9,10},{10,1... | collective-permute-start | bytes 393224 | tf_op jit(solution)/shard_map/ppermute | solution.py:447
  11.1 5.3 %collective-permute-start.3 = (bf16[8,64,128]{2,1,0:T(8,128)(2,1)S(1)}, bf16[8,64,128]{2,1,0:T(8,128)(2,1)S(1)}, u32[]{:S(2)}, u32[]{:S(2)}) collective-permute-start(bf16[8,64,128]{2,1,0:T(8,128)(2,1)S(1)} %get-tuple-element.42), channel_id=1, source_target_pairs={{0,3},{1,0},{2,1},{3,2},{4,7},{5,4},{6,5},{7,6},{8,11},{9,8},{10,9... | collective-permute-start | bytes 393224 | tf_op jit(solution)/shard_map/ppermute | solution.py:447
  23.8 5.5 %collective-permute-start.6 = (f32[4,32,256]{2,1,0:T(8,128)S(1)}, f32[4,32,256]{2,1,0:T(8,128)S(1)}, u32[]{:S(2)}, u32[]{:S(2)}) collective-permute-start(f32[4,32,256]{2,1,0:T(8,128)S(1)} %get-tuple-element.57), channel_id=1, source_target_pairs={{0,32},{32,0},{64,96},{96,64},{1,33},{33,1},{65,97},{97,65},{2,34}... | collective-permute-start | bytes 393224 | tf_op jit(solution)/shard_map/ppermute | solution.py:451
  25.4 4.9 %collective-permute-start.4 = (bf16[256,128]{1,0:T(8,128)(2,1)S(1)}, bf16[256,128]{1,0:T(8,128)(2,1)S(1)}, u32[]{:S(2)}, u32[]{:S(2)}) collective-permute-start(bf16[256,128]{1,0:T(8,128)(2,1)S(1)} %get-tuple-element.49), channel_id=1, source_target_pairs={{0,1},{1,2},{2,3},{3,0},{4,5},{5,6},{6,7},{7,4},{8,9},{9,10},{10,1... | collective-permute-start | bytes 196616 | tf_op jit(solution)/shard_map/ppermute | solution.py:447
  26.0 4.3 %collective-permute-start.5 = (bf16[256,128]{1,0:T(8,128)(2,1)S(1)}, bf16[256,128]{1,0:T(8,128)(2,1)S(1)}, u32[]{:S(2)}, u32[]{:S(2)}) collective-permute-start(bf16[256,128]{1,0:T(8,128)(2,1)S(1)} %get-tuple-element.50), channel_id=1, source_target_pairs={{0,3},{1,0},{2,1},{3,2},{4,7},{5,4},{6,5},{7,6},{8,11},{9,8},{10,9... | collective-permute-start | bytes 196616 | tf_op jit(solution)/shard_map/ppermute | solution.py:447
  35.9 2.2 %collective-permute-start.7 = (f32[4,32,256]{2,1,0:T(8,128)S(1)}, f32[4,32,256]{2,1,0:T(8,128)S(1)}, u32[]{:S(2)}, u32[]{:S(2)}) collective-permute-start(f32[4,32,256]{2,1,0:T(8,128)S(1)} %get-tuple-element.62), channel_id=1, source_target_pairs={{0,32},{32,0},{64,96},{96,64},{1,33},{33,1},{65,97},{97,65},{2,34}... | collective-permute-start | bytes 393224 | tf_op jit(solution)/shard_map/ppermute | solution.py:451
  36.9 3.6 %collective-permute-start.9 = (f32[2,32,256]{2,1,0:T(8,128)S(1)}, f32[2,32,256]{2,1,0:T(8,128)S(1)}, u32[]{:S(2)}, u32[]{:S(2)}) collective-permute-start(f32[2,32,256]{2,1,0:T(8,128)S(1)} %get-tuple-element.64), channel_id=1, source_target_pairs={{0,64},{32,96},{64,0},{96,32},{1,65},{33,97},{65,1},{97,33},{2,66}... | collective-permute-start | bytes 196616 | tf_op jit(solution)/shard_map/ppermute | solution.py:456
  38.1 3.3 %collective-permute-start.8 = (f32[2,32,256]{2,1,0:T(8,128)S(1)}, f32[2,32,256]{2,1,0:T(8,128)S(1)}, u32[]{:S(2)}, u32[]{:S(2)}) collective-permute-start(f32[2,32,256]{2,1,0:T(8,128)S(1)} %slice_add_fusion), channel_id=1, source_target_pairs={{0,64},{32,96},{64,0},{96,32},{1,65},{33,97},{65,1},{97,33},{2,66}... | collective-permute-start | bytes 196616 | tf_op jit(solution)/shard_map/ppermute | solution.py:456

commit v4 on v3

--- a/solution.py
+++ b/solution.py
@@ -9,6 +9,7 @@
 HALO = 2 * PASSES
 LANES = 128
 NEAR = 4
+INNER_FLOPS = 4 * 10**9
 BF16 = jnp.bfloat16
 F32 = jnp.float32
 
@@ -67,7 +68,43 @@
     return jnp.swapaxes(value.astype(F32), 0, 1)
 
 
-def start_kernel(place, p_hbm, increment_hbm, taper_hbm, to_near, to_far, to_left, to_right, p, g, taper, increment, sems):
+def write_strip(out, p, g, pick, order, packs=()):
+    members, levels, _, cols = p.shape
+    main = members * cols
+
+    def put(pair, lanes, field, first=0):
+        rows = slice(first + 2 * pair * levels, first + 2 * (pair + 1) * levels)
+        both = jnp.concatenate([field[order[2 * pair]], field[order[2 * pair + 1]]], axis=0)
+        out[rows, lanes] = both.astype(BF16)
+
+    for half in range(2):
+        lanes = slice(half * LANES, (half + 1) * LANES)
+        weight = facing(g[:, pick, lanes])
+        hi = weight.astype(BF16).astype(F32)
+        for k, part in enumerate((hi, weight - hi)):
+            for pair in range(NEAR // 2):
+                put(pair, slice(main, main + LANES), part, (2 * k + half) * NEAR * levels)
+        for m in range(members):
+            to = slice(m * cols + half * LANES, m * cols + (half + 1) * LANES)
+            field = facing(p[m, :, pick, lanes])
+            product = field * weight
+            for pair in range(HALO // 2):
+                put(pair, to, field if 2 * pair < NEAR else product)
+    for k, side in enumerate(packs):
+        field = facing(side[:, pick, :])
+        lane = lane_of(field.shape)
+        weight = field + roll(field, -HALO)
+        total = jnp.zeros_like(field)
+        for m in range(members):
+            inside = (lane >= HALO * m) & (lane < HALO * (m + 1))
+            total = jnp.where(inside, roll(weight, HALO * (m - members)), total)
+        product = field * total
+        to = slice(main + (k + 1) * LANES, main + (k + 2) * LANES)
+        for pair in range(HALO // 2):
+            put(pair, to, field if 2 * pair < NEAR else product)
+
+
+def start_kernel(place, p_hbm, increment_hbm, taper_hbm, to_near, to_left, to_right, p, g, taper, increment, sems):
     members, levels, rows, cols = p.shape
     copies = []
     for i in (0, rows // HALO - 1, *range(1, rows // HALO - 1)):
@@ -81,25 +118,6 @@
         for copy in group:
             copy.start()
 
-    def strip(out, pick, order):
-        def put(pair, lanes, field, first=0):
-            rows_at = slice(first + 2 * pair * levels, first + 2 * (pair + 1) * levels)
-            both = jnp.concatenate([field[order[2 * pair]], field[order[2 * pair + 1]]], axis=0)
-            out[rows_at, lanes] = both.astype(BF16)
-
-        for half in range(2):
-            lanes = slice(half * LANES, (half + 1) * LANES)
-            weight = facing(g[:, pick, lanes])
-            hi = weight.astype(BF16).astype(F32)
-            for k, part in enumerate((hi, weight - hi)):
-                for pair in range(NEAR // 2):
-                    put(pair, slice(members * cols, members * cols + LANES), part, (2 * k + half) * NEAR * levels)
-            for m in range(members):
-                to = slice(m * cols + half * LANES, m * cols + (half + 1) * LANES)
-                field = facing(p[m, :, pick, lanes])
-                for pair in range(HALO // 2):
-                    put(pair, to, field if 2 * pair < NEAR else field * weight)
-
     def packed(pick, column, shift):
         fields = [p[m, :, pick, column].astype(F32) for m in range(members)]
         hi, lo = split(g[:, pick, column])
@@ -120,40 +138,44 @@
 
             @pl.when(place[1] == k)
             def _():
-                strip(to_near, pick, order)
-
-            @pl.when(place[1] != k)
-            def _():
-                strip(to_far, pick, order)
+                write_strip(to_near, p, g, pick, order)
         to_left[:, pick, :] = packed(pick, slice(0, LANES), 0)
         to_right[:, pick, :] = packed(pick, slice(cols - LANES, cols), HALO)
 
 
-def corners_kernel(top, bottom, to_left, to_right):
-    count = top.shape[0]
-    pairs = count // 16
-    for edge, strip in enumerate((top, bottom)):
-        main = strip.shape[1] - LANES
-        members = main // (2 * LANES)
-        for pair in range(pairs):
-            rows = slice(16 * pair, 16 * (pair + 1))
-            out = slice(edge * count + 16 * pair, edge * count + 16 * (pair + 1))
-            fields = [
-                [strip[rows, (2 * m + half) * LANES : (2 * m + half + 1) * LANES].astype(F32) for m in range(members)]
-                for half in range(2)
-            ]
-            if 2 * pair < NEAR:
-                for half in range(2):
-                    for k in range(2):
-                        first = (2 * k + half) * (count // 4) + 16 * pair
-                        fields[half].append(strip[first : first + 16, main:].astype(F32))
-            lane = lane_of((16, LANES))
-            for ref, half, shift in ((to_left, 0, 0), (to_right, 1, HALO)):
-                total = jnp.zeros((16, LANES), F32)
-                for e, field in enumerate(fields[half]):
-                    inside = (lane >= HALO * e) & (lane < HALO * (e + 1))
-                    total = jnp.where(inside, roll(field, shift + HALO * e), total)
-                ref[out, :] = total.astype(BF16)
+def far_kernel(place, p, g, left, right, to_far):
+    rows = p.shape[2]
+    for k in range(2):
+        pick = slice(k * (rows - HALO), k * (rows - HALO) + HALO)
+        order = range(HALO) if k == 0 else range(HALO - 1, -1, -1)
+
+        @pl.when(place[1] != k)
+        def _():
+            write_strip(to_far, p, g, pick, order, (left, right))
+
+
+def corners_kernel(strip, to_left, to_right):
+    count = strip.shape[0]
+    main = strip.shape[1] - LANES
+    members = main // (2 * LANES)
+    for pair in range(count // 16):
+        rows = slice(16 * pair, 16 * (pair + 1))
+        fields = [
+            [strip[rows, (2 * m + half) * LANES : (2 * m + half + 1) * LANES].astype(F32) for m in range(members)]
+            for half in range(2)
+        ]
+        if 2 * pair < NEAR:
+            for half in range(2):
+                for k in range(2):
+                    first = (2 * k + half) * (count // 4) + 16 * pair
+                    fields[half].append(strip[first : first + 16, main:].astype(F32))
+        lane = lane_of((16, LANES))
+        for ref, half, shift in ((to_left, 0, 0), (to_right, 1, HALO)):
+            total = jnp.zeros((16, LANES), F32)
+            for e, field in enumerate(fields[half]):
+                inside = (lane >= HALO * e) & (lane < HALO * (e + 1))
+                total = jnp.where(inside, roll(field, shift + HALO * e), total)
+            ref[rows, :] = total.astype(BF16)
 
 
 def turned(value):
@@ -335,56 +357,51 @@
     lax.fori_loop(0, (rows - 2 * HALO) // HALO, last, 0)
 
 
-def lift_kernel(top, bottom, to_fields, to_weights, main_values, main_weights):
-    fine, levels = main_values.shape[2:4]
-    count = top.shape[0]
-    main = top.shape[1] - LANES
-    for first in range(0, fine, 2):
-        width = min(2, fine - first)
-        lanes = slice(first * LANES, (first + width) * LANES)
-        for edge, strip in enumerate((top, bottom)):
-            field = dot(strip[:, :main], to_fields[:main, lanes])
-            part = count // 4
-            near = jnp.concatenate([strip[k * part : (k + 1) * part, main:] for k in range(4)], axis=1)
-            weight = dot(near, to_weights[: 4 * LANES, lanes])
-            for k in range(width):
-                pick = slice(k * LANES, (k + 1) * LANES)
-                main_values[edge, :, first + k] = field[:, pick].reshape(HALO, levels, LANES)
-                main_weights[edge, :, first + k] = weight[:, pick].reshape(NEAR, levels, LANES)
-
-
 def outer_kernel(
-    place, taper, left, right, main_values, main_weights, edges, edge_values,
+    place, taper, near, far, left, right, edges, edge_values, keep_inner, send_inner,
     to_fields, to_weights, back, kappa,
     keep, send,
     x,
 ):
     levels, rows, cols = taper.shape
+    keep[:, HALO : rows - HALO, :] = keep_inner[...]
+    send[:, HALO : rows - HALO, :] = send_inner[...]
     fine = edge_values.shape[2]
     members = LANES * fine // (cols + 2 * HALO)
     linear, constant, scale = factors(kappa[...], 4 * members)
     inside = jnp.where(place[0] == 1, 0.0, 1.0).astype(F32)
-    packs = jnp.concatenate([left[...], right[...]], axis=1)
-    size = HALO * levels
-    near_packs = jnp.concatenate([packs[edge * size : edge * size + NEAR * levels] for edge in range(2)], axis=0)
+    main = members * cols
+    part = NEAR * levels
+    sides = [jnp.concatenate([left[...], right[...]], axis=1), far[:, main + LANES :]]
+    fields = jnp.concatenate(
+        [jnp.concatenate([strip[:, :main], side], axis=1) for strip, side in zip((near, far), sides)], axis=0
+    )
+    weights = jnp.concatenate(
+        [
+            jnp.concatenate(
+                [strip[k * part : (k + 1) * part, main : main + LANES] for k in range(4)] + [side[:part]], axis=1
+            )
+            for strip, side in zip((near, far), sides)
+        ],
+        axis=0,
+    )
     for first in range(0, fine, 2):
         width = min(2, fine - first)
         lanes = slice(first * LANES, (first + width) * LANES)
-        field = dot(packs, to_fields[members * cols :, lanes])
-        weight = dot(near_packs, to_weights[2 * cols :, lanes])
+        field = dot(fields, to_fields[:, lanes])
+        weight = dot(weights, to_weights[:, lanes])
         for k in range(width):
             pick = slice(k * LANES, (k + 1) * LANES)
-            part = field[:, pick].reshape(2, HALO, levels, LANES)
-            near = weight[:, pick].reshape(2, NEAR, levels, LANES)
+            value_of = field[:, pick].reshape(2, HALO, levels, LANES)
+            weight_of = weight[:, pick].reshape(2, NEAR, levels, LANES)
             for edge in range(2):
                 for distance in range(HALO):
-                    value = main_values[edge, distance, first + k] + part[edge, distance]
+                    value = value_of[edge, distance]
                     if distance < NEAR:
-                        value = value * (main_weights[edge, distance, first + k] + near[edge, distance])
+                        value = value * weight_of[edge, distance]
                     if edge == 1 and distance == 0:
                         value = value * inside
                     x[edge, HALO - 1 - distance, 2 + first + k] = value
-
 
     def wrap(edge, row):
         def target(c, value):
@@ -432,11 +449,10 @@
             axis=1,
         )
         own = slice(edge * (rows - HALO), edge * (rows - HALO) + HALO)
-        pick = slice(edge * HALO, (edge + 1) * HALO)
         finish(
             product, back[...], scale,
             lambda lanes: taper[:, own, lanes],
-            lambda natural, lanes: to_owner(place, natural, keep, send, pick, lanes, levels),
+            lambda natural, lanes: to_owner(place, natural, keep, send, own, lanes, levels),
             levels,
         )
 
@@ -465,7 +481,7 @@
     smem = pl.BlockSpec(memory_space=pltpu.SMEM)
     hbm = pl.BlockSpec(memory_space=pltpu.HBM)
 
-    def call(kernel, name, outs, ins, scratch=(), specs=None):
+    def call(kernel, name, outs, ins, scratch=(), specs=None, cost=None):
         return pl.pallas_call(
             kernel,
             out_shape=tuple(outs),
@@ -473,10 +489,13 @@
             out_specs=(vmem,) * len(outs),
             scratch_shapes=list(scratch),
             compiler_params=pltpu.CompilerParams(vmem_limit_bytes=20 * 1024 * 1024),
+            cost_estimate=cost,
             name=name,
         )(*ins)
 
-    strip = shape((HALO * levels, members * cols + LANES), BF16)
+    def strip(blocks):
+        return shape((HALO * levels, members * cols + blocks * LANES), BF16)
+
     pack = shape((levels, rows, LANES), BF16)
     whole = shape((levels, rows, cols), F32)
     kappa = jnp.broadcast_to(kappa[:, None], tile)
@@ -489,15 +508,14 @@
         mem // 2,
     ])
 
-    to_near, to_far, to_left, to_right, p, g = call(
+    to_near, to_left, to_right, p, g = call(
         start_kernel, "start",
-        (strip, strip, pack, pack, shape(perturbations.shape, BF16), whole),
+        (strip(1), pack, pack, shape(perturbations.shape, BF16), whole),
         (place, *(pltpu.with_memory_space_constraint(a, pltpu.HBM) for a in (perturbations, increment, taper_norm))),
         (pltpu.VMEM(whole.shape, F32), pltpu.VMEM(whole.shape, F32), pltpu.SemaphoreType.DMA((rows // HALO, 3))),
         specs=[smem] + [hbm] * 3,
     )
     near = lax.ppermute(to_near, "lat", [(i, i ^ 1) for i in range(count)])
-    far = lax.ppermute(to_far, "lat", [(i, (i + 1 - 2 * (1 - i % 2)) % count) for i in range(count)])
     left = shifted(to_right, "lon", 1, True)
     right = shifted(to_left, "lon", -1, True)
 
@@ -514,6 +532,16 @@
         (pltpu.VMEM((rows * levels, members * cols), BF16), pltpu.VMEM((rows * levels, 2 * cols), BF16)),
     )
 
+    p, g, own_values = lax.optimization_barrier((p, g, own_values))
+    (to_far,) = call(far_kernel, "far", (strip(3),), (place, p, g, left, right), specs=[smem] + [vmem] * 4)
+    far = lax.ppermute(to_far, "lat", [(i, (i + 1 - 2 * (1 - i % 2)) % count) for i in range(count)])
+    near, to_far = lax.optimization_barrier((near, to_far))
+    side = shape((HALO * levels, LANES), BF16)
+    to_left, to_right = call(corners_kernel, "corners", (side, side), (near,))
+    near_left = shifted(to_right, "lon", 1, True)
+    near_right = shifted(to_left, "lon", -1, True)
+    own_values, to_left = lax.optimization_barrier((own_values, to_left))
+
     part = shape((levels // 2, rows - 2 * HALO, cols), F32)
     keep, send, edges, edge_values = call(
         inner_kernel, "inner",
@@ -525,35 +553,20 @@
             pltpu.VMEM((rows * levels, 2 * LANES), BF16),
         ),
         specs=[smem] + [vmem] * 9,
-    )
-    near, far, edges = lax.optimization_barrier((near, far, edges))
-
-    side = shape((2 * HALO * levels, LANES), BF16)
-    to_left, to_right = call(corners_kernel, "corners", (side, side), (near, far))
-    left = shifted(to_right, "lon", 1, True)
-    right = shifted(to_left, "lon", -1, True)
-    near, far, send, to_left, _ = lax.optimization_barrier((near, far, send, to_left, to_right))
-    here, there = over_core(keep, send)
-    main_values, main_weights = call(
-        lift_kernel, "lift",
-        (shape((2, HALO, fine, *tile), F32), shape((2, NEAR, fine, *tile), F32)),
-        (near, far, to_fields, to_weights),
-    )
-    here, there, edges = lax.optimization_barrier((here, there, edges))
-    middle = over_plane(here, there)
-    part = shape((levels // 2, 2 * HALO, cols), F32)
+        cost=pl.CostEstimate(flops=INNER_FLOPS, bytes_accessed=1 << 20, transcendentals=0),
+    )
+    part = shape((levels // 2, rows, cols), F32)
     keep, send = call(
         outer_kernel, "outer",
         (part, part),
         (
-            place, taper_norm, left, right, main_values, main_weights, edges, edge_values,
+            place, taper_norm, near, far, near_left, near_right, edges, edge_values, keep, send,
             to_fields, to_weights, back, kappa,
         ),
         (pltpu.VMEM((2, 2 * HALO, fine + 4, *tile), F32),),
-        specs=[smem] + [vmem] * 11,
-    )
-    outside = over_plane(*over_core(keep, send))
-    return jnp.concatenate([outside[:, :HALO], middle, outside[:, HALO:]], axis=1)
+        specs=[smem] + [vmem] * 13,
+    )
+    return over_plane(*over_core(keep, send))
 
 
 def solution(mesh):

time: 42.4 us -> 42.3 us (level)
  waiting for transfers between devices: 3.26 us -> 5.84 us
  starting transfers between devices: 17.2 us -> 14.7 us
    ppermute x2 -> x1, waiting for transfers between devices: 2.25 us -> 3.97 us  [over_plane(): return here + lax.ppermute(there, 'mem', [(i, i ^ 2) for i in range(4)])]
    ppermute x2 -> x1, starting transfers between devices: 2.26 us -> 0.82 us  [over_plane(): return here + lax.ppermute(there, 'mem', [(i, i ^ 2) for i in range(4)])]
    ppermute x2 -> x1, waiting for transfers between devices: 0.01 us -> 1.16 us  [over_core(): got = lax.ppermute(send, 'mem', [(i, i ^ 1) for i in range(4)])]
    ppermute x4, starting transfers between devices: 5.37 us -> 4.21 us  [shifted(): return lax.ppermute(value, axis, pairs)]
    ppermute x4, waiting for transfers between devices: 1 us -> 0.01 us  [shifted(): return lax.ppermute(value, axis, pairs)]
    ppermute x1, waiting for transfers between devices: 0.01 us -> 0.69 us  [local(): lax.ppermute(to_far, 'lat', [(i, (i + 1 - 2 * (1 - i % 2)) % count) for i...]
    concatenate x1 -> x0, other arithmetic: 0.67 us -> none  [local(): jnp.concatenate([outside[:, :HALO], middle, outside[:, HALO:]], axis=1)]
    add x2 -> x1, other arithmetic: 0.02 us -> 0.68 us  [over_plane(): return here + lax.ppermute(there, 'mem', [(i, i ^ 2) for i in range(4)])]
  transfers between devices with their start and end apart: 10 -> 8, of which waited for: 3 -> 3; matrix products, arithmetic and copies ran while one was open for 0% -> 0% of each run, Pallas kernels for 29% -> 28%
where the time goes in v4:
time: 42.3 us; the launch traced here: 42.1 us
  Pallas kernels  20.6 us (49%)
  starting transfers between devices  14.7 us (35%)
  waiting for transfers between devices  5.84 us (14%)
  other arithmetic  0.78 us (2%)
    pallas_call x6, Pallas kernels, call(): pl.pallas_call(kernel, out_shape=tuple(outs), in_specs=specs or [vmem] *...  20.6 us
    ppermute x1, starting transfers between devices, local(): near = lax.ppermute(to_near, 'lat', [(i, i ^ 1) for i in range(count)])  4.5 us
    ppermute x4, starting transfers between devices, shifted(): return lax.ppermute(value, axis, pairs)  4.21 us
    ppermute x1, waiting for transfers between devices, over_plane(): return here + lax.ppermute(there, 'mem', [(i, i ^ 2) for i in range(4)])  3.97 us
    ppermute x1, starting transfers between devices, local(): lax.ppermute(to_far, 'lat', [(i, (i + 1 - 2 * (1 - i % 2)) % count) for i...  2.61 us
    ppermute x1, starting transfers between devices, over_core(): got = lax.ppermute(send, 'mem', [(i, i ^ 1) for i in range(4)])  2.54 us
    ppermute x1, waiting for transfers between devices, over_core(): got = lax.ppermute(send, 'mem', [(i, i ^ 1) for i in range(4)])  1.16 us
  transfers between devices with their start and end apart: 8, of which 3 were waited for; matrix products, arithmetic and copies ran while one was open for 0% of the time, Pallas kernels for 28%

profile of v4, /device:TPU:1, one launch (start us, length us, event | category | flops | bytes accessed | tf_op | source)
XLA Modules:
  0.0 42.1 jit_solution(4195113721691107743)
XLA Ops:
  0.0 0.1 pad_add_fusion.place
  0.1 2.6 %start.1 = (bf16[128,1152]{1,0:T(8,128)(2,1)S(1)}, bf16[8,64,128]{2,1,0:T(8,128)(2,1)S(1)}, bf16[8,64,128]{2,1,0:T(8,128)(2,1)S(1)}, bf16[4,8,64,256]{3,2,1,0:T(8,128)(2,1)S(1)}, f32[8,64,256]{2,1,0:T(8,128)S(1)}) custom-call(s32[4]{0:T(128)S(1)} %pad_add_fusion.place, bf16[4,8,64,256]{3,2,1,0:T(8,128)(2,1)} %p_hbm.1, f32[8,64,256]{2,1,0:T(8,128)} %increment_hbm.1, ...), custom_call_target="tpu_custom_call" | custom-call | tf_op jit(solution)/shard_map/start/pallas_call | solution.py:485
  2.6 0.0 copy-start.1
  2.7 0.0 copy-start
  2.7 4.5 %collective-permute-start = (bf16[128,1152]{1,0:T(8,128)(2,1)S(1)}, bf16[128,1152]{1,0:T(8,128)(2,1)S(1)}, u32[]{:S(2)}, u32[]{:S(2)}) collective-permute-start(bf16[128,1152]{1,0:T(8,128)(2,1)S(1)} %get-tuple-element.28), channel_id=1, source_target_pairs={{0,4},{4,0},{8,12},{12,8},{16,20},{20,16},{24,28},{28,24},{1,5},{5... | collective-permute-start | bytes 884744 | tf_op jit(solution)/shard_map/ppermute | solution.py:518
  7.2 1.2 %collective-permute-start.1 = (bf16[8,64,128]{2,1,0:T(8,128)(2,1)S(1)}, bf16[8,64,128]{2,1,0:T(8,128)(2,1)S(1)}, u32[]{:S(2)}, u32[]{:S(2)}) collective-permute-start(bf16[8,64,128]{2,1,0:T(8,128)(2,1)S(1)} %get-tuple-element.34), channel_id=1, source_target_pairs={{0,1},{1,2},{2,3},{3,0},{4,5},{5,6},{6,7},{7,4},{8,9},{9,10},{10,1... | collective-permute-start | bytes 393224 | tf_op jit(solution)/shard_map/ppermute | solution.py:463
  8.4 1.5 %collective-permute-start.2 = (bf16[8,64,128]{2,1,0:T(8,128)(2,1)S(1)}, bf16[8,64,128]{2,1,0:T(8,128)(2,1)S(1)}, u32[]{:S(2)}, u32[]{:S(2)}) collective-permute-start(bf16[8,64,128]{2,1,0:T(8,128)(2,1)S(1)} %get-tuple-element.35), channel_id=1, source_target_pairs={{0,3},{1,0},{2,1},{3,2},{4,7},{5,4},{6,5},{7,6},{8,11},{9,8},{10,9... | collective-permute-start | bytes 393224 | tf_op jit(solution)/shard_map/ppermute | solution.py:463
  9.9 3.8 %prepare.1 = (f32[64,9,8,128]{3,2,1,0:T(8,128)S(1)}, f32[64,9,8,128]{3,2,1,0:T(8,128)S(1)}, bf16[1280,1152]{1,0:T(8,128)(2,1)S(1)}, bf16[768,1152]{1,0:T(8,128)(2,1)S(1)}, bf16[1152,256]{1,0:T(8,128)(2,1)S(1)}) custom-call(bf16[4,8,64,256]{3,2,1,0:T(8,128)(2,1)S(1)} %get-tuple-element.32.p, f32[8,64,256]{2,1,0:T(8,128)S(1)} %get-tuple-element.33.g), custom_call_target="tpu_custom_call" | custom-call | tf_op jit(solution)/shard_map/prepare/pallas_call | solution.py:485
  13.7 0.0 collective-permute-done.2.right
  13.7 0.9 %far.1 = bf16[128,1408]{1,0:T(8,128)(2,1)S(1)} custom-call(s32[4]{0:T(128)S(1)} %pad_add_fusion.place, bf16[4,8,64,256]{3,2,1,0:T(8,128)(2,1)S(1)} %get-tuple-element.32.p, f32[8,64,256]{2,1,0:T(8,128)S(1)} %get-tuple-element.33.g, bf16[8,64,128]{2,1,0:T(8,128)(2,1)S(1)} %collective-permute-done.1.left, bf16[8,64,128]{2,1,0:T(8,128)(2,1)S(1)} %collective-permute-done.2.right), custom_call_target="tpu_custom_call" | custom-call | tf_op jit(solution)/shard_map/far/pallas_call | solution.py:485
  14.6 2.6 %collective-permute-start.3 = (bf16[128,1408]{1,0:T(8,128)(2,1)S(1)}, bf16[128,1408]{1,0:T(8,128)(2,1)S(1)}, u32[]{:S(2)}, u32[]{:S(2)}) collective-permute-start(bf16[128,1408]{1,0:T(8,128)(2,1)S(1)} %far.1), channel_id=1, source_target_pairs={{0,28},{4,8},{8,4},{12,16},{16,12},{20,24},{24,20},{28,0},{1,29},{... | collective-permute-start | bytes 1081352 | tf_op jit(solution)/shard_map/ppermute | solution.py:537
  17.2 0.1 corners.1
  17.4 1.4 %collective-permute-start.5 = (bf16[128,128]{1,0:T(8,128)(2,1)S(1)}, bf16[128,128]{1,0:T(8,128)(2,1)S(1)}, u32[]{:S(2)}, u32[]{:S(2)}) collective-permute-start(bf16[128,128]{1,0:T(8,128)(2,1)S(1)} %get-tuple-element.38), channel_id=1, source_target_pairs={{0,3},{1,0},{2,1},{3,2},{4,7},{5,4},{6,5},{7,6},{8,11},{9,8},{10,9... | collective-permute-start | bytes 98312 | tf_op jit(solution)/shard_map/ppermute | solution.py:463
  18.8 0.1 collective-permute-start.4
  18.9 0.1 broadcast_in_dim.2.kappa
  19.0 7.0 %inner.1 = (f32[4,32,256]{2,1,0:T(8,128)S(1)}, f32[4,32,256]{2,1,0:T(8,128)S(1)}, f32[2,8,4,13,8,128]{5,4,3,2,1,0:T(8,128)S(1)}, f32[2,16,9,8,128]{4,3,2,1,0:T(8,128)S(1)}) custom-call(s32[4]{0:T(128)S(1)} %pad_add_fusion.place, f32[64,9,8,128]{3,2,1,0:T(8,128)S(1)} %get-tuple-element.40.own_values, f32[64,9,8,128]{3,2,1,0:T(8,128)S(1)} %get-tuple-element.41.own_weights, ...), custom_call_target="tpu_custom_call" | custom-call | flops 4000000000 | bytes 1048576 | tf_op jit(solution)/shard_map/inner/pallas_call | solution.py:485
  26.0 0.0 collective-permute-done.4.left
  26.0 0.7 %collective-permute-done.3.far = bf16[128,1408]{1,0:T(8,128)(2,1)S(1)} collective-permute-done((bf16[128,1408]{1,0:T(8,128)(2,1)S(1)}, bf16[128,1408]{1,0:T(8,128)(2,1)S(1)}, u32[]{:S(2)}, u32[]{:S(2)}) %collective-permute-start.3) | collective-permute-done | bytes 360480 | tf_op jit(solution)/shard_map/ppermute | solution.py:537
  26.7 6.2 %outer.1 = (f32[4,64,256]{2,1,0:T(8,128)S(1)}, f32[4,64,256]{2,1,0:T(8,128)S(1)}) custom-call(s32[4]{0:T(128)S(1)} %pad_add_fusion.place, f32[8,64,256]{2,1,0:T(8,128)S(1)} %copy-done, bf16[128,1152]{1,0:T(8,128)(2,1)S(1)} %collective-permute-done.strip.near, bf16[128,1408]{1,0:T(8,128)(2,1)S(1)} %collective-permute-done.3.far, ...), custom_call_target="tpu_custom_call" | custom-call | tf_op jit(solution)/shard_map/outer/pallas_call | solution.py:485
  32.9 2.5 %collective-permute-start.6 = (f32[4,64,256]{2,1,0:T(8,128)S(1)}, f32[4,64,256]{2,1,0:T(8,128)S(1)}, u32[]{:S(2)}, u32[]{:S(2)}) collective-permute-start(f32[4,64,256]{2,1,0:T(8,128)S(1)} %get-tuple-element.50), channel_id=1, source_target_pairs={{0,32},{32,0},{64,96},{96,64},{1,33},{33,1},{65,97},{97,65},{2,34}... | collective-permute-start | bytes 786440 | tf_op jit(solution)/shard_map/ppermute | solution.py:467
  35.5 1.2 %collective-permute-done.6 = f32[4,64,256]{2,1,0:T(8,128)S(1)} collective-permute-done((f32[4,64,256]{2,1,0:T(8,128)S(1)}, f32[4,64,256]{2,1,0:T(8,128)S(1)}, u32[]{:S(2)}, u32[]{:S(2)}) %collective-permute-start.6) | collective-permute-done | bytes 262176 | tf_op jit(solution)/shard_map/ppermute | solution.py:467
  36.7 0.8 %collective-permute-start.7 = (f32[2,64,256]{2,1,0:T(8,128)S(1)}, f32[2,64,256]{2,1,0:T(8,128)S(1)}, u32[]{:S(2)}, u32[]{:S(2)}) collective-permute-start(f32[2,64,256]{2,1,0:T(8,128)S(1)} %slice_add_fusion), channel_id=1, source_target_pairs={{0,64},{32,96},{64,0},{96,32},{1,65},{33,97},{65,1},{97,33},{2,66}... | collective-permute-start | bytes 393224 | tf_op jit(solution)/shard_map/ppermute | solution.py:472
  37.5 4.0 %collective-permute-done.7 = f32[2,64,256]{2,1,0:T(8,128)S(1)} collective-permute-done((f32[2,64,256]{2,1,0:T(8,128)S(1)}, f32[2,64,256]{2,1,0:T(8,128)S(1)}, u32[]{:S(2)}, u32[]{:S(2)}) %collective-permute-start.7) | collective-permute-done | bytes 131104 | tf_op jit(solution)/shard_map/ppermute | solution.py:472
  41.4 0.7 %fusion = f32[2,64,256]{2,1,0:T(8,128)} fusion(f32[2,64,256]{2,1,0:T(8,128)S(1)} %collective-permute-done.7, f32[4,64,256]{2,1,0:T(8,128)S(1)} %collective-permute-done.6, f32[4,64,256]{2,1,0:T(8,128)S(1)} %get-tuple-element.49), kind=kLoop, calls=%fused_computation.2 | loop fusion | flops 65536 | bytes 524288 | tf_op jit(solution)/shard_map/add | solution.py:472
  (6 shorter events, 0.0 us)
Async XLA Ops:
  2.6 16.3 %copy-start.1 = (f32[8]{0:T(128)S(1)}, f32[8]{0:T(128)}, u32[]{:S(2)}) copy-start(f32[8]{0:T(128)} %param.7) | copy-start | bytes 100
  2.7 16.3 %copy-start = (f32[8,64,256]{2,1,0:T(8,128)S(1)}, f32[8,64,256]{2,1,0:T(8,128)}, u32[]{:S(2)}) copy-start(f32[8,64,256]{2,1,0:T(8,128)} %taper.3) | copy-start | bytes 1572868
  2.7 14.6 %collective-permute-start = (bf16[128,1152]{1,0:T(8,128)(2,1)S(1)}, bf16[128,1152]{1,0:T(8,128)(2,1)S(1)}, u32[]{:S(2)}, u32[]{:S(2)}) collective-permute-start(bf16[128,1152]{1,0:T(8,128)(2,1)S(1)} %get-tuple-element.28), channel_id=1, source_target_pairs={{0,4},{4,0},{8,12},{12,8},{16,20},{20,16},{24,28},{28,24},{1,5},{5... | collective-permute-start | bytes 884744 | tf_op jit(solution)/shard_map/ppermute | solution.py:518
  7.2 6.5 %collective-permute-start.1 = (bf16[8,64,128]{2,1,0:T(8,128)(2,1)S(1)}, bf16[8,64,128]{2,1,0:T(8,128)(2,1)S(1)}, u32[]{:S(2)}, u32[]{:S(2)}) collective-permute-start(bf16[8,64,128]{2,1,0:T(8,128)(2,1)S(1)} %get-tuple-element.34), channel_id=1, source_target_pairs={{0,1},{1,2},{2,3},{3,0},{4,5},{5,6},{6,7},{7,4},{8,9},{9,10},{10,1... | collective-permute-start | bytes 393224 | tf_op jit(solution)/shard_map/ppermute | solution.py:463
  8.4 5.3 %collective-permute-start.2 = (bf16[8,64,128]{2,1,0:T(8,128)(2,1)S(1)}, bf16[8,64,128]{2,1,0:T(8,128)(2,1)S(1)}, u32[]{:S(2)}, u32[]{:S(2)}) collective-permute-start(bf16[8,64,128]{2,1,0:T(8,128)(2,1)S(1)} %get-tuple-element.35), channel_id=1, source_target_pairs={{0,3},{1,0},{2,1},{3,2},{4,7},{5,4},{6,5},{7,6},{8,11},{9,8},{10,9... | collective-permute-start | bytes 393224 | tf_op jit(solution)/shard_map/ppermute | solution.py:463
  14.6 12.1 %collective-permute-start.3 = (bf16[128,1408]{1,0:T(8,128)(2,1)S(1)}, bf16[128,1408]{1,0:T(8,128)(2,1)S(1)}, u32[]{:S(2)}, u32[]{:S(2)}) collective-permute-start(bf16[128,1408]{1,0:T(8,128)(2,1)S(1)} %far.1), channel_id=1, source_target_pairs={{0,28},{4,8},{8,4},{12,16},{16,12},{20,24},{24,20},{28,0},{1,29},{... | collective-permute-start | bytes 1081352 | tf_op jit(solution)/shard_map/ppermute | solution.py:537
  17.4 8.6 %collective-permute-start.5 = (bf16[128,128]{1,0:T(8,128)(2,1)S(1)}, bf16[128,128]{1,0:T(8,128)(2,1)S(1)}, u32[]{:S(2)}, u32[]{:S(2)}) collective-permute-start(bf16[128,128]{1,0:T(8,128)(2,1)S(1)} %get-tuple-element.38), channel_id=1, source_target_pairs={{0,3},{1,0},{2,1},{3,2},{4,7},{5,4},{6,5},{7,6},{8,11},{9,8},{10,9... | collective-permute-start | bytes 98312 | tf_op jit(solution)/shard_map/ppermute | solution.py:463
  18.8 7.2 %collective-permute-start.4 = (bf16[128,128]{1,0:T(8,128)(2,1)S(1)}, bf16[128,128]{1,0:T(8,128)(2,1)S(1)}, u32[]{:S(2)}, u32[]{:S(2)}) collective-permute-start(bf16[128,128]{1,0:T(8,128)(2,1)S(1)} %get-tuple-element.37), channel_id=1, source_target_pairs={{0,1},{1,2},{2,3},{3,0},{4,5},{5,6},{6,7},{7,4},{8,9},{9,10},{10,1... | collective-permute-start | bytes 98312 | tf_op jit(solution)/shard_map/ppermute | solution.py:463
  32.9 3.7 %collective-permute-start.6 = (f32[4,64,256]{2,1,0:T(8,128)S(1)}, f32[4,64,256]{2,1,0:T(8,128)S(1)}, u32[]{:S(2)}, u32[]{:S(2)}) collective-permute-start(f32[4,64,256]{2,1,0:T(8,128)S(1)} %get-tuple-element.50), channel_id=1, source_target_pairs={{0,32},{32,0},{64,96},{96,64},{1,33},{33,1},{65,97},{97,65},{2,34}... | collective-permute-start | bytes 786440 | tf_op jit(solution)/shard_map/ppermute | solution.py:467
  36.7 4.8 %collective-permute-start.7 = (f32[2,64,256]{2,1,0:T(8,128)S(1)}, f32[2,64,256]{2,1,0:T(8,128)S(1)}, u32[]{:S(2)}, u32[]{:S(2)}) collective-permute-start(f32[2,64,256]{2,1,0:T(8,128)S(1)} %slice_add_fusion), channel_id=1, source_target_pairs={{0,64},{32,96},{64,0},{96,32},{1,65},{33,97},{65,1},{97,33},{2,66}... | collective-permute-start | bytes 393224 | tf_op jit(solution)/shard_map/ppermute | solution.py:472

commit v5 on v4

--- a/solution.py
+++ b/solution.py
@@ -10,6 +10,7 @@
 LANES = 128
 NEAR = 4
 INNER_FLOPS = 4 * 10**9
+OUTER_FLOPS = 4 * 10**9
 BF16 = jnp.bfloat16
 F32 = jnp.float32
 
@@ -35,8 +36,9 @@
     return fine * (lane % chunks) + first - HALO, lane // chunks
 
 
-def fill_selectors(to_fields, to_weights, back, members, cols):
+def fill_selectors(to_fields, to_weights, to_sides, back, members, cols):
     fine = back.shape[0] // LANES
+    nowhere = -4 * LANES
 
     def mark(hit):
         return jnp.where(hit, 1.0, 0.0).astype(BF16)
@@ -51,13 +53,18 @@
             to_fields[m * cols : (m + 1) * cols, lanes] = mark(here & (member == m))
         for part in range(2):
             to_weights[part * cols : (part + 1) * cols, lanes] = mark(here)
-        shape = (2 * LANES, LANES)
-        column, member = target_column(shape, first, members, cols)
-        row = lax.broadcasted_iota(jnp.int32, shape, 0)
-        base = jnp.where(column < 0, column + HALO, jnp.where(column >= cols, column - cols + LANES, -4 * LANES))
-        to_fields[members * cols :, lanes] = mark(row == base + HALO * member)
-        hi = base + HALO * members
-        to_weights[2 * cols :, lanes] = mark((row == hi) | (row == hi + HALO))
+        for ref, base, count, offsets in (
+            (to_fields, members * cols, LANES, (0,)), (to_sides, 0, 2 * LANES, (0, LANES // 2)),
+        ):
+            shape = (count, LANES)
+            column, member = target_column(shape, first, members, cols)
+            row = lax.broadcasted_iota(jnp.int32, shape, 0)
+            after = column - cols + count // 2
+            at = jnp.where(column < 0, column + HALO, jnp.where(column >= cols, after, nowhere)) + HALO * member
+            hit = row == at
+            for offset in offsets[1:]:
+                hit = hit | (row == at + offset)
+            ref[base : base + count, lanes] = mark(hit)
         shape = (LANES, cols)
         lane = lax.broadcasted_iota(jnp.int32, shape, 0)
         column = fine * (lane % (LANES // members)) + first - HALO
@@ -68,40 +75,36 @@
     return jnp.swapaxes(value.astype(F32), 0, 1)
 
 
-def write_strip(out, p, g, pick, order, packs=()):
+def write_strip(out, p, g, pick, order, sides=None):
     members, levels, _, cols = p.shape
-    main = members * cols
 
     def put(pair, lanes, field, first=0):
-        rows = slice(first + 2 * pair * levels, first + 2 * (pair + 1) * levels)
+        rows = slice((first + 2 * pair) * levels, (first + 2 * pair + 2) * levels)
         both = jnp.concatenate([field[order[2 * pair]], field[order[2 * pair + 1]]], axis=0)
         out[rows, lanes] = both.astype(BF16)
 
     for half in range(2):
         lanes = slice(half * LANES, (half + 1) * LANES)
-        weight = facing(g[:, pick, lanes])
-        hi = weight.astype(BF16).astype(F32)
-        for k, part in enumerate((hi, weight - hi)):
-            for pair in range(NEAR // 2):
-                put(pair, slice(main, main + LANES), part, (2 * k + half) * NEAR * levels)
+        weight = g[:, pick, lanes]
         for m in range(members):
             to = slice(m * cols + half * LANES, m * cols + (half + 1) * LANES)
-            field = facing(p[m, :, pick, lanes])
-            product = field * weight
+            product = facing(p[m, :, pick, lanes].astype(F32) * weight)
+            rest = product - product.astype(BF16).astype(F32)
             for pair in range(HALO // 2):
-                put(pair, to, field if 2 * pair < NEAR else product)
-    for k, side in enumerate(packs):
-        field = facing(side[:, pick, :])
-        lane = lane_of(field.shape)
-        weight = field + roll(field, -HALO)
-        total = jnp.zeros_like(field)
-        for m in range(members):
-            inside = (lane >= HALO * m) & (lane < HALO * (m + 1))
-            total = jnp.where(inside, roll(weight, HALO * (m - members)), total)
-        product = field * total
-        to = slice(main + (k + 1) * LANES, main + (k + 2) * LANES)
+                put(pair, to, product)
+            for pair in range(NEAR // 2):
+                put(pair, to, rest, HALO)
+    if sides is not None:
+        left, right = (facing(side[:, pick, :]) for side in sides)
+        lane = lane_of(left.shape)
+        half = LANES // 2
+        to = slice(members * cols, members * cols + LANES)
+        product = jnp.where(lane < half, left, roll(right, half))
+        rest = jnp.where(lane < half, roll(left, half), right)
         for pair in range(HALO // 2):
-            put(pair, to, field if 2 * pair < NEAR else product)
+            put(pair, to, product)
+        for pair in range(NEAR // 2):
+            put(pair, to, rest, HALO)
 
 
 def start_kernel(place, p_hbm, increment_hbm, taper_hbm, to_near, to_left, to_right, p, g, taper, increment, sems):
@@ -119,14 +122,13 @@
             copy.start()
 
     def packed(pick, column, shift):
-        fields = [p[m, :, pick, column].astype(F32) for m in range(members)]
-        hi, lo = split(g[:, pick, column])
-        fields += [hi.astype(F32), lo.astype(F32)]
-        lane = lane_of(fields[0].shape)
-        total = jnp.zeros_like(fields[0])
-        for e, field in enumerate(fields):
+        products = [p[m, :, pick, column].astype(F32) * g[:, pick, column] for m in range(members)]
+        products += [product - product.astype(BF16).astype(F32) for product in products]
+        lane = lane_of(products[0].shape)
+        total = jnp.zeros_like(products[0])
+        for e, product in enumerate(products):
             inside = (lane >= HALO * e) & (lane < HALO * (e + 1))
-            total = jnp.where(inside, roll(field, shift + HALO * e), total)
+            total = jnp.where(inside, roll(product, shift + HALO * e), total)
         return total.astype(BF16)
 
     for k, (pick, group) in enumerate(copies):
@@ -155,26 +157,17 @@
 
 
 def corners_kernel(strip, to_left, to_right):
-    count = strip.shape[0]
-    main = strip.shape[1] - LANES
+    count, main = strip.shape
     members = main // (2 * LANES)
-    for pair in range(count // 16):
-        rows = slice(16 * pair, 16 * (pair + 1))
-        fields = [
-            [strip[rows, (2 * m + half) * LANES : (2 * m + half + 1) * LANES].astype(F32) for m in range(members)]
-            for half in range(2)
-        ]
-        if 2 * pair < NEAR:
-            for half in range(2):
-                for k in range(2):
-                    first = (2 * k + half) * (count // 4) + 16 * pair
-                    fields[half].append(strip[first : first + 16, main:].astype(F32))
+    for first in range(0, count, 16):
+        rows = slice(first, first + 16)
         lane = lane_of((16, LANES))
-        for ref, half, shift in ((to_left, 0, 0), (to_right, 1, HALO)):
+        for ref, half, base, shift in ((to_left, 0, LANES // 2, 0), (to_right, 1, 0, HALO)):
             total = jnp.zeros((16, LANES), F32)
-            for e, field in enumerate(fields[half]):
-                inside = (lane >= HALO * e) & (lane < HALO * (e + 1))
-                total = jnp.where(inside, roll(field, shift + HALO * e), total)
+            for m in range(members):
+                field = strip[rows, (2 * m + half) * LANES : (2 * m + half + 1) * LANES].astype(F32)
+                at = base + HALO * m
+                total = jnp.where((lane >= at) & (lane < at + HALO), roll(field, shift + at), total)
             ref[rows, :] = total.astype(BF16)
 
 
@@ -246,10 +239,10 @@
     return jnp.dot(a, b, preferred_element_type=F32)
 
 
-def prepare_kernel(p, g, own_values, own_weights, to_fields, to_weights, back, fields, weights):
+def prepare_kernel(p, g, own_values, own_products, to_fields, to_sides, back, fields, weights, to_weights):
     members, levels, rows, cols = p.shape
     fine = back.shape[0] // LANES
-    fill_selectors(to_fields, to_weights, back, members, cols)
+    fill_selectors(to_fields, to_weights, to_sides, back, members, cols)
     for i in range(rows // HALO):
         pick = slice(i * HALO, (i + 1) * HALO)
         out = slice(i * HALO * levels, (i + 1) * HALO * levels)
@@ -265,17 +258,18 @@
         width = min(2, fine - first)
         lanes = slice(first * LANES, (first + width) * LANES)
         field = dot(fields[...], to_fields[: members * cols, lanes])
-        weight = dot(weights[...], to_weights[: 2 * cols, lanes])
+        weight = dot(weights[...], to_weights[:, lanes])
+        product = field * weight
         for k in range(width):
             pick = slice(k * LANES, (k + 1) * LANES)
             own_values[:, first + k] = field[:, pick].reshape(rows, levels, LANES)
-            own_weights[:, first + k] = weight[:, pick].reshape(rows, levels, LANES)
+            own_products[:, first + k] = product[:, pick].reshape(rows, levels, LANES)
 
 
 def inner_kernel(
-    place, own_values, own_weights, taper, left, right, to_fields, to_weights, back, kappa,
+    place, values, own_products, taper, left, right, to_sides, back, kappa,
     keep, send, edges, edge_values,
-    x, values, packs,
+    x, packs,
 ):
     levels, rows, cols = taper.shape
     fine = x.shape[1] - 4
@@ -287,14 +281,10 @@
             packs[out, lanes] = turned(ref[:, i * HALO : (i + 1) * HALO, :]).astype(BF16)
     for first in range(0, fine, 2):
         width = min(2, fine - first)
-        lanes = slice(first * LANES, (first + width) * LANES)
-        field = dot(packs[...], to_fields[members * cols :, lanes])
-        weight = dot(packs[...], to_weights[2 * cols :, lanes])
+        beside = dot(packs[...], to_sides[:, first * LANES : (first + width) * LANES])
         for k in range(width):
             pick = slice(k * LANES, (k + 1) * LANES)
-            value = own_values[:, first + k] + field[:, pick].reshape(rows, levels, LANES)
-            values[:, first + k] = value
-            x[:, 2 + first + k] = value * (own_weights[:, first + k] + weight[:, pick].reshape(rows, levels, LANES))
+            x[:, 2 + first + k] = own_products[:, first + k] + beside[:, pick].reshape(rows, levels, LANES)
     upper, lower = place[1], 1 - place[1]
     for k in range(HALO):
         edge_values[upper, k] = values[k]
@@ -358,47 +348,29 @@
 
 
 def outer_kernel(
-    place, taper, near, far, left, right, edges, edge_values, keep_inner, send_inner,
-    to_fields, to_weights, back, kappa,
+    place, taper, near, far, left, right, edges, edge_values, to_fields, back, kappa,
     keep, send,
-    x,
+    x, fields,
 ):
     levels, rows, cols = taper.shape
-    keep[:, HALO : rows - HALO, :] = keep_inner[...]
-    send[:, HALO : rows - HALO, :] = send_inner[...]
     fine = edge_values.shape[2]
     members = LANES * fine // (cols + 2 * HALO)
     linear, constant, scale = factors(kappa[...], 4 * members)
     inside = jnp.where(place[0] == 1, 0.0, 1.0).astype(F32)
-    main = members * cols
-    part = NEAR * levels
-    sides = [jnp.concatenate([left[...], right[...]], axis=1), far[:, main + LANES :]]
-    fields = jnp.concatenate(
-        [jnp.concatenate([strip[:, :main], side], axis=1) for strip, side in zip((near, far), sides)], axis=0
-    )
-    weights = jnp.concatenate(
-        [
-            jnp.concatenate(
-                [strip[k * part : (k + 1) * part, main : main + LANES] for k in range(4)] + [side[:part]], axis=1
-            )
-            for strip, side in zip((near, far), sides)
-        ],
-        axis=0,
-    )
+    count, main = near.shape
+    fields[:count, :main] = near[...]
+    fields[:count, main:] = left[...] + right[...]
+    fields[count:, :] = far[...]
     for first in range(0, fine, 2):
         width = min(2, fine - first)
-        lanes = slice(first * LANES, (first + width) * LANES)
-        field = dot(fields, to_fields[:, lanes])
-        weight = dot(weights, to_weights[:, lanes])
+        field = dot(fields[...], to_fields[:, first * LANES : (first + width) * LANES])
         for k in range(width):
-            pick = slice(k * LANES, (k + 1) * LANES)
-            value_of = field[:, pick].reshape(2, HALO, levels, LANES)
-            weight_of = weight[:, pick].reshape(2, NEAR, levels, LANES)
+            part = field[:, k * LANES : (k + 1) * LANES].reshape(2, HALO + NEAR, levels, LANES)
             for edge in range(2):
                 for distance in range(HALO):
-                    value = value_of[edge, distance]
+                    value = part[edge, distance]
                     if distance < NEAR:
-                        value = value * weight_of[edge, distance]
+                        value = value + part[edge, HALO + distance]
                     if edge == 1 and distance == 0:
                         value = value * inside
                     x[edge, HALO - 1 - distance, 2 + first + k] = value
@@ -449,10 +421,11 @@
             axis=1,
         )
         own = slice(edge * (rows - HALO), edge * (rows - HALO) + HALO)
+        pick = slice(edge * HALO, (edge + 1) * HALO)
         finish(
             product, back[...], scale,
             lambda lanes: taper[:, own, lanes],
-            lambda natural, lanes: to_owner(place, natural, keep, send, own, lanes, levels),
+            lambda natural, lanes: to_owner(place, natural, keep, send, pick, lanes, levels),
             levels,
         )
 
@@ -494,7 +467,7 @@
         )(*ins)
 
     def strip(blocks):
-        return shape((HALO * levels, members * cols + blocks * LANES), BF16)
+        return shape(((HALO + NEAR) * levels, members * cols + blocks * LANES), BF16)
 
     pack = shape((levels, rows, LANES), BF16)
     whole = shape((levels, rows, cols), F32)
@@ -510,7 +483,7 @@
 
     to_near, to_left, to_right, p, g = call(
         start_kernel, "start",
-        (strip(1), pack, pack, shape(perturbations.shape, BF16), whole),
+        (strip(0), pack, pack, shape(perturbations.shape, BF16), whole),
         (place, *(pltpu.with_memory_space_constraint(a, pltpu.HBM) for a in (perturbations, increment, taper_norm))),
         (pltpu.VMEM(whole.shape, F32), pltpu.VMEM(whole.shape, F32), pltpu.SemaphoreType.DMA((rows // HALO, 3))),
         specs=[smem] + [hbm] * 3,
@@ -520,23 +493,27 @@
     right = shifted(to_left, "lon", -1, True)
 
     values = shape((rows, fine, *tile), F32)
-    own_values, own_weights, to_fields, to_weights, back = call(
+    own_values, own_products, to_fields, to_sides, back = call(
         prepare_kernel, "prepare",
         (
             values, values,
-            shape((members * cols + 2 * LANES, fine * LANES), BF16),
-            shape((2 * cols + 2 * LANES, fine * LANES), BF16),
+            shape((members * cols + LANES, fine * LANES), BF16),
+            shape((2 * LANES, fine * LANES), BF16),
             shape((fine * LANES, cols), BF16),
         ),
         (p, g),
-        (pltpu.VMEM((rows * levels, members * cols), BF16), pltpu.VMEM((rows * levels, 2 * cols), BF16)),
+        (
+            pltpu.VMEM((rows * levels, members * cols), BF16),
+            pltpu.VMEM((rows * levels, 2 * cols), BF16),
+            pltpu.VMEM((2 * cols, fine * LANES), BF16),
+        ),
     )
 
     p, g, own_values = lax.optimization_barrier((p, g, own_values))
-    (to_far,) = call(far_kernel, "far", (strip(3),), (place, p, g, left, right), specs=[smem] + [vmem] * 4)
+    (to_far,) = call(far_kernel, "far", (strip(1),), (place, p, g, left, right), specs=[smem] + [vmem] * 4)
     far = lax.ppermute(to_far, "lat", [(i, (i + 1 - 2 * (1 - i % 2)) % count) for i in range(count)])
     near, to_far = lax.optimization_barrier((near, to_far))
-    side = shape((HALO * levels, LANES), BF16)
+    side = shape(((HALO + NEAR) * levels, LANES), BF16)
     to_left, to_right = call(corners_kernel, "corners", (side, side), (near,))
     near_left = shifted(to_right, "lon", 1, True)
     near_right = shifted(to_left, "lon", -1, True)
@@ -546,27 +523,32 @@
     keep, send, edges, edge_values = call(
         inner_kernel, "inner",
         (part, part, shape((2, PASSES, 4, fine + 4, *tile), F32), shape((2, HALO, fine, *tile), F32)),
-        (place, own_values, own_weights, taper_norm, left, right, to_fields, to_weights, back, kappa),
+        (place, own_values, own_products, taper_norm, left, right, to_sides, back, kappa),
         (
             pltpu.VMEM((rows, fine + 4, *tile), F32),
-            pltpu.VMEM((rows, fine, *tile), F32),
             pltpu.VMEM((rows * levels, 2 * LANES), BF16),
         ),
-        specs=[smem] + [vmem] * 9,
+        specs=[smem] + [vmem] * 8,
         cost=pl.CostEstimate(flops=INNER_FLOPS, bytes_accessed=1 << 20, transcendentals=0),
     )
-    part = shape((levels // 2, rows, cols), F32)
+    middle = over_plane(*over_core(keep, send))
+    part = shape((levels // 2, 2 * HALO, cols), F32)
     keep, send = call(
         outer_kernel, "outer",
         (part, part),
         (
-            place, taper_norm, near, far, near_left, near_right, edges, edge_values, keep, send,
-            to_fields, to_weights, back, kappa,
+            place, taper_norm, near, far, near_left, near_right, edges, edge_values,
+            to_fields, back, kappa,
         ),
-        (pltpu.VMEM((2, 2 * HALO, fine + 4, *tile), F32),),
-        specs=[smem] + [vmem] * 13,
+        (
+            pltpu.VMEM((2, 2 * HALO, fine + 4, *tile), F32),
+            pltpu.VMEM((2 * (HALO + NEAR) * levels, members * cols + LANES), BF16),
+        ),
+        specs=[smem] + [vmem] * 10,
+        cost=pl.CostEstimate(flops=OUTER_FLOPS, bytes_accessed=1 << 20, transcendentals=0),
     )
-    return over_plane(*over_core(keep, send))
+    outside = over_plane(*over_core(keep, send))
+    return jnp.concatenate([outside[:, :HALO], middle, outside[:, HALO:]], axis=1)
 
 
 def solution(mesh):

time: 42.3 us -> 41.4 us (0.979)
  waiting for transfers between devices: 5.84 us -> 3.53 us
  starting transfers between devices: 14.7 us -> 16.7 us
  Pallas kernels: 20.6 us -> 20.1 us
    ppermute x1 -> x2, starting transfers between devices: 2.54 us -> 3.72 us  [over_core(): got = lax.ppermute(send, 'mem', [(i, i ^ 1) for i in range(4)])]
    ppermute x1 -> x2, waiting for transfers between devices: 1.16 us -> 0.15 us  [over_core(): got = lax.ppermute(send, 'mem', [(i, i ^ 1) for i in range(4)])]
    ppermute x1 -> x2, starting transfers between devices: 0.82 us -> 1.64 us  [over_plane(): return here + lax.ppermute(there, 'mem', [(i, i ^ 2) for i in range(4)])]
    ppermute x1, waiting for transfers between devices: 0.69 us -> 0.01 us  [local(): lax.ppermute(to_far, 'lat', [(i, (i + 1 - 2 * (1 - i % 2)) % count) for i...]
    concatenate x0 -> x1, other arithmetic: none -> 0.67 us  [local(): jnp.concatenate([outside[:, :HALO], middle, outside[:, HALO:]], axis=1)]
    add x1 -> x2, other arithmetic: 0.68 us -> 0.03 us  [over_plane(): return here + lax.ppermute(there, 'mem', [(i, i ^ 2) for i in range(4)])]
    ppermute x1 -> x2, waiting for transfers between devices: 3.97 us -> 3.37 us  [over_plane(): return here + lax.ppermute(there, 'mem', [(i, i ^ 2) for i in range(4)])]
    pallas_call x6, Pallas kernels: 20.6 us -> 20.1 us  [call(): pl.pallas_call(kernel, out_shape=tuple(outs), in_specs=specs or [vmem] *...]
  transfers between devices with their start and end apart: 8 -> 10, of which waited for: 3 -> 3; matrix products, arithmetic and copies ran while one was open for 0% -> 0% of each run, Pallas kernels for 28% -> 42%
where the time goes in v5:
time: 41.4 us; the launch traced here: 41.3 us
  Pallas kernels  20.1 us (49%)
  starting transfers between devices  16.7 us (40%)
  waiting for transfers between devices  3.53 us (9%)
  other arithmetic  0.79 us (2%)
    pallas_call x6, Pallas kernels, call(): pl.pallas_call(kernel, out_shape=tuple(outs), in_specs=specs or [vmem] *...  20.1 us
    ppermute x1, starting transfers between devices, local(): near = lax.ppermute(to_near, 'lat', [(i, i ^ 1) for i in range(count)])  4.5 us
    ppermute x4, starting transfers between devices, shifted(): return lax.ppermute(value, axis, pairs)  4.21 us
    ppermute x2, starting transfers between devices, over_core(): got = lax.ppermute(send, 'mem', [(i, i ^ 1) for i in range(4)])  3.72 us
    ppermute x2, waiting for transfers between devices, over_plane(): return here + lax.ppermute(there, 'mem', [(i, i ^ 2) for i in range(4)])  3.37 us
    ppermute x1, starting transfers between devices, local(): lax.ppermute(to_far, 'lat', [(i, (i + 1 - 2 * (1 - i % 2)) % count) for i...  2.61 us
    ppermute x2, starting transfers between devices, over_plane(): return here + lax.ppermute(there, 'mem', [(i, i ^ 2) for i in range(4)])  1.64 us
  transfers between devices with their start and end apart: 10, of which 3 were waited for; matrix products, arithmetic and copies ran while one was open for 0% of the time, Pallas kernels for 42%

profile of v5, /device:TPU:1, one launch (start us, length us, event | category | flops | bytes accessed | tf_op | source)
XLA Modules:
  0.0 41.3 jit_solution(7044109838636166479)
XLA Ops:
  0.0 0.1 pad_add_fusion.place
  0.1 2.7 %start.1 = (bf16[160,1024]{1,0:T(8,128)(2,1)S(1)}, bf16[8,64,128]{2,1,0:T(8,128)(2,1)S(1)}, bf16[8,64,128]{2,1,0:T(8,128)(2,1)S(1)}, bf16[4,8,64,256]{3,2,1,0:T(8,128)(2,1)S(1)}, f32[8,64,256]{2,1,0:T(8,128)S(1)}) custom-call(s32[4]{0:T(128)S(1)} %pad_add_fusion.place, bf16[4,8,64,256]{3,2,1,0:T(8,128)(2,1)} %p_hbm.1, f32[8,64,256]{2,1,0:T(8,128)} %increment_hbm.1, ...), custom_call_target="tpu_custom_call" | custom-call | tf_op jit(solution)/shard_map/start/pallas_call | solution.py:458
  2.8 0.0 copy-start.1
  2.8 0.0 copy-start
  2.8 4.5 %collective-permute-start = (bf16[160,1024]{1,0:T(8,128)(2,1)S(1)}, bf16[160,1024]{1,0:T(8,128)(2,1)S(1)}, u32[]{:S(2)}, u32[]{:S(2)}) collective-permute-start(bf16[160,1024]{1,0:T(8,128)(2,1)S(1)} %get-tuple-element.28), channel_id=1, source_target_pairs={{0,4},{4,0},{8,12},{12,8},{16,20},{20,16},{24,28},{28,24},{1,5},{5... | collective-permute-start | bytes 983048 | tf_op jit(solution)/shard_map/ppermute | solution.py:491
  7.3 1.2 %collective-permute-start.1 = (bf16[8,64,128]{2,1,0:T(8,128)(2,1)S(1)}, bf16[8,64,128]{2,1,0:T(8,128)(2,1)S(1)}, u32[]{:S(2)}, u32[]{:S(2)}) collective-permute-start(bf16[8,64,128]{2,1,0:T(8,128)(2,1)S(1)} %get-tuple-element.34), channel_id=1, source_target_pairs={{0,1},{1,2},{2,3},{3,0},{4,5},{5,6},{6,7},{7,4},{8,9},{9,10},{10,1... | collective-permute-start | bytes 393224 | tf_op jit(solution)/shard_map/ppermute | solution.py:436
  8.5 1.5 %collective-permute-start.2 = (bf16[8,64,128]{2,1,0:T(8,128)(2,1)S(1)}, bf16[8,64,128]{2,1,0:T(8,128)(2,1)S(1)}, u32[]{:S(2)}, u32[]{:S(2)}) collective-permute-start(bf16[8,64,128]{2,1,0:T(8,128)(2,1)S(1)} %get-tuple-element.35), channel_id=1, source_target_pairs={{0,3},{1,0},{2,1},{3,2},{4,7},{5,4},{6,5},{7,6},{8,11},{9,8},{10,9... | collective-permute-start | bytes 393224 | tf_op jit(solution)/shard_map/ppermute | solution.py:436
  10.0 3.7 %prepare.1 = (f32[64,9,8,128]{3,2,1,0:T(8,128)S(1)}, f32[64,9,8,128]{3,2,1,0:T(8,128)S(1)}, bf16[1152,1152]{1,0:T(8,128)(2,1)S(1)}, bf16[256,1152]{1,0:T(8,128)(2,1)S(1)}, bf16[1152,256]{1,0:T(8,128)(2,1)S(1)}) custom-call(bf16[4,8,64,256]{3,2,1,0:T(8,128)(2,1)S(1)} %get-tuple-element.32.p, f32[8,64,256]{2,1,0:T(8,128)S(1)} %get-tuple-element.33.g), custom_call_target="tpu_custom_call" | custom-call | tf_op jit(solution)/shard_map/prepare/pallas_call | solution.py:458
  13.7 0.8 %far.1 = bf16[160,1152]{1,0:T(8,128)(2,1)S(1)} custom-call(s32[4]{0:T(128)S(1)} %pad_add_fusion.place, bf16[4,8,64,256]{3,2,1,0:T(8,128)(2,1)S(1)} %get-tuple-element.32.p, f32[8,64,256]{2,1,0:T(8,128)S(1)} %get-tuple-element.33.g, bf16[8,64,128]{2,1,0:T(8,128)(2,1)S(1)} %collective-permute-done.1.left, bf16[8,64,128]{2,1,0:T(8,128)(2,1)S(1)} %collective-permute-done.2.right), custom_call_target="tpu_custom_call" | custom-call | tf_op jit(solution)/shard_map/far/pallas_call | solution.py:458
  14.5 2.6 %collective-permute-start.3 = (bf16[160,1152]{1,0:T(8,128)(2,1)S(1)}, bf16[160,1152]{1,0:T(8,128)(2,1)S(1)}, u32[]{:S(2)}, u32[]{:S(2)}) collective-permute-start(bf16[160,1152]{1,0:T(8,128)(2,1)S(1)} %far.1), channel_id=1, source_target_pairs={{0,28},{4,8},{8,4},{12,16},{16,12},{20,24},{24,20},{28,0},{1,29},{... | collective-permute-start | bytes 1105928 | tf_op jit(solution)/shard_map/ppermute | solution.py:514
  17.1 0.2 corners.1
  17.3 1.5 %collective-permute-start.5 = (bf16[160,128]{1,0:T(8,128)(2,1)S(1)}, bf16[160,128]{1,0:T(8,128)(2,1)S(1)}, u32[]{:S(2)}, u32[]{:S(2)}) collective-permute-start(bf16[160,128]{1,0:T(8,128)(2,1)S(1)} %get-tuple-element.38), channel_id=1, source_target_pairs={{0,3},{1,0},{2,1},{3,2},{4,7},{5,4},{6,5},{7,6},{8,11},{9,8},{10,9... | collective-permute-start | bytes 122888 | tf_op jit(solution)/shard_map/ppermute | solution.py:436
  18.8 0.0 collective-permute-start.4
  18.8 0.1 broadcast_in_dim.2.kappa
  18.9 6.7 %inner.1 = (f32[4,32,256]{2,1,0:T(8,128)S(1)}, f32[4,32,256]{2,1,0:T(8,128)S(1)}, f32[2,8,4,13,8,128]{5,4,3,2,1,0:T(8,128)S(1)}, f32[2,16,9,8,128]{4,3,2,1,0:T(8,128)S(1)}) custom-call(s32[4]{0:T(128)S(1)} %pad_add_fusion.place, f32[64,9,8,128]{3,2,1,0:T(8,128)S(1)} %get-tuple-element.40.values, f32[64,9,8,128]{3,2,1,0:T(8,128)S(1)} %get-tuple-element.41.own_products, ...), custom_call_target="tpu_custom_call" | custom-call | flops 4000000000 | bytes 1048576 | tf_op jit(solution)/shard_map/inner/pallas_call | solution.py:458
  25.6 2.6 %collective-permute-start.8 = (f32[4,32,256]{2,1,0:T(8,128)S(1)}, f32[4,32,256]{2,1,0:T(8,128)S(1)}, u32[]{:S(2)}, u32[]{:S(2)}) collective-permute-start(f32[4,32,256]{2,1,0:T(8,128)S(1)} %get-tuple-element.50), channel_id=1, source_target_pairs={{0,32},{32,0},{64,96},{96,64},{1,33},{33,1},{65,97},{97,65},{2,34}... | collective-permute-start | bytes 393224 | tf_op jit(solution)/shard_map/ppermute | solution.py:440
  28.1 6.1 %outer.1 = (f32[4,32,256]{2,1,0:T(8,128)S(1)}, f32[4,32,256]{2,1,0:T(8,128)S(1)}) custom-call(s32[4]{0:T(128)S(1)} %pad_add_fusion.place, f32[8,64,256]{2,1,0:T(8,128)S(1)} %copy-done, bf16[160,1024]{1,0:T(8,128)(2,1)S(1)} %collective-permute-done.strip.near, bf16[160,1152]{1,0:T(8,128)(2,1)S(1)} %collective-permute-done.3.far, ...), custom_call_target="tpu_custom_call" | custom-call | flops 4000000000 | bytes 1048576 | tf_op jit(solution)/shard_map/outer/pallas_call | solution.py:458
  34.3 1.1 %collective-permute-start.6 = (f32[4,32,256]{2,1,0:T(8,128)S(1)}, f32[4,32,256]{2,1,0:T(8,128)S(1)}, u32[]{:S(2)}, u32[]{:S(2)}) collective-permute-start(f32[4,32,256]{2,1,0:T(8,128)S(1)} %get-tuple-element.48), channel_id=1, source_target_pairs={{0,32},{32,0},{64,96},{96,64},{1,33},{33,1},{65,97},{97,65},{2,34}... | collective-permute-start | bytes 393224 | tf_op jit(solution)/shard_map/ppermute | solution.py:440
  35.4 0.8 %collective-permute-start.9 = (f32[2,32,256]{2,1,0:T(8,128)S(1)}, f32[2,32,256]{2,1,0:T(8,128)S(1)}, u32[]{:S(2)}, u32[]{:S(2)}) collective-permute-start(f32[2,32,256]{2,1,0:T(8,128)S(1)} %slice_add_fusion), channel_id=1, source_target_pairs={{0,64},{32,96},{64,0},{96,32},{1,65},{33,97},{65,1},{97,33},{2,66}... | collective-permute-start | bytes 196616 | tf_op jit(solution)/shard_map/ppermute | solution.py:445
  36.3 0.1 collective-permute-done.6
  36.4 0.8 %collective-permute-start.7 = (f32[2,32,256]{2,1,0:T(8,128)S(1)}, f32[2,32,256]{2,1,0:T(8,128)S(1)}, u32[]{:S(2)}, u32[]{:S(2)}) collective-permute-start(f32[2,32,256]{2,1,0:T(8,128)S(1)} %slice_add_fusion.2), channel_id=1, source_target_pairs={{0,64},{32,96},{64,0},{96,32},{1,65},{33,97},{65,1},{97,33},{2,66}... | collective-permute-start | bytes 196616 | tf_op jit(solution)/shard_map/ppermute | solution.py:445
  37.2 2.0 %collective-permute-done.9 = f32[2,32,256]{2,1,0:T(8,128)S(1)} collective-permute-done((f32[2,32,256]{2,1,0:T(8,128)S(1)}, f32[2,32,256]{2,1,0:T(8,128)S(1)}, u32[]{:S(2)}, u32[]{:S(2)}) %collective-permute-start.9) | collective-permute-done | bytes 65568 | tf_op jit(solution)/shard_map/ppermute | solution.py:445
  39.2 1.4 %collective-permute-done.7 = f32[2,32,256]{2,1,0:T(8,128)S(1)} collective-permute-done((f32[2,32,256]{2,1,0:T(8,128)S(1)}, f32[2,32,256]{2,1,0:T(8,128)S(1)}, u32[]{:S(2)}, u32[]{:S(2)}) %collective-permute-start.7) | collective-permute-done | bytes 65568 | tf_op jit(solution)/shard_map/ppermute | solution.py:445
  40.6 0.7 %pad_maximum_fusion = f32[2,64,256]{2,1,0:T(8,128)} fusion(f32[2,16,256]{2,1,0:T(8,128)S(1)} %get-tuple-element.52, f32[2,32,256]{2,1,0:T(8,128)S(1)} %fusion, f32[2,16,256]{2,1,0:T(8,128)S(1)} %get-tuple-element.51), kind=kLoop, calls=%fused_computation | loop fusion | flops 65536 | bytes 262144 | tf_op jit(solution)/shard_map/concatenate | solution.py:551
  (14 shorter events, 0.1 us)
Async XLA Ops:
  2.8 16.0 %copy-start.1 = (f32[8]{0:T(128)S(1)}, f32[8]{0:T(128)}, u32[]{:S(2)}) copy-start(f32[8]{0:T(128)} %param.7) | copy-start | bytes 100
  2.8 16.1 %copy-start = (f32[8,64,256]{2,1,0:T(8,128)S(1)}, f32[8,64,256]{2,1,0:T(8,128)}, u32[]{:S(2)}) copy-start(f32[8,64,256]{2,1,0:T(8,128)} %taper.3) | copy-start | bytes 1572868
  2.8 14.3 %collective-permute-start = (bf16[160,1024]{1,0:T(8,128)(2,1)S(1)}, bf16[160,1024]{1,0:T(8,128)(2,1)S(1)}, u32[]{:S(2)}, u32[]{:S(2)}) collective-permute-start(bf16[160,1024]{1,0:T(8,128)(2,1)S(1)} %get-tuple-element.28), channel_id=1, source_target_pairs={{0,4},{4,0},{8,12},{12,8},{16,20},{20,16},{24,28},{28,24},{1,5},{5... | collective-permute-start | bytes 983048 | tf_op jit(solution)/shard_map/ppermute | solution.py:491
  7.3 6.4 %collective-permute-start.1 = (bf16[8,64,128]{2,1,0:T(8,128)(2,1)S(1)}, bf16[8,64,128]{2,1,0:T(8,128)(2,1)S(1)}, u32[]{:S(2)}, u32[]{:S(2)}) collective-permute-start(bf16[8,64,128]{2,1,0:T(8,128)(2,1)S(1)} %get-tuple-element.34), channel_id=1, source_target_pairs={{0,1},{1,2},{2,3},{3,0},{4,5},{5,6},{6,7},{7,4},{8,9},{9,10},{10,1... | collective-permute-start | bytes 393224 | tf_op jit(solution)/shard_map/ppermute | solution.py:436
  8.5 5.2 %collective-permute-start.2 = (bf16[8,64,128]{2,1,0:T(8,128)(2,1)S(1)}, bf16[8,64,128]{2,1,0:T(8,128)(2,1)S(1)}, u32[]{:S(2)}, u32[]{:S(2)}) collective-permute-start(bf16[8,64,128]{2,1,0:T(8,128)(2,1)S(1)} %get-tuple-element.35), channel_id=1, source_target_pairs={{0,3},{1,0},{2,1},{3,2},{4,7},{5,4},{6,5},{7,6},{8,11},{9,8},{10,9... | collective-permute-start | bytes 393224 | tf_op jit(solution)/shard_map/ppermute | solution.py:436
  14.5 13.6 %collective-permute-start.3 = (bf16[160,1152]{1,0:T(8,128)(2,1)S(1)}, bf16[160,1152]{1,0:T(8,128)(2,1)S(1)}, u32[]{:S(2)}, u32[]{:S(2)}) collective-permute-start(bf16[160,1152]{1,0:T(8,128)(2,1)S(1)} %far.1), channel_id=1, source_target_pairs={{0,28},{4,8},{8,4},{12,16},{16,12},{20,24},{24,20},{28,0},{1,29},{... | collective-permute-start | bytes 1105928 | tf_op jit(solution)/shard_map/ppermute | solution.py:514
  17.3 10.9 %collective-permute-start.5 = (bf16[160,128]{1,0:T(8,128)(2,1)S(1)}, bf16[160,128]{1,0:T(8,128)(2,1)S(1)}, u32[]{:S(2)}, u32[]{:S(2)}) collective-permute-start(bf16[160,128]{1,0:T(8,128)(2,1)S(1)} %get-tuple-element.38), channel_id=1, source_target_pairs={{0,3},{1,0},{2,1},{3,2},{4,7},{5,4},{6,5},{7,6},{8,11},{9,8},{10,9... | collective-permute-start | bytes 122888 | tf_op jit(solution)/shard_map/ppermute | solution.py:436
  18.8 9.4 %collective-permute-start.4 = (bf16[160,128]{1,0:T(8,128)(2,1)S(1)}, bf16[160,128]{1,0:T(8,128)(2,1)S(1)}, u32[]{:S(2)}, u32[]{:S(2)}) collective-permute-start(bf16[160,128]{1,0:T(8,128)(2,1)S(1)} %get-tuple-element.37), channel_id=1, source_target_pairs={{0,1},{1,2},{2,3},{3,0},{4,5},{5,6},{6,7},{7,4},{8,9},{9,10},{10,1... | collective-permute-start | bytes 122888 | tf_op jit(solution)/shard_map/ppermute | solution.py:436
  25.6 9.9 %collective-permute-start.8 = (f32[4,32,256]{2,1,0:T(8,128)S(1)}, f32[4,32,256]{2,1,0:T(8,128)S(1)}, u32[]{:S(2)}, u32[]{:S(2)}) collective-permute-start(f32[4,32,256]{2,1,0:T(8,128)S(1)} %get-tuple-element.50), channel_id=1, source_target_pairs={{0,32},{32,0},{64,96},{96,64},{1,33},{33,1},{65,97},{97,65},{2,34}... | collective-permute-start | bytes 393224 | tf_op jit(solution)/shard_map/ppermute | solution.py:440
  34.3 2.1 %collective-permute-start.6 = (f32[4,32,256]{2,1,0:T(8,128)S(1)}, f32[4,32,256]{2,1,0:T(8,128)S(1)}, u32[]{:S(2)}, u32[]{:S(2)}) collective-permute-start(f32[4,32,256]{2,1,0:T(8,128)S(1)} %get-tuple-element.48), channel_id=1, source_target_pairs={{0,32},{32,0},{64,96},{96,64},{1,33},{33,1},{65,97},{97,65},{2,34}... | collective-permute-start | bytes 393224 | tf_op jit(solution)/shard_map/ppermute | solution.py:440
  35.4 3.8 %collective-permute-start.9 = (f32[2,32,256]{2,1,0:T(8,128)S(1)}, f32[2,32,256]{2,1,0:T(8,128)S(1)}, u32[]{:S(2)}, u32[]{:S(2)}) collective-permute-start(f32[2,32,256]{2,1,0:T(8,128)S(1)} %slice_add_fusion), channel_id=1, source_target_pairs={{0,64},{32,96},{64,0},{96,32},{1,65},{33,97},{65,1},{97,33},{2,66}... | collective-permute-start | bytes 196616 | tf_op jit(solution)/shard_map/ppermute | solution.py:445
  36.4 4.2 %collective-permute-start.7 = (f32[2,32,256]{2,1,0:T(8,128)S(1)}, f32[2,32,256]{2,1,0:T(8,128)S(1)}, u32[]{:S(2)}, u32[]{:S(2)}) collective-permute-start(f32[2,32,256]{2,1,0:T(8,128)S(1)} %slice_add_fusion.2), channel_id=1, source_target_pairs={{0,64},{32,96},{64,0},{96,32},{1,65},{33,97},{65,1},{97,33},{2,66}... | collective-permute-start | bytes 196616 | tf_op jit(solution)/shard_map/ppermute | solution.py:445

commit v6 on v5

--- a/solution.py
+++ b/solution.py
@@ -220,19 +220,12 @@
         write(natural, lanes)
 
 
-def to_owner(place, natural, keep, send, pick, lanes, levels):
+def to_owner(place, natural, ordered, pick, lanes, levels):
     core, plane = place[2], place[3]
     for level in range(levels):
-        owner_plane, owner_core, within = level // 4, level // 2 % 2, level % 2
-        slot = jnp.where(plane == owner_plane, 0, 2) + within
-
-        @pl.when(core == owner_core)
-        def _():
-            keep[slot, pick, lanes] = natural[level]
-
-        @pl.when(core != owner_core)
-        def _():
-            send[slot, pick, lanes] = natural[level]
+        other_core = jnp.where(core == level // 2 % 2, 0, 1)
+        other_plane = jnp.where(plane == level // 4, 0, 1)
+        ordered[levels // 2 * other_core + 2 * other_plane + level % 2, pick, lanes] = natural[level]
 
 
 def dot(a, b):
@@ -269,7 +262,7 @@
 def inner_kernel(
     place, values, own_products, taper, left, right, to_sides, back, kappa,
     keep, send, edges, edge_values,
-    x, packs,
+    x, packs, ordered,
 ):
     levels, rows, cols = taper.shape
     fine = x.shape[1] - 4
@@ -325,32 +318,34 @@
             if turn < PASSES - 1:
                 wrap(i)
 
-    def last(i, _):
+    def last(i):
         first = i * HALO
         from_row = first + HALO
         product = jnp.concatenate(
             [
-                (x[pl.ds(from_row, HALO), c + 2] * values[pl.ds(from_row, HALO), c]).reshape(HALO * levels, LANES)
+                (x[slice(from_row, from_row + HALO), c + 2] * values[slice(from_row, from_row + HALO), c]).reshape(HALO * levels, LANES)
                 for c in range(fine)
             ],
             axis=1,
         )
-        pick = pl.ds(pl.multiple_of(first, HALO), HALO)
+        pick = slice(first, first + HALO)
         finish(
             product, back[...], scale,
-            lambda lanes: taper[:, pl.ds(pl.multiple_of(from_row, HALO), HALO), lanes],
-            lambda natural, lanes: to_owner(place, natural, keep, send, pick, lanes, levels),
+            lambda lanes: taper[:, slice(from_row, from_row + HALO), lanes],
+            lambda natural, lanes: to_owner(place, natural, ordered, pick, lanes, levels),
             levels,
         )
-        return 0
-
-    lax.fori_loop(0, (rows - 2 * HALO) // HALO, last, 0)
+
+    for i in range((rows - 2 * HALO) // HALO):
+        last(i)
+    keep[...] = ordered[: levels // 2]
+    send[...] = ordered[levels // 2 :]
 
 
 def outer_kernel(
     place, taper, near, far, left, right, edges, edge_values, to_fields, back, kappa,
     keep, send,
-    x, fields,
+    x, fields, ordered,
 ):
     levels, rows, cols = taper.shape
     fine = edge_values.shape[2]
@@ -425,9 +420,11 @@
         finish(
             product, back[...], scale,
             lambda lanes: taper[:, own, lanes],
-            lambda natural, lanes: to_owner(place, natural, keep, send, pick, lanes, levels),
+            lambda natural, lanes: to_owner(place, natural, ordered, pick, lanes, levels),
             levels,
         )
+    keep[...] = ordered[: levels // 2]
+    send[...] = ordered[levels // 2 :]
 
 
 def shifted(value, axis, step, wrap):
@@ -527,6 +524,7 @@
         (
             pltpu.VMEM((rows, fine + 4, *tile), F32),
             pltpu.VMEM((rows * levels, 2 * LANES), BF16),
+            pltpu.VMEM((levels, rows - 2 * HALO, cols), F32),
         ),
         specs=[smem] + [vmem] * 8,
         cost=pl.CostEstimate(flops=INNER_FLOPS, bytes_accessed=1 << 20, transcendentals=0),
@@ -543,6 +541,7 @@
         (
             pltpu.VMEM((2, 2 * HALO, fine + 4, *tile), F32),
             pltpu.VMEM((2 * (HALO + NEAR) * levels, members * cols + LANES), BF16),
+            pltpu.VMEM((levels, 2 * HALO, cols), F32),
         ),
         specs=[smem] + [vmem] * 10,
         cost=pl.CostEstimate(flops=OUTER_FLOPS, bytes_accessed=1 << 20, transcendentals=0),

time: 41.4 us -> 40.8 us (0.986)
  Pallas kernels: 20.1 us -> 19.4 us
    pallas_call x6, Pallas kernels: 20.1 us -> 19.4 us  [call(): pl.pallas_call(kernel, out_shape=tuple(outs), in_specs=specs or [vmem] *...]
  transfers between devices with their start and end apart: 10 -> 10, of which waited for: 3 -> 3; matrix products, arithmetic and copies ran while one was open for 0% -> 0% of each run, Pallas kernels for 42% -> 41%
where the time goes in v6:
time: 40.8 us; the launch traced here: 40.7 us
  Pallas kernels  19.4 us (48%)
  starting transfers between devices  16.8 us (41%)
  waiting for transfers between devices  3.53 us (9%)
  other arithmetic  0.79 us (2%)
    pallas_call x6, Pallas kernels, call(): pl.pallas_call(kernel, out_shape=tuple(outs), in_specs=specs or [vmem] *...  19.4 us
    ppermute x1, starting transfers between devices, local(): near = lax.ppermute(to_near, 'lat', [(i, i ^ 1) for i in range(count)])  4.5 us
    ppermute x4, starting transfers between devices, shifted(): return lax.ppermute(value, axis, pairs)  4.21 us
    ppermute x2, starting transfers between devices, over_core(): got = lax.ppermute(send, 'mem', [(i, i ^ 1) for i in range(4)])  3.85 us
    ppermute x2, waiting for transfers between devices, over_plane(): return here + lax.ppermute(there, 'mem', [(i, i ^ 2) for i in range(4)])  3.37 us
    ppermute x1, starting transfers between devices, local(): lax.ppermute(to_far, 'lat', [(i, (i + 1 - 2 * (1 - i % 2)) % count) for i...  2.61 us
    ppermute x2, starting transfers between devices, over_plane(): return here + lax.ppermute(there, 'mem', [(i, i ^ 2) for i in range(4)])  1.64 us
  transfers between devices with their start and end apart: 10, of which 3 were waited for; matrix products, arithmetic and copies ran while one was open for 0% of the time, Pallas kernels for 41%

profile of v6, /device:TPU:1, one launch (start us, length us, event | category | flops | bytes accessed | tf_op | source)
XLA Modules:
  0.0 40.7 jit_solution(9112528275383057776)
XLA Ops:
  0.0 0.1 pad_add_fusion.place
  0.1 2.7 %start.1 = (bf16[160,1024]{1,0:T(8,128)(2,1)S(1)}, bf16[8,64,128]{2,1,0:T(8,128)(2,1)S(1)}, bf16[8,64,128]{2,1,0:T(8,128)(2,1)S(1)}, bf16[4,8,64,256]{3,2,1,0:T(8,128)(2,1)S(1)}, f32[8,64,256]{2,1,0:T(8,128)S(1)}) custom-call(s32[4]{0:T(128)S(1)} %pad_add_fusion.place, bf16[4,8,64,256]{3,2,1,0:T(8,128)(2,1)} %p_hbm.1, f32[8,64,256]{2,1,0:T(8,128)} %increment_hbm.1, ...), custom_call_target="tpu_custom_call" | custom-call | tf_op jit(solution)/shard_map/start/pallas_call | solution.py:455
  2.8 0.0 copy-start.1
  2.8 0.0 copy-start
  2.8 4.5 %collective-permute-start = (bf16[160,1024]{1,0:T(8,128)(2,1)S(1)}, bf16[160,1024]{1,0:T(8,128)(2,1)S(1)}, u32[]{:S(2)}, u32[]{:S(2)}) collective-permute-start(bf16[160,1024]{1,0:T(8,128)(2,1)S(1)} %get-tuple-element.28), channel_id=1, source_target_pairs={{0,4},{4,0},{8,12},{12,8},{16,20},{20,16},{24,28},{28,24},{1,5},{5... | collective-permute-start | bytes 983048 | tf_op jit(solution)/shard_map/ppermute | solution.py:488
  7.3 1.2 %collective-permute-start.1 = (bf16[8,64,128]{2,1,0:T(8,128)(2,1)S(1)}, bf16[8,64,128]{2,1,0:T(8,128)(2,1)S(1)}, u32[]{:S(2)}, u32[]{:S(2)}) collective-permute-start(bf16[8,64,128]{2,1,0:T(8,128)(2,1)S(1)} %get-tuple-element.34), channel_id=1, source_target_pairs={{0,1},{1,2},{2,3},{3,0},{4,5},{5,6},{6,7},{7,4},{8,9},{9,10},{10,1... | collective-permute-start | bytes 393224 | tf_op jit(solution)/shard_map/ppermute | solution.py:433
  8.5 1.5 %collective-permute-start.2 = (bf16[8,64,128]{2,1,0:T(8,128)(2,1)S(1)}, bf16[8,64,128]{2,1,0:T(8,128)(2,1)S(1)}, u32[]{:S(2)}, u32[]{:S(2)}) collective-permute-start(bf16[8,64,128]{2,1,0:T(8,128)(2,1)S(1)} %get-tuple-element.35), channel_id=1, source_target_pairs={{0,3},{1,0},{2,1},{3,2},{4,7},{5,4},{6,5},{7,6},{8,11},{9,8},{10,9... | collective-permute-start | bytes 393224 | tf_op jit(solution)/shard_map/ppermute | solution.py:433
  10.0 3.7 %prepare.1 = (f32[64,9,8,128]{3,2,1,0:T(8,128)S(1)}, f32[64,9,8,128]{3,2,1,0:T(8,128)S(1)}, bf16[1152,1152]{1,0:T(8,128)(2,1)S(1)}, bf16[256,1152]{1,0:T(8,128)(2,1)S(1)}, bf16[1152,256]{1,0:T(8,128)(2,1)S(1)}) custom-call(bf16[4,8,64,256]{3,2,1,0:T(8,128)(2,1)S(1)} %get-tuple-element.32.p, f32[8,64,256]{2,1,0:T(8,128)S(1)} %get-tuple-element.33.g), custom_call_target="tpu_custom_call" | custom-call | tf_op jit(solution)/shard_map/prepare/pallas_call | solution.py:455
  13.7 0.8 %far.1 = bf16[160,1152]{1,0:T(8,128)(2,1)S(1)} custom-call(s32[4]{0:T(128)S(1)} %pad_add_fusion.place, bf16[4,8,64,256]{3,2,1,0:T(8,128)(2,1)S(1)} %get-tuple-element.32.p, f32[8,64,256]{2,1,0:T(8,128)S(1)} %get-tuple-element.33.g, bf16[8,64,128]{2,1,0:T(8,128)(2,1)S(1)} %collective-permute-done.1.left, bf16[8,64,128]{2,1,0:T(8,128)(2,1)S(1)} %collective-permute-done.2.right), custom_call_target="tpu_custom_call" | custom-call | tf_op jit(solution)/shard_map/far/pallas_call | solution.py:455
  14.5 2.6 %collective-permute-start.3 = (bf16[160,1152]{1,0:T(8,128)(2,1)S(1)}, bf16[160,1152]{1,0:T(8,128)(2,1)S(1)}, u32[]{:S(2)}, u32[]{:S(2)}) collective-permute-start(bf16[160,1152]{1,0:T(8,128)(2,1)S(1)} %far.1), channel_id=1, source_target_pairs={{0,28},{4,8},{8,4},{12,16},{16,12},{20,24},{24,20},{28,0},{1,29},{... | collective-permute-start | bytes 1105928 | tf_op jit(solution)/shard_map/ppermute | solution.py:511
  17.1 0.2 corners.1
  17.3 1.5 %collective-permute-start.5 = (bf16[160,128]{1,0:T(8,128)(2,1)S(1)}, bf16[160,128]{1,0:T(8,128)(2,1)S(1)}, u32[]{:S(2)}, u32[]{:S(2)}) collective-permute-start(bf16[160,128]{1,0:T(8,128)(2,1)S(1)} %get-tuple-element.38), channel_id=1, source_target_pairs={{0,3},{1,0},{2,1},{3,2},{4,7},{5,4},{6,5},{7,6},{8,11},{9,8},{10,9... | collective-permute-start | bytes 122888 | tf_op jit(solution)/shard_map/ppermute | solution.py:433
  18.8 0.0 collective-permute-start.4
  18.8 0.1 broadcast_in_dim.2.kappa
  18.9 6.5 %inner.1 = (f32[4,32,256]{2,1,0:T(8,128)S(1)}, f32[4,32,256]{2,1,0:T(8,128)S(1)}, f32[2,8,4,13,8,128]{5,4,3,2,1,0:T(8,128)S(1)}, f32[2,16,9,8,128]{4,3,2,1,0:T(8,128)S(1)}) custom-call(s32[4]{0:T(128)S(1)} %pad_add_fusion.place, f32[64,9,8,128]{3,2,1,0:T(8,128)S(1)} %get-tuple-element.40.values, f32[64,9,8,128]{3,2,1,0:T(8,128)S(1)} %get-tuple-element.41.own_products, ...), custom_call_target="tpu_custom_call" | custom-call | flops 4000000000 | bytes 1048576 | tf_op jit(solution)/shard_map/inner/pallas_call | solution.py:455
  25.4 2.6 %collective-permute-start.8 = (f32[4,32,256]{2,1,0:T(8,128)S(1)}, f32[4,32,256]{2,1,0:T(8,128)S(1)}, u32[]{:S(2)}, u32[]{:S(2)}) collective-permute-start(f32[4,32,256]{2,1,0:T(8,128)S(1)} %get-tuple-element.50), channel_id=1, source_target_pairs={{0,32},{32,0},{64,96},{96,64},{1,33},{33,1},{65,97},{97,65},{2,34}... | collective-permute-start | bytes 393224 | tf_op jit(solution)/shard_map/ppermute | solution.py:437
  28.0 5.5 %outer.1 = (f32[4,32,256]{2,1,0:T(8,128)S(1)}, f32[4,32,256]{2,1,0:T(8,128)S(1)}) custom-call(s32[4]{0:T(128)S(1)} %pad_add_fusion.place, f32[8,64,256]{2,1,0:T(8,128)S(1)} %copy-done, bf16[160,1024]{1,0:T(8,128)(2,1)S(1)} %collective-permute-done.strip.near, bf16[160,1152]{1,0:T(8,128)(2,1)S(1)} %collective-permute-done.3.far, ...), custom_call_target="tpu_custom_call" | custom-call | flops 4000000000 | bytes 1048576 | tf_op jit(solution)/shard_map/outer/pallas_call | solution.py:455
  33.5 1.3 %collective-permute-start.6 = (f32[4,32,256]{2,1,0:T(8,128)S(1)}, f32[4,32,256]{2,1,0:T(8,128)S(1)}, u32[]{:S(2)}, u32[]{:S(2)}) collective-permute-start(f32[4,32,256]{2,1,0:T(8,128)S(1)} %get-tuple-element.48), channel_id=1, source_target_pairs={{0,32},{32,0},{64,96},{96,64},{1,33},{33,1},{65,97},{97,65},{2,34}... | collective-permute-start | bytes 393224 | tf_op jit(solution)/shard_map/ppermute | solution.py:437
  34.8 0.8 %collective-permute-start.9 = (f32[2,32,256]{2,1,0:T(8,128)S(1)}, f32[2,32,256]{2,1,0:T(8,128)S(1)}, u32[]{:S(2)}, u32[]{:S(2)}) collective-permute-start(f32[2,32,256]{2,1,0:T(8,128)S(1)} %slice_add_fusion), channel_id=1, source_target_pairs={{0,64},{32,96},{64,0},{96,32},{1,65},{33,97},{65,1},{97,33},{2,66}... | collective-permute-start | bytes 196616 | tf_op jit(solution)/shard_map/ppermute | solution.py:442
  35.6 0.1 collective-permute-done.6
  35.8 0.8 %collective-permute-start.7 = (f32[2,32,256]{2,1,0:T(8,128)S(1)}, f32[2,32,256]{2,1,0:T(8,128)S(1)}, u32[]{:S(2)}, u32[]{:S(2)}) collective-permute-start(f32[2,32,256]{2,1,0:T(8,128)S(1)} %slice_add_fusion.2), channel_id=1, source_target_pairs={{0,64},{32,96},{64,0},{96,32},{1,65},{33,97},{65,1},{97,33},{2,66}... | collective-permute-start | bytes 196616 | tf_op jit(solution)/shard_map/ppermute | solution.py:442
  36.6 2.0 %collective-permute-done.9 = f32[2,32,256]{2,1,0:T(8,128)S(1)} collective-permute-done((f32[2,32,256]{2,1,0:T(8,128)S(1)}, f32[2,32,256]{2,1,0:T(8,128)S(1)}, u32[]{:S(2)}, u32[]{:S(2)}) %collective-permute-start.9) | collective-permute-done | bytes 65568 | tf_op jit(solution)/shard_map/ppermute | solution.py:442
  38.6 1.4 %collective-permute-done.7 = f32[2,32,256]{2,1,0:T(8,128)S(1)} collective-permute-done((f32[2,32,256]{2,1,0:T(8,128)S(1)}, f32[2,32,256]{2,1,0:T(8,128)S(1)}, u32[]{:S(2)}, u32[]{:S(2)}) %collective-permute-start.7) | collective-permute-done | bytes 65568 | tf_op jit(solution)/shard_map/ppermute | solution.py:442
  40.0 0.7 %pad_maximum_fusion = f32[2,64,256]{2,1,0:T(8,128)} fusion(f32[2,16,256]{2,1,0:T(8,128)S(1)} %get-tuple-element.52, f32[2,32,256]{2,1,0:T(8,128)S(1)} %fusion, f32[2,16,256]{2,1,0:T(8,128)S(1)} %get-tuple-element.51), kind=kLoop, calls=%fused_computation | loop fusion | flops 65536 | bytes 262144 | tf_op jit(solution)/shard_map/concatenate | solution.py:550
  (14 shorter events, 0.1 us)
Async XLA Ops:
  2.8 16.0 %copy-start.1 = (f32[8]{0:T(128)S(1)}, f32[8]{0:T(128)}, u32[]{:S(2)}) copy-start(f32[8]{0:T(128)} %param.7) | copy-start | bytes 100
  2.8 16.1 %copy-start = (f32[8,64,256]{2,1,0:T(8,128)S(1)}, f32[8,64,256]{2,1,0:T(8,128)}, u32[]{:S(2)}) copy-start(f32[8,64,256]{2,1,0:T(8,128)} %taper.3) | copy-start | bytes 1572868
  2.8 14.3 %collective-permute-start = (bf16[160,1024]{1,0:T(8,128)(2,1)S(1)}, bf16[160,1024]{1,0:T(8,128)(2,1)S(1)}, u32[]{:S(2)}, u32[]{:S(2)}) collective-permute-start(bf16[160,1024]{1,0:T(8,128)(2,1)S(1)} %get-tuple-element.28), channel_id=1, source_target_pairs={{0,4},{4,0},{8,12},{12,8},{16,20},{20,16},{24,28},{28,24},{1,5},{5... | collective-permute-start | bytes 983048 | tf_op jit(solution)/shard_map/ppermute | solution.py:488
  7.3 6.4 %collective-permute-start.1 = (bf16[8,64,128]{2,1,0:T(8,128)(2,1)S(1)}, bf16[8,64,128]{2,1,0:T(8,128)(2,1)S(1)}, u32[]{:S(2)}, u32[]{:S(2)}) collective-permute-start(bf16[8,64,128]{2,1,0:T(8,128)(2,1)S(1)} %get-tuple-element.34), channel_id=1, source_target_pairs={{0,1},{1,2},{2,3},{3,0},{4,5},{5,6},{6,7},{7,4},{8,9},{9,10},{10,1... | collective-permute-start | bytes 393224 | tf_op jit(solution)/shard_map/ppermute | solution.py:433
  8.5 5.2 %collective-permute-start.2 = (bf16[8,64,128]{2,1,0:T(8,128)(2,1)S(1)}, bf16[8,64,128]{2,1,0:T(8,128)(2,1)S(1)}, u32[]{:S(2)}, u32[]{:S(2)}) collective-permute-start(bf16[8,64,128]{2,1,0:T(8,128)(2,1)S(1)} %get-tuple-element.35), channel_id=1, source_target_pairs={{0,3},{1,0},{2,1},{3,2},{4,7},{5,4},{6,5},{7,6},{8,11},{9,8},{10,9... | collective-permute-start | bytes 393224 | tf_op jit(solution)/shard_map/ppermute | solution.py:433
  14.5 13.5 %collective-permute-start.3 = (bf16[160,1152]{1,0:T(8,128)(2,1)S(1)}, bf16[160,1152]{1,0:T(8,128)(2,1)S(1)}, u32[]{:S(2)}, u32[]{:S(2)}) collective-permute-start(bf16[160,1152]{1,0:T(8,128)(2,1)S(1)} %far.1), channel_id=1, source_target_pairs={{0,28},{4,8},{8,4},{12,16},{16,12},{20,24},{24,20},{28,0},{1,29},{... | collective-permute-start | bytes 1105928 | tf_op jit(solution)/shard_map/ppermute | solution.py:511
  17.3 10.7 %collective-permute-start.5 = (bf16[160,128]{1,0:T(8,128)(2,1)S(1)}, bf16[160,128]{1,0:T(8,128)(2,1)S(1)}, u32[]{:S(2)}, u32[]{:S(2)}) collective-permute-start(bf16[160,128]{1,0:T(8,128)(2,1)S(1)} %get-tuple-element.38), channel_id=1, source_target_pairs={{0,3},{1,0},{2,1},{3,2},{4,7},{5,4},{6,5},{7,6},{8,11},{9,8},{10,9... | collective-permute-start | bytes 122888 | tf_op jit(solution)/shard_map/ppermute | solution.py:433
  18.8 9.2 %collective-permute-start.4 = (bf16[160,128]{1,0:T(8,128)(2,1)S(1)}, bf16[160,128]{1,0:T(8,128)(2,1)S(1)}, u32[]{:S(2)}, u32[]{:S(2)}) collective-permute-start(bf16[160,128]{1,0:T(8,128)(2,1)S(1)} %get-tuple-element.37), channel_id=1, source_target_pairs={{0,1},{1,2},{2,3},{3,0},{4,5},{5,6},{6,7},{7,4},{8,9},{9,10},{10,1... | collective-permute-start | bytes 122888 | tf_op jit(solution)/shard_map/ppermute | solution.py:433
  25.4 9.4 %collective-permute-start.8 = (f32[4,32,256]{2,1,0:T(8,128)S(1)}, f32[4,32,256]{2,1,0:T(8,128)S(1)}, u32[]{:S(2)}, u32[]{:S(2)}) collective-permute-start(f32[4,32,256]{2,1,0:T(8,128)S(1)} %get-tuple-element.50), channel_id=1, source_target_pairs={{0,32},{32,0},{64,96},{96,64},{1,33},{33,1},{65,97},{97,65},{2,34}... | collective-permute-start | bytes 393224 | tf_op jit(solution)/shard_map/ppermute | solution.py:437
  33.5 2.3 %collective-permute-start.6 = (f32[4,32,256]{2,1,0:T(8,128)S(1)}, f32[4,32,256]{2,1,0:T(8,128)S(1)}, u32[]{:S(2)}, u32[]{:S(2)}) collective-permute-start(f32[4,32,256]{2,1,0:T(8,128)S(1)} %get-tuple-element.48), channel_id=1, source_target_pairs={{0,32},{32,0},{64,96},{96,64},{1,33},{33,1},{65,97},{97,65},{2,34}... | collective-permute-start | bytes 393224 | tf_op jit(solution)/shard_map/ppermute | solution.py:437
  34.8 3.8 %collective-permute-start.9 = (f32[2,32,256]{2,1,0:T(8,128)S(1)}, f32[2,32,256]{2,1,0:T(8,128)S(1)}, u32[]{:S(2)}, u32[]{:S(2)}) collective-permute-start(f32[2,32,256]{2,1,0:T(8,128)S(1)} %slice_add_fusion), channel_id=1, source_target_pairs={{0,64},{32,96},{64,0},{96,32},{1,65},{33,97},{65,1},{97,33},{2,66}... | collective-permute-start | bytes 196616 | tf_op jit(solution)/shard_map/ppermute | solution.py:442
  35.8 4.2 %collective-permute-start.7 = (f32[2,32,256]{2,1,0:T(8,128)S(1)}, f32[2,32,256]{2,1,0:T(8,128)S(1)}, u32[]{:S(2)}, u32[]{:S(2)}) collective-permute-start(f32[2,32,256]{2,1,0:T(8,128)S(1)} %slice_add_fusion.2), channel_id=1, source_target_pairs={{0,64},{32,96},{64,0},{96,32},{1,65},{33,97},{65,1},{97,33},{2,66}... | collective-permute-start | bytes 196616 | tf_op jit(solution)/shard_map/ppermute | solution.py:442

commit v7 on v6

--- a/solution.py
+++ b/solution.py
@@ -29,36 +29,31 @@
     return hi, (value - hi.astype(F32)).astype(BF16)
 
 
-def target_column(shape, first, members, cols):
+def target_column(lane, first, members, cols):
     chunks = LANES // members
     fine = (cols + 2 * HALO) // chunks
-    lane = lax.broadcasted_iota(jnp.int32, shape, 1)
-    return fine * (lane % chunks) + first - HALO, lane // chunks
-
-
-def fill_selectors(to_fields, to_weights, to_sides, back, members, cols):
+    return fine * (lane & (chunks - 1)) + first - HALO, lane >> (chunks.bit_length() - 1)
+
+
+def fill_selectors(wanted, to_fields, to_weights, to_sides, back, members, cols):
     fine = back.shape[0] // LANES
     nowhere = -4 * LANES
 
     def mark(hit):
         return jnp.where(hit, 1.0, 0.0).astype(BF16)
 
-    for first in range(fine):
+    for first in wanted:
         lanes = slice(first * LANES, (first + 1) * LANES)
-        shape = (cols, LANES)
-        column, member = target_column(shape, first, members, cols)
-        row = lax.broadcasted_iota(jnp.int32, shape, 0)
-        here = row == column
+        column, member = target_column(lax.broadcasted_iota(jnp.int32, (1, LANES), 1), first, members, cols)
+        marked = mark(lax.broadcasted_iota(jnp.int32, (cols, LANES), 0) == column)
         for m in range(members):
-            to_fields[m * cols : (m + 1) * cols, lanes] = mark(here & (member == m))
+            to_fields[m * cols : (m + 1) * cols, lanes] = marked * mark(member == m)
         for part in range(2):
-            to_weights[part * cols : (part + 1) * cols, lanes] = mark(here)
+            to_weights[part * cols : (part + 1) * cols, lanes] = marked
         for ref, base, count, offsets in (
             (to_fields, members * cols, LANES, (0,)), (to_sides, 0, 2 * LANES, (0, LANES // 2)),
         ):
-            shape = (count, LANES)
-            column, member = target_column(shape, first, members, cols)
-            row = lax.broadcasted_iota(jnp.int32, shape, 0)
+            row = lax.broadcasted_iota(jnp.int32, (count, LANES), 0)
             after = column - cols + count // 2
             at = jnp.where(column < 0, column + HALO, jnp.where(column >= cols, after, nowhere)) + HALO * member
             hit = row == at
@@ -66,8 +61,7 @@
                 hit = hit | (row == at + offset)
             ref[base : base + count, lanes] = mark(hit)
         shape = (LANES, cols)
-        lane = lax.broadcasted_iota(jnp.int32, shape, 0)
-        column = fine * (lane % (LANES // members)) + first - HALO
+        column, _ = target_column(lax.broadcasted_iota(jnp.int32, shape, 0), first, members, cols)
         back[lanes, :] = mark(lax.broadcasted_iota(jnp.int32, shape, 1) == column)
 
 
@@ -75,7 +69,7 @@
     return jnp.swapaxes(value.astype(F32), 0, 1)
 
 
-def write_strip(out, p, g, pick, order, sides=None):
+def write_strip(out, p, g, pick, order):
     members, levels, _, cols = p.shape
 
     def put(pair, lanes, field, first=0):
@@ -94,17 +88,20 @@
                 put(pair, to, product)
             for pair in range(NEAR // 2):
                 put(pair, to, rest, HALO)
-    if sides is not None:
-        left, right = (facing(side[:, pick, :]) for side in sides)
-        lane = lane_of(left.shape)
-        half = LANES // 2
-        to = slice(members * cols, members * cols + LANES)
-        product = jnp.where(lane < half, left, roll(right, half))
-        rest = jnp.where(lane < half, roll(left, half), right)
-        for pair in range(HALO // 2):
-            put(pair, to, product)
-        for pair in range(NEAR // 2):
-            put(pair, to, rest, HALO)
+
+
+def write_sides(out, lanes, left, right, pick, order):
+    levels = left.shape[0]
+    left, right = facing(left[:, pick, :]), facing(right[:, pick, :])
+    lane = lane_of(left.shape)
+    half = LANES // 2
+    product = jnp.where(lane < half, left, roll(right, half))
+    rest = jnp.where(lane < half, roll(left, half), right)
+    for count, first, field in ((HALO, 0, product), (NEAR, HALO, rest)):
+        for pair in range(count // 2):
+            rows = slice((first + 2 * pair) * levels, (first + 2 * pair + 2) * levels)
+            both = jnp.concatenate([field[order[2 * pair]], field[order[2 * pair + 1]]], axis=0)
+            out[rows, lanes] = both.astype(BF16)
 
 
 def start_kernel(place, p_hbm, increment_hbm, taper_hbm, to_near, to_left, to_right, p, g, taper, increment, sems):
@@ -145,30 +142,20 @@
         to_right[:, pick, :] = packed(pick, slice(cols - LANES, cols), HALO)
 
 
-def far_kernel(place, p, g, left, right, to_far):
-    rows = p.shape[2]
+def far_kernel(place, p, g, left, right, to_far, to_near_sides):
+    members, _, rows, cols = p.shape
     for k in range(2):
         pick = slice(k * (rows - HALO), k * (rows - HALO) + HALO)
         order = range(HALO) if k == 0 else range(HALO - 1, -1, -1)
 
         @pl.when(place[1] != k)
         def _():
-            write_strip(to_far, p, g, pick, order, (left, right))
-
-
-def corners_kernel(strip, to_left, to_right):
-    count, main = strip.shape
-    members = main // (2 * LANES)
-    for first in range(0, count, 16):
-        rows = slice(first, first + 16)
-        lane = lane_of((16, LANES))
-        for ref, half, base, shift in ((to_left, 0, LANES // 2, 0), (to_right, 1, 0, HALO)):
-            total = jnp.zeros((16, LANES), F32)
-            for m in range(members):
-                field = strip[rows, (2 * m + half) * LANES : (2 * m + half + 1) * LANES].astype(F32)
-                at = base + HALO * m
-                total = jnp.where((lane >= at) & (lane < at + HALO), roll(field, shift + at), total)
-            ref[rows, :] = total.astype(BF16)
+            write_strip(to_far, p, g, pick, order)
+            write_sides(to_far, slice(members * cols, members * cols + LANES), left, right, pick, order)
+
+        @pl.when(place[1] == k)
+        def _():
+            write_sides(to_near_sides, slice(0, LANES), left, right, pick, order)
 
 
 def turned(value):
@@ -235,7 +222,12 @@
 def prepare_kernel(p, g, own_values, own_products, to_fields, to_sides, back, fields, weights, to_weights):
     members, levels, rows, cols = p.shape
     fine = back.shape[0] // LANES
-    fill_selectors(to_fields, to_weights, to_sides, back, members, cols)
+
+    def fill(first):
+        wanted = range(first, min(first + 2, fine))
+        fill_selectors(wanted, to_fields, to_weights, to_sides, back, members, cols)
+
+    fill(0)
     for i in range(rows // HALO):
         pick = slice(i * HALO, (i + 1) * HALO)
         out = slice(i * HALO * levels, (i + 1) * HALO * levels)
@@ -250,6 +242,7 @@
     for first in range(0, fine, 2):
         width = min(2, fine - first)
         lanes = slice(first * LANES, (first + width) * LANES)
+        fill(first + 2)
         field = dot(fields[...], to_fields[: members * cols, lanes])
         weight = dot(weights[...], to_weights[:, lanes])
         product = field * weight
@@ -343,7 +336,7 @@
 
 
 def outer_kernel(
-    place, taper, near, far, left, right, edges, edge_values, to_fields, back, kappa,
+    place, taper, near, far, near_sides, edges, edge_values, to_fields, back, kappa,
     keep, send,
     x, fields, ordered,
 ):
@@ -354,7 +347,7 @@
     inside = jnp.where(place[0] == 1, 0.0, 1.0).astype(F32)
     count, main = near.shape
     fields[:count, :main] = near[...]
-    fields[:count, main:] = left[...] + right[...]
+    fields[:count, main:] = near_sides[...]
     fields[count:, :] = far[...]
     for first in range(0, fine, 2):
         width = min(2, fine - first)
@@ -507,14 +500,13 @@
     )
 
     p, g, own_values = lax.optimization_barrier((p, g, own_values))
-    (to_far,) = call(far_kernel, "far", (strip(1),), (place, p, g, left, right), specs=[smem] + [vmem] * 4)
+    side = shape(((HALO + NEAR) * levels, LANES), BF16)
+    to_far, to_near_sides = call(
+        far_kernel, "far", (strip(1), side), (place, p, g, left, right), specs=[smem] + [vmem] * 4
+    )
     far = lax.ppermute(to_far, "lat", [(i, (i + 1 - 2 * (1 - i % 2)) % count) for i in range(count)])
-    near, to_far = lax.optimization_barrier((near, to_far))
-    side = shape(((HALO + NEAR) * levels, LANES), BF16)
-    to_left, to_right = call(corners_kernel, "corners", (side, side), (near,))
-    near_left = shifted(to_right, "lon", 1, True)
-    near_right = shifted(to_left, "lon", -1, True)
-    own_values, to_left = lax.optimization_barrier((own_values, to_left))
+    near_sides = lax.ppermute(to_near_sides, "lat", [(i, i ^ 1) for i in range(count)])
+    own_values, to_far = lax.optimization_barrier((own_values, to_far))
 
     part = shape((levels // 2, rows - 2 * HALO, cols), F32)
     keep, send, edges, edge_values = call(
@@ -535,7 +527,7 @@
         outer_kernel, "outer",
         (part, part),
         (
-            place, taper_norm, near, far, near_left, near_right, edges, edge_values,
+            place, taper_norm, near, far, near_sides, edges, edge_values,
             to_fields, back, kappa,
         ),
         (
@@ -543,7 +535,7 @@
             pltpu.VMEM((2 * (HALO + NEAR) * levels, members * cols + LANES), BF16),
             pltpu.VMEM((levels, 2 * HALO, cols), F32),
         ),
-        specs=[smem] + [vmem] * 10,
+        specs=[smem] + [vmem] * 9,
         cost=pl.CostEstimate(flops=OUTER_FLOPS, bytes_accessed=1 << 20, transcendentals=0),
     )
     outside = over_plane(*over_core(keep, send))

time: 40.8 us -> 41.8 us (1.025)
  waiting for transfers between devices: 3.53 us -> 5.83 us
  starting transfers between devices: 16.8 us -> 15.6 us
    ppermute x0 -> x1, waiting for transfers between devices: none -> 2.29 us  [local(): lax.ppermute(to_near_sides, 'lat', [(i, i ^ 1) for i in range(count)])]
    ppermute x0 -> x1, starting transfers between devices: none -> 1.53 us  [local(): lax.ppermute(to_near_sides, 'lat', [(i, i ^ 1) for i in range(count)])]
    ppermute x2, starting transfers between devices: 3.85 us -> 2.73 us  [over_core(): got = lax.ppermute(send, 'mem', [(i, i ^ 1) for i in range(4)])]
    ppermute x1, starting transfers between devices: 4.5 us -> 3.71 us  [local(): near = lax.ppermute(to_near, 'lat', [(i, i ^ 1) for i in range(count)])]
    ppermute x4 -> x2, starting transfers between devices: 4.21 us -> 3.46 us  [shifted(): return lax.ppermute(value, axis, pairs)]
    pallas_call x6 -> x5, Pallas kernels: 19.4 us -> 19.3 us  [call(): pl.pallas_call(kernel, out_shape=tuple(outs), in_specs=specs or [vmem] *...]
  transfers between devices with their start and end apart: 10 -> 9, of which waited for: 3 -> 4; matrix products, arithmetic and copies ran while one was open for 0% -> 0% of each run, Pallas kernels for 41% -> 40%
where the time goes in v7:
time: 41.8 us; the launch traced here: 41.6 us
  Pallas kernels  19.3 us (46%)
  starting transfers between devices  15.6 us (37%)
  waiting for transfers between devices  5.83 us (14%)
  other arithmetic  0.79 us (2%)
    pallas_call x5, Pallas kernels, call(): pl.pallas_call(kernel, out_shape=tuple(outs), in_specs=specs or [vmem] *...  19.3 us
    ppermute x1, starting transfers between devices, local(): near = lax.ppermute(to_near, 'lat', [(i, i ^ 1) for i in range(count)])  3.71 us
    ppermute x2, starting transfers between devices, shifted(): return lax.ppermute(value, axis, pairs)  3.46 us
    ppermute x2, waiting for transfers between devices, over_plane(): return here + lax.ppermute(there, 'mem', [(i, i ^ 2) for i in range(4)])  3.37 us
    ppermute x2, starting transfers between devices, over_core(): got = lax.ppermute(send, 'mem', [(i, i ^ 1) for i in range(4)])  2.73 us
    ppermute x1, starting transfers between devices, local(): lax.ppermute(to_far, 'lat', [(i, (i + 1 - 2 * (1 - i % 2)) % count) for i...  2.53 us
    ppermute x1, waiting for transfers between devices, local(): lax.ppermute(to_near_sides, 'lat', [(i, i ^ 1) for i in range(count)])  2.29 us
    ppermute x2, starting transfers between devices, over_plane(): return here + lax.ppermute(there, 'mem', [(i, i ^ 2) for i in range(4)])  1.63 us
  transfers between devices with their start and end apart: 9, of which 4 were waited for; matrix products, arithmetic and copies ran while one was open for 0% of the time, Pallas kernels for 40%

profile of v7, /device:TPU:1, one launch (start us, length us, event | category | flops | bytes accessed | tf_op | source)
XLA Modules:
  0.0 41.6 jit_solution(14150214274411814136)
XLA Ops:
  0.0 0.1 pad_add_fusion.place
  0.1 2.7 %start.1 = (bf16[160,1024]{1,0:T(8,128)(2,1)S(1)}, bf16[8,64,128]{2,1,0:T(8,128)(2,1)S(1)}, bf16[8,64,128]{2,1,0:T(8,128)(2,1)S(1)}, bf16[4,8,64,256]{3,2,1,0:T(8,128)(2,1)S(1)}, f32[8,64,256]{2,1,0:T(8,128)S(1)}) custom-call(s32[4]{0:T(128)S(1)} %pad_add_fusion.place, bf16[4,8,64,256]{3,2,1,0:T(8,128)(2,1)} %p_hbm.1, f32[8,64,256]{2,1,0:T(8,128)} %increment_hbm.1, ...), custom_call_target="tpu_custom_call" | custom-call | tf_op jit(solution)/shard_map/start/pallas_call | solution.py:448
  2.8 2.1 %collective-permute-start.1 = (bf16[8,64,128]{2,1,0:T(8,128)(2,1)S(1)}, bf16[8,64,128]{2,1,0:T(8,128)(2,1)S(1)}, u32[]{:S(2)}, u32[]{:S(2)}) collective-permute-start(bf16[8,64,128]{2,1,0:T(8,128)(2,1)S(1)} %get-tuple-element.33), channel_id=1, source_target_pairs={{0,1},{1,2},{2,3},{3,0},{4,5},{5,6},{6,7},{7,4},{8,9},{9,10},{10,1... | collective-permute-start | bytes 393224 | tf_op jit(solution)/shard_map/ppermute | solution.py:426
  4.9 1.3 %collective-permute-start.2 = (bf16[8,64,128]{2,1,0:T(8,128)(2,1)S(1)}, bf16[8,64,128]{2,1,0:T(8,128)(2,1)S(1)}, u32[]{:S(2)}, u32[]{:S(2)}) collective-permute-start(bf16[8,64,128]{2,1,0:T(8,128)(2,1)S(1)} %get-tuple-element.34), channel_id=1, source_target_pairs={{0,3},{1,0},{2,1},{3,2},{4,7},{5,4},{6,5},{7,6},{8,11},{9,8},{10,9... | collective-permute-start | bytes 393224 | tf_op jit(solution)/shard_map/ppermute | solution.py:426
  6.3 3.7 %collective-permute-start = (bf16[160,1024]{1,0:T(8,128)(2,1)S(1)}, bf16[160,1024]{1,0:T(8,128)(2,1)S(1)}, u32[]{:S(2)}, u32[]{:S(2)}) collective-permute-start(bf16[160,1024]{1,0:T(8,128)(2,1)S(1)} %get-tuple-element.27), channel_id=1, source_target_pairs={{0,4},{4,0},{8,12},{12,8},{16,20},{20,16},{24,28},{28,24},{1,5},{5... | collective-permute-start | bytes 983048 | tf_op jit(solution)/shard_map/ppermute | solution.py:481
  10.0 3.7 %prepare.1 = (f32[64,9,8,128]{3,2,1,0:T(8,128)S(1)}, f32[64,9,8,128]{3,2,1,0:T(8,128)S(1)}, bf16[1152,1152]{1,0:T(8,128)(2,1)S(1)}, bf16[256,1152]{1,0:T(8,128)(2,1)S(1)}, bf16[1152,256]{1,0:T(8,128)(2,1)S(1)}) custom-call(bf16[4,8,64,256]{3,2,1,0:T(8,128)(2,1)S(1)} %get-tuple-element.31.p, f32[8,64,256]{2,1,0:T(8,128)S(1)} %get-tuple-element.32.g), custom_call_target="tpu_custom_call" | custom-call | tf_op jit(solution)/shard_map/prepare/pallas_call | solution.py:448
  13.7 0.0 collective-permute-done.1.left
  13.7 0.0 collective-permute-done.2.right
  13.7 0.9 %far.1 = (bf16[160,1152]{1,0:T(8,128)(2,1)S(1)}, bf16[160,128]{1,0:T(8,128)(2,1)S(1)}) custom-call(s32[4]{0:T(128)S(1)} %pad_add_fusion.place, bf16[4,8,64,256]{3,2,1,0:T(8,128)(2,1)S(1)} %get-tuple-element.31.p, f32[8,64,256]{2,1,0:T(8,128)S(1)} %get-tuple-element.32.g, bf16[8,64,128]{2,1,0:T(8,128)(2,1)S(1)} %collective-permute-done.1.left, ...), custom_call_target="tpu_custom_call" | custom-call | tf_op jit(solution)/shard_map/far/pallas_call | solution.py:448
  14.6 2.5 %collective-permute-start.3 = (bf16[160,1152]{1,0:T(8,128)(2,1)S(1)}, bf16[160,1152]{1,0:T(8,128)(2,1)S(1)}, u32[]{:S(2)}, u32[]{:S(2)}) collective-permute-start(bf16[160,1152]{1,0:T(8,128)(2,1)S(1)} %get-tuple-element.35), channel_id=1, source_target_pairs={{0,28},{4,8},{8,4},{12,16},{16,12},{20,24},{24,20},{28,0},{1,29},{... | collective-permute-start | bytes 1105928 | tf_op jit(solution)/shard_map/ppermute | solution.py:507
  17.1 1.5 %collective-permute-start.4 = (bf16[160,128]{1,0:T(8,128)(2,1)S(1)}, bf16[160,128]{1,0:T(8,128)(2,1)S(1)}, u32[]{:S(2)}, u32[]{:S(2)}) collective-permute-start(bf16[160,128]{1,0:T(8,128)(2,1)S(1)} %get-tuple-element.36), channel_id=1, source_target_pairs={{0,4},{4,0},{8,12},{12,8},{16,20},{20,16},{24,28},{28,24},{1,5},{5... | collective-permute-start | bytes 122888 | tf_op jit(solution)/shard_map/ppermute | solution.py:508
  18.6 0.1 broadcast_in_dim.2.kappa
  18.7 6.5 %inner.1 = (f32[4,32,256]{2,1,0:T(8,128)S(1)}, f32[4,32,256]{2,1,0:T(8,128)S(1)}, f32[2,8,4,13,8,128]{5,4,3,2,1,0:T(8,128)S(1)}, f32[2,16,9,8,128]{4,3,2,1,0:T(8,128)S(1)}) custom-call(s32[4]{0:T(128)S(1)} %pad_add_fusion.place, f32[64,9,8,128]{3,2,1,0:T(8,128)S(1)} %get-tuple-element.38.values, f32[64,9,8,128]{3,2,1,0:T(8,128)S(1)} %get-tuple-element.39.own_products, ...), custom_call_target="tpu_custom_call" | custom-call | flops 4000000000 | bytes 1048576 | tf_op jit(solution)/shard_map/inner/pallas_call | solution.py:448
  25.2 2.2 %collective-permute-start.7 = (f32[4,32,256]{2,1,0:T(8,128)S(1)}, f32[4,32,256]{2,1,0:T(8,128)S(1)}, u32[]{:S(2)}, u32[]{:S(2)}) collective-permute-start(f32[4,32,256]{2,1,0:T(8,128)S(1)} %get-tuple-element.48), channel_id=1, source_target_pairs={{0,32},{32,0},{64,96},{96,64},{1,33},{33,1},{65,97},{97,65},{2,34}... | collective-permute-start | bytes 393224 | tf_op jit(solution)/shard_map/ppermute | solution.py:430
  27.3 2.3 %collective-permute-done.4.near_sides = bf16[160,128]{1,0:T(8,128)(2,1)S(1)} collective-permute-done((bf16[160,128]{1,0:T(8,128)(2,1)S(1)}, bf16[160,128]{1,0:T(8,128)(2,1)S(1)}, u32[]{:S(2)}, u32[]{:S(2)}) %collective-permute-start.4) | collective-permute-done | bytes 40992 | tf_op jit(solution)/shard_map/ppermute | solution.py:508
  29.6 0.0 collective-permute-done.near
  29.6 5.5 %outer.1 = (f32[4,32,256]{2,1,0:T(8,128)S(1)}, f32[4,32,256]{2,1,0:T(8,128)S(1)}) custom-call(s32[4]{0:T(128)S(1)} %pad_add_fusion.place, f32[8,64,256]{2,1,0:T(8,128)S(1)} %copy-done, bf16[160,1024]{1,0:T(8,128)(2,1)S(1)} %collective-permute-done.near, bf16[160,1152]{1,0:T(8,128)(2,1)S(1)} %collective-permute-done.3.far, ...), custom_call_target="tpu_custom_call" | custom-call | flops 4000000000 | bytes 1048576 | tf_op jit(solution)/shard_map/outer/pallas_call | solution.py:448
  35.2 0.6 %collective-permute-start.5 = (f32[4,32,256]{2,1,0:T(8,128)S(1)}, f32[4,32,256]{2,1,0:T(8,128)S(1)}, u32[]{:S(2)}, u32[]{:S(2)}) collective-permute-start(f32[4,32,256]{2,1,0:T(8,128)S(1)} %get-tuple-element.46), channel_id=1, source_target_pairs={{0,32},{32,0},{64,96},{96,64},{1,33},{33,1},{65,97},{97,65},{2,34}... | collective-permute-start | bytes 393224 | tf_op jit(solution)/shard_map/ppermute | solution.py:430
  35.8 0.8 %collective-permute-start.8 = (f32[2,32,256]{2,1,0:T(8,128)S(1)}, f32[2,32,256]{2,1,0:T(8,128)S(1)}, u32[]{:S(2)}, u32[]{:S(2)}) collective-permute-start(f32[2,32,256]{2,1,0:T(8,128)S(1)} %slice_add_fusion), channel_id=1, source_target_pairs={{0,64},{32,96},{64,0},{96,32},{1,65},{33,97},{65,1},{97,33},{2,66}... | collective-permute-start | bytes 196616 | tf_op jit(solution)/shard_map/ppermute | solution.py:435
  36.6 0.2 collective-permute-done.5
  36.7 0.8 %collective-permute-start.6 = (f32[2,32,256]{2,1,0:T(8,128)S(1)}, f32[2,32,256]{2,1,0:T(8,128)S(1)}, u32[]{:S(2)}, u32[]{:S(2)}) collective-permute-start(f32[2,32,256]{2,1,0:T(8,128)S(1)} %slice_add_fusion.2), channel_id=1, source_target_pairs={{0,64},{32,96},{64,0},{96,32},{1,65},{33,97},{65,1},{97,33},{2,66}... | collective-permute-start | bytes 196616 | tf_op jit(solution)/shard_map/ppermute | solution.py:435
  37.5 2.0 %collective-permute-done.8 = f32[2,32,256]{2,1,0:T(8,128)S(1)} collective-permute-done((f32[2,32,256]{2,1,0:T(8,128)S(1)}, f32[2,32,256]{2,1,0:T(8,128)S(1)}, u32[]{:S(2)}, u32[]{:S(2)}) %collective-permute-start.8) | collective-permute-done | bytes 65568 | tf_op jit(solution)/shard_map/ppermute | solution.py:435
  39.5 1.4 %collective-permute-done.6 = f32[2,32,256]{2,1,0:T(8,128)S(1)} collective-permute-done((f32[2,32,256]{2,1,0:T(8,128)S(1)}, f32[2,32,256]{2,1,0:T(8,128)S(1)}, u32[]{:S(2)}, u32[]{:S(2)}) %collective-permute-start.6) | collective-permute-done | bytes 65568 | tf_op jit(solution)/shard_map/ppermute | solution.py:435
  41.0 0.7 %pad_maximum_fusion = f32[2,64,256]{2,1,0:T(8,128)} fusion(f32[2,16,256]{2,1,0:T(8,128)S(1)} %get-tuple-element.50, f32[2,32,256]{2,1,0:T(8,128)S(1)} %fusion, f32[2,16,256]{2,1,0:T(8,128)S(1)} %get-tuple-element.49), kind=kLoop, calls=%fused_computation | loop fusion | flops 65536 | bytes 262144 | tf_op jit(solution)/shard_map/concatenate | solution.py:542
  (11 shorter events, 0.1 us)
Async XLA Ops:
  0.1 18.5 %copy-start.1 = (f32[8]{0:T(128)S(1)}, f32[8]{0:T(128)}, u32[]{:S(2)}) copy-start(f32[8]{0:T(128)} %param.7) | copy-start | bytes 100
  0.1 18.6 %copy-start = (f32[8,64,256]{2,1,0:T(8,128)S(1)}, f32[8,64,256]{2,1,0:T(8,128)}, u32[]{:S(2)}) copy-start(f32[8,64,256]{2,1,0:T(8,128)} %taper.3) | copy-start | bytes 1572868
  2.8 10.9 %collective-permute-start.1 = (bf16[8,64,128]{2,1,0:T(8,128)(2,1)S(1)}, bf16[8,64,128]{2,1,0:T(8,128)(2,1)S(1)}, u32[]{:S(2)}, u32[]{:S(2)}) collective-permute-start(bf16[8,64,128]{2,1,0:T(8,128)(2,1)S(1)} %get-tuple-element.33), channel_id=1, source_target_pairs={{0,1},{1,2},{2,3},{3,0},{4,5},{5,6},{6,7},{7,4},{8,9},{9,10},{10,1... | collective-permute-start | bytes 393224 | tf_op jit(solution)/shard_map/ppermute | solution.py:426
  4.9 8.8 %collective-permute-start.2 = (bf16[8,64,128]{2,1,0:T(8,128)(2,1)S(1)}, bf16[8,64,128]{2,1,0:T(8,128)(2,1)S(1)}, u32[]{:S(2)}, u32[]{:S(2)}) collective-permute-start(bf16[8,64,128]{2,1,0:T(8,128)(2,1)S(1)} %get-tuple-element.34), channel_id=1, source_target_pairs={{0,3},{1,0},{2,1},{3,2},{4,7},{5,4},{6,5},{7,6},{8,11},{9,8},{10,9... | collective-permute-start | bytes 393224 | tf_op jit(solution)/shard_map/ppermute | solution.py:426
  6.3 23.4 %collective-permute-start = (bf16[160,1024]{1,0:T(8,128)(2,1)S(1)}, bf16[160,1024]{1,0:T(8,128)(2,1)S(1)}, u32[]{:S(2)}, u32[]{:S(2)}) collective-permute-start(bf16[160,1024]{1,0:T(8,128)(2,1)S(1)} %get-tuple-element.27), channel_id=1, source_target_pairs={{0,4},{4,0},{8,12},{12,8},{16,20},{20,16},{24,28},{28,24},{1,5},{5... | collective-permute-start | bytes 983048 | tf_op jit(solution)/shard_map/ppermute | solution.py:481
  14.6 15.1 %collective-permute-start.3 = (bf16[160,1152]{1,0:T(8,128)(2,1)S(1)}, bf16[160,1152]{1,0:T(8,128)(2,1)S(1)}, u32[]{:S(2)}, u32[]{:S(2)}) collective-permute-start(bf16[160,1152]{1,0:T(8,128)(2,1)S(1)} %get-tuple-element.35), channel_id=1, source_target_pairs={{0,28},{4,8},{8,4},{12,16},{16,12},{20,24},{24,20},{28,0},{1,29},{... | collective-permute-start | bytes 1105928 | tf_op jit(solution)/shard_map/ppermute | solution.py:507
  17.1 12.6 %collective-permute-start.4 = (bf16[160,128]{1,0:T(8,128)(2,1)S(1)}, bf16[160,128]{1,0:T(8,128)(2,1)S(1)}, u32[]{:S(2)}, u32[]{:S(2)}) collective-permute-start(bf16[160,128]{1,0:T(8,128)(2,1)S(1)} %get-tuple-element.36), channel_id=1, source_target_pairs={{0,4},{4,0},{8,12},{12,8},{16,20},{20,16},{24,28},{28,24},{1,5},{5... | collective-permute-start | bytes 122888 | tf_op jit(solution)/shard_map/ppermute | solution.py:508
  25.2 10.5 %collective-permute-start.7 = (f32[4,32,256]{2,1,0:T(8,128)S(1)}, f32[4,32,256]{2,1,0:T(8,128)S(1)}, u32[]{:S(2)}, u32[]{:S(2)}) collective-permute-start(f32[4,32,256]{2,1,0:T(8,128)S(1)} %get-tuple-element.48), channel_id=1, source_target_pairs={{0,32},{32,0},{64,96},{96,64},{1,33},{33,1},{65,97},{97,65},{2,34}... | collective-permute-start | bytes 393224 | tf_op jit(solution)/shard_map/ppermute | solution.py:430
  35.2 1.6 %collective-permute-start.5 = (f32[4,32,256]{2,1,0:T(8,128)S(1)}, f32[4,32,256]{2,1,0:T(8,128)S(1)}, u32[]{:S(2)}, u32[]{:S(2)}) collective-permute-start(f32[4,32,256]{2,1,0:T(8,128)S(1)} %get-tuple-element.46), channel_id=1, source_target_pairs={{0,32},{32,0},{64,96},{96,64},{1,33},{33,1},{65,97},{97,65},{2,34}... | collective-permute-start | bytes 393224 | tf_op jit(solution)/shard_map/ppermute | solution.py:430
  35.8 3.8 %collective-permute-start.8 = (f32[2,32,256]{2,1,0:T(8,128)S(1)}, f32[2,32,256]{2,1,0:T(8,128)S(1)}, u32[]{:S(2)}, u32[]{:S(2)}) collective-permute-start(f32[2,32,256]{2,1,0:T(8,128)S(1)} %slice_add_fusion), channel_id=1, source_target_pairs={{0,64},{32,96},{64,0},{96,32},{1,65},{33,97},{65,1},{97,33},{2,66}... | collective-permute-start | bytes 196616 | tf_op jit(solution)/shard_map/ppermute | solution.py:435
  36.7 4.2 %collective-permute-start.6 = (f32[2,32,256]{2,1,0:T(8,128)S(1)}, f32[2,32,256]{2,1,0:T(8,128)S(1)}, u32[]{:S(2)}, u32[]{:S(2)}) collective-permute-start(f32[2,32,256]{2,1,0:T(8,128)S(1)} %slice_add_fusion.2), channel_id=1, source_target_pairs={{0,64},{32,96},{64,0},{96,32},{1,65},{33,97},{65,1},{97,33},{2,66}... | collective-permute-start | bytes 196616 | tf_op jit(solution)/shard_map/ppermute | solution.py:435

commit v8 on v7

--- a/solution.py
+++ b/solution.py
@@ -142,7 +142,7 @@
         to_right[:, pick, :] = packed(pick, slice(cols - LANES, cols), HALO)
 
 
-def far_kernel(place, p, g, left, right, to_far, to_near_sides):
+def far_kernel(place, p, g, left, right, to_far):
     members, _, rows, cols = p.shape
     for k in range(2):
         pick = slice(k * (rows - HALO), k * (rows - HALO) + HALO)
@@ -152,6 +152,13 @@
         def _():
             write_strip(to_far, p, g, pick, order)
             write_sides(to_far, slice(members * cols, members * cols + LANES), left, right, pick, order)
+
+
+def near_sides_kernel(place, left, right, to_near_sides):
+    rows = left.shape[1]
+    for k in range(2):
+        pick = slice(k * (rows - HALO), k * (rows - HALO) + HALO)
+        order = range(HALO) if k == 0 else range(HALO - 1, -1, -1)
 
         @pl.when(place[1] == k)
         def _():
@@ -501,12 +508,14 @@
 
     p, g, own_values = lax.optimization_barrier((p, g, own_values))
     side = shape(((HALO + NEAR) * levels, LANES), BF16)
-    to_far, to_near_sides = call(
-        far_kernel, "far", (strip(1), side), (place, p, g, left, right), specs=[smem] + [vmem] * 4
+    (to_far,) = call(far_kernel, "far", (strip(1),), (place, p, g, left, right), specs=[smem] + [vmem] * 4)
+    far = lax.ppermute(to_far, "lat", [(i, (i + 1 - 2 * (1 - i % 2)) % count) for i in range(count)])
+    left, right, to_far = lax.optimization_barrier((left, right, to_far))
+    (to_near_sides,) = call(
+        near_sides_kernel, "near_sides", (side,), (place, left, right), specs=[smem] + [vmem] * 2
     )
-    far = lax.ppermute(to_far, "lat", [(i, (i + 1 - 2 * (1 - i % 2)) % count) for i in range(count)])
     near_sides = lax.ppermute(to_near_sides, "lat", [(i, i ^ 1) for i in range(count)])
-    own_values, to_far = lax.optimization_barrier((own_values, to_far))
+    own_values, near, to_near_sides = lax.optimization_barrier((own_values, near, to_near_sides))
 
     part = shape((levels // 2, rows - 2 * HALO, cols), F32)
     keep, send, edges, edge_values = call(

time: 41.8 us -> 41.7 us (level)
  waiting for transfers between devices: 5.83 us -> 4.91 us
  Pallas kernels: 19.3 us -> 19.8 us
    ppermute x1, waiting for transfers between devices: 2.29 us -> 1.38 us  [local(): lax.ppermute(to_near_sides, 'lat', [(i, i ^ 1) for i in range(count)])]
    ppermute x1, starting transfers between devices: 3.71 us -> 4.5 us  [local(): near = lax.ppermute(to_near, 'lat', [(i, i ^ 1) for i in range(count)])]
    ppermute x2, starting transfers between devices: 3.46 us -> 2.68 us  [shifted(): return lax.ppermute(value, axis, pairs)]
    pallas_call x5 -> x6, Pallas kernels: 19.3 us -> 19.8 us  [call(): pl.pallas_call(kernel, out_shape=tuple(outs), in_specs=specs or [vmem] *...]
  transfers between devices with their start and end apart: 9 -> 9, of which waited for: 4 -> 4; matrix products, arithmetic and copies ran while one was open for 0% -> 0% of each run, Pallas kernels for 40% -> 41%
where the time goes in v8:
time: 41.7 us; the launch traced here: 41.6 us
  Pallas kernels  19.8 us (47%)
  starting transfers between devices  15.9 us (38%)
  waiting for transfers between devices  4.91 us (12%)
  other arithmetic  0.79 us (2%)
    pallas_call x6, Pallas kernels, call(): pl.pallas_call(kernel, out_shape=tuple(outs), in_specs=specs or [vmem] *...  19.8 us
    ppermute x1, starting transfers between devices, local(): near = lax.ppermute(to_near, 'lat', [(i, i ^ 1) for i in range(count)])  4.5 us
    ppermute x2, waiting for transfers between devices, over_plane(): return here + lax.ppermute(there, 'mem', [(i, i ^ 2) for i in range(4)])  3.37 us
    ppermute x2, starting transfers between devices, over_core(): got = lax.ppermute(send, 'mem', [(i, i ^ 1) for i in range(4)])  2.73 us
    ppermute x2, starting transfers between devices, shifted(): return lax.ppermute(value, axis, pairs)  2.68 us
    ppermute x1, starting transfers between devices, local(): lax.ppermute(to_far, 'lat', [(i, (i + 1 - 2 * (1 - i % 2)) % count) for i...  2.61 us
    ppermute x1, starting transfers between devices, local(): lax.ppermute(to_near_sides, 'lat', [(i, i ^ 1) for i in range(count)])  1.71 us
    ppermute x2, starting transfers between devices, over_plane(): return here + lax.ppermute(there, 'mem', [(i, i ^ 2) for i in range(4)])  1.64 us
  transfers between devices with their start and end apart: 9, of which 4 were waited for; matrix products, arithmetic and copies ran while one was open for 0% of the time, Pallas kernels for 41%

profile of v8, /device:TPU:1, one launch (start us, length us, event | category | flops | bytes accessed | tf_op | source)
XLA Modules:
  0.0 41.6 jit_solution(8071715266445627605)
XLA Ops:
  0.0 0.1 pad_add_fusion.place
  0.1 2.7 %start.1 = (bf16[160,1024]{1,0:T(8,128)(2,1)S(1)}, bf16[8,64,128]{2,1,0:T(8,128)(2,1)S(1)}, bf16[8,64,128]{2,1,0:T(8,128)(2,1)S(1)}, bf16[4,8,64,256]{3,2,1,0:T(8,128)(2,1)S(1)}, f32[8,64,256]{2,1,0:T(8,128)S(1)}) custom-call(s32[4]{0:T(128)S(1)} %pad_add_fusion.place, bf16[4,8,64,256]{3,2,1,0:T(8,128)(2,1)} %p_hbm.1, f32[8,64,256]{2,1,0:T(8,128)} %increment_hbm.1, ...), custom_call_target="tpu_custom_call" | custom-call | tf_op jit(solution)/shard_map/start/pallas_call | solution.py:455
  2.8 0.0 copy-start.1
  2.8 0.0 copy-start
  2.8 4.5 %collective-permute-start = (bf16[160,1024]{1,0:T(8,128)(2,1)S(1)}, bf16[160,1024]{1,0:T(8,128)(2,1)S(1)}, u32[]{:S(2)}, u32[]{:S(2)}) collective-permute-start(bf16[160,1024]{1,0:T(8,128)(2,1)S(1)} %get-tuple-element.32), channel_id=1, source_target_pairs={{0,4},{4,0},{8,12},{12,8},{16,20},{20,16},{24,28},{28,24},{1,5},{5... | collective-permute-start | bytes 983048 | tf_op jit(solution)/shard_map/ppermute | solution.py:488
  7.3 1.2 %collective-permute-start.1 = (bf16[8,64,128]{2,1,0:T(8,128)(2,1)S(1)}, bf16[8,64,128]{2,1,0:T(8,128)(2,1)S(1)}, u32[]{:S(2)}, u32[]{:S(2)}) collective-permute-start(bf16[8,64,128]{2,1,0:T(8,128)(2,1)S(1)} %get-tuple-element.33), channel_id=1, source_target_pairs={{0,1},{1,2},{2,3},{3,0},{4,5},{5,6},{6,7},{7,4},{8,9},{9,10},{10,1... | collective-permute-start | bytes 393224 | tf_op jit(solution)/shard_map/ppermute | solution.py:433
  8.5 1.5 %collective-permute-start.2 = (bf16[8,64,128]{2,1,0:T(8,128)(2,1)S(1)}, bf16[8,64,128]{2,1,0:T(8,128)(2,1)S(1)}, u32[]{:S(2)}, u32[]{:S(2)}) collective-permute-start(bf16[8,64,128]{2,1,0:T(8,128)(2,1)S(1)} %get-tuple-element.34), channel_id=1, source_target_pairs={{0,3},{1,0},{2,1},{3,2},{4,7},{5,4},{6,5},{7,6},{8,11},{9,8},{10,9... | collective-permute-start | bytes 393224 | tf_op jit(solution)/shard_map/ppermute | solution.py:433
  10.0 3.7 %prepare.1 = (f32[64,9,8,128]{3,2,1,0:T(8,128)S(1)}, f32[64,9,8,128]{3,2,1,0:T(8,128)S(1)}, bf16[1152,1152]{1,0:T(8,128)(2,1)S(1)}, bf16[256,1152]{1,0:T(8,128)(2,1)S(1)}, bf16[1152,256]{1,0:T(8,128)(2,1)S(1)}) custom-call(bf16[4,8,64,256]{3,2,1,0:T(8,128)(2,1)S(1)} %get-tuple-element.35.p, f32[8,64,256]{2,1,0:T(8,128)S(1)} %get-tuple-element.36.g), custom_call_target="tpu_custom_call" | custom-call | tf_op jit(solution)/shard_map/prepare/pallas_call | solution.py:455
  13.7 0.8 %far.1 = bf16[160,1152]{1,0:T(8,128)(2,1)S(1)} custom-call(s32[4]{0:T(128)S(1)} %pad_add_fusion.place, bf16[4,8,64,256]{3,2,1,0:T(8,128)(2,1)S(1)} %get-tuple-element.35.p, f32[8,64,256]{2,1,0:T(8,128)S(1)} %get-tuple-element.36.g, bf16[8,64,128]{2,1,0:T(8,128)(2,1)S(1)} %collective-permute-done.1.left, bf16[8,64,128]{2,1,0:T(8,128)(2,1)S(1)} %collective-permute-done.2.right), custom_call_target="tpu_custom_call" | custom-call | tf_op jit(solution)/shard_map/far/pallas_call | solution.py:455
  14.5 2.6 %collective-permute-start.3 = (bf16[160,1152]{1,0:T(8,128)(2,1)S(1)}, bf16[160,1152]{1,0:T(8,128)(2,1)S(1)}, u32[]{:S(2)}, u32[]{:S(2)}) collective-permute-start(bf16[160,1152]{1,0:T(8,128)(2,1)S(1)} %far.1), channel_id=1, source_target_pairs={{0,28},{4,8},{8,4},{12,16},{16,12},{20,24},{24,20},{28,0},{1,29},{... | collective-permute-start | bytes 1105928 | tf_op jit(solution)/shard_map/ppermute | solution.py:512
  17.1 0.6 %near_sides.1 = bf16[160,128]{1,0:T(8,128)(2,1)S(1)} custom-call(s32[4]{0:T(128)S(1)} %pad_add_fusion.place, bf16[8,64,128]{2,1,0:T(8,128)(2,1)S(1)} %collective-permute-done.1.left, bf16[8,64,128]{2,1,0:T(8,128)(2,1)S(1)} %collective-permute-done.2.right), custom_call_target="tpu_custom_call" | custom-call | tf_op jit(solution)/shard_map/near_sides/pallas_call | solution.py:455
  17.7 1.7 %collective-permute-start.4 = (bf16[160,128]{1,0:T(8,128)(2,1)S(1)}, bf16[160,128]{1,0:T(8,128)(2,1)S(1)}, u32[]{:S(2)}, u32[]{:S(2)}) collective-permute-start(bf16[160,128]{1,0:T(8,128)(2,1)S(1)} %near_sides.1), channel_id=1, source_target_pairs={{0,4},{4,0},{8,12},{12,8},{16,20},{20,16},{24,28},{28,24},{1,5},{5... | collective-permute-start | bytes 122888 | tf_op jit(solution)/shard_map/ppermute | solution.py:517
  19.4 0.1 broadcast_in_dim.2.kappa
  19.5 6.5 %inner.1 = (f32[4,32,256]{2,1,0:T(8,128)S(1)}, f32[4,32,256]{2,1,0:T(8,128)S(1)}, f32[2,8,4,13,8,128]{5,4,3,2,1,0:T(8,128)S(1)}, f32[2,16,9,8,128]{4,3,2,1,0:T(8,128)S(1)}) custom-call(s32[4]{0:T(128)S(1)} %pad_add_fusion.place, f32[64,9,8,128]{3,2,1,0:T(8,128)S(1)} %get-tuple-element.40.values, f32[64,9,8,128]{3,2,1,0:T(8,128)S(1)} %get-tuple-element.41.own_products, ...), custom_call_target="tpu_custom_call" | custom-call | flops 4000000000 | bytes 1048576 | tf_op jit(solution)/shard_map/inner/pallas_call | solution.py:455
  26.0 2.2 %collective-permute-start.7 = (f32[4,32,256]{2,1,0:T(8,128)S(1)}, f32[4,32,256]{2,1,0:T(8,128)S(1)}, u32[]{:S(2)}, u32[]{:S(2)}) collective-permute-start(f32[4,32,256]{2,1,0:T(8,128)S(1)} %get-tuple-element.50), channel_id=1, source_target_pairs={{0,32},{32,0},{64,96},{96,64},{1,33},{33,1},{65,97},{97,65},{2,34}... | collective-permute-start | bytes 393224 | tf_op jit(solution)/shard_map/ppermute | solution.py:437
  28.2 1.4 %collective-permute-done.4.near_sides = bf16[160,128]{1,0:T(8,128)(2,1)S(1)} collective-permute-done((bf16[160,128]{1,0:T(8,128)(2,1)S(1)}, bf16[160,128]{1,0:T(8,128)(2,1)S(1)}, u32[]{:S(2)}, u32[]{:S(2)}) %collective-permute-start.4) | collective-permute-done | bytes 40992 | tf_op jit(solution)/shard_map/ppermute | solution.py:517
  29.6 5.5 %outer.1 = (f32[4,32,256]{2,1,0:T(8,128)S(1)}, f32[4,32,256]{2,1,0:T(8,128)S(1)}) custom-call(s32[4]{0:T(128)S(1)} %pad_add_fusion.place, f32[8,64,256]{2,1,0:T(8,128)S(1)} %copy-done, bf16[160,1024]{1,0:T(8,128)(2,1)S(1)} %collective-permute-done.near, bf16[160,1152]{1,0:T(8,128)(2,1)S(1)} %collective-permute-done.3.far, ...), custom_call_target="tpu_custom_call" | custom-call | flops 4000000000 | bytes 1048576 | tf_op jit(solution)/shard_map/outer/pallas_call | solution.py:455
  35.1 0.6 %collective-permute-start.5 = (f32[4,32,256]{2,1,0:T(8,128)S(1)}, f32[4,32,256]{2,1,0:T(8,128)S(1)}, u32[]{:S(2)}, u32[]{:S(2)}) collective-permute-start(f32[4,32,256]{2,1,0:T(8,128)S(1)} %get-tuple-element.48), channel_id=1, source_target_pairs={{0,32},{32,0},{64,96},{96,64},{1,33},{33,1},{65,97},{97,65},{2,34}... | collective-permute-start | bytes 393224 | tf_op jit(solution)/shard_map/ppermute | solution.py:437
  35.7 0.8 %collective-permute-start.8 = (f32[2,32,256]{2,1,0:T(8,128)S(1)}, f32[2,32,256]{2,1,0:T(8,128)S(1)}, u32[]{:S(2)}, u32[]{:S(2)}) collective-permute-start(f32[2,32,256]{2,1,0:T(8,128)S(1)} %slice_add_fusion), channel_id=1, source_target_pairs={{0,64},{32,96},{64,0},{96,32},{1,65},{33,97},{65,1},{97,33},{2,66}... | collective-permute-start | bytes 196616 | tf_op jit(solution)/shard_map/ppermute | solution.py:442
  36.5 0.1 collective-permute-done.5
  36.7 0.8 %collective-permute-start.6 = (f32[2,32,256]{2,1,0:T(8,128)S(1)}, f32[2,32,256]{2,1,0:T(8,128)S(1)}, u32[]{:S(2)}, u32[]{:S(2)}) collective-permute-start(f32[2,32,256]{2,1,0:T(8,128)S(1)} %slice_add_fusion.2), channel_id=1, source_target_pairs={{0,64},{32,96},{64,0},{96,32},{1,65},{33,97},{65,1},{97,33},{2,66}... | collective-permute-start | bytes 196616 | tf_op jit(solution)/shard_map/ppermute | solution.py:442
  37.5 2.0 %collective-permute-done.8 = f32[2,32,256]{2,1,0:T(8,128)S(1)} collective-permute-done((f32[2,32,256]{2,1,0:T(8,128)S(1)}, f32[2,32,256]{2,1,0:T(8,128)S(1)}, u32[]{:S(2)}, u32[]{:S(2)}) %collective-permute-start.8) | collective-permute-done | bytes 65568 | tf_op jit(solution)/shard_map/ppermute | solution.py:442
  39.5 1.4 %collective-permute-done.6 = f32[2,32,256]{2,1,0:T(8,128)S(1)} collective-permute-done((f32[2,32,256]{2,1,0:T(8,128)S(1)}, f32[2,32,256]{2,1,0:T(8,128)S(1)}, u32[]{:S(2)}, u32[]{:S(2)}) %collective-permute-start.6) | collective-permute-done | bytes 65568 | tf_op jit(solution)/shard_map/ppermute | solution.py:442
  40.9 0.7 %pad_maximum_fusion = f32[2,64,256]{2,1,0:T(8,128)} fusion(f32[2,16,256]{2,1,0:T(8,128)S(1)} %get-tuple-element.52, f32[2,32,256]{2,1,0:T(8,128)S(1)} %fusion, f32[2,16,256]{2,1,0:T(8,128)S(1)} %get-tuple-element.51), kind=kLoop, calls=%fused_computation | loop fusion | flops 65536 | bytes 262144 | tf_op jit(solution)/shard_map/concatenate | solution.py:551
  (12 shorter events, 0.1 us)
Async XLA Ops:
  2.8 16.7 %copy-start.1 = (f32[8]{0:T(128)S(1)}, f32[8]{0:T(128)}, u32[]{:S(2)}) copy-start(f32[8]{0:T(128)} %param.7) | copy-start | bytes 100
  2.8 16.7 %copy-start = (f32[8,64,256]{2,1,0:T(8,128)S(1)}, f32[8,64,256]{2,1,0:T(8,128)}, u32[]{:S(2)}) copy-start(f32[8,64,256]{2,1,0:T(8,128)} %taper.3) | copy-start | bytes 1572868
  2.8 16.6 %collective-permute-start = (bf16[160,1024]{1,0:T(8,128)(2,1)S(1)}, bf16[160,1024]{1,0:T(8,128)(2,1)S(1)}, u32[]{:S(2)}, u32[]{:S(2)}) collective-permute-start(bf16[160,1024]{1,0:T(8,128)(2,1)S(1)} %get-tuple-element.32), channel_id=1, source_target_pairs={{0,4},{4,0},{8,12},{12,8},{16,20},{20,16},{24,28},{28,24},{1,5},{5... | collective-permute-start | bytes 983048 | tf_op jit(solution)/shard_map/ppermute | solution.py:488
  7.3 6.4 %collective-permute-start.1 = (bf16[8,64,128]{2,1,0:T(8,128)(2,1)S(1)}, bf16[8,64,128]{2,1,0:T(8,128)(2,1)S(1)}, u32[]{:S(2)}, u32[]{:S(2)}) collective-permute-start(bf16[8,64,128]{2,1,0:T(8,128)(2,1)S(1)} %get-tuple-element.33), channel_id=1, source_target_pairs={{0,1},{1,2},{2,3},{3,0},{4,5},{5,6},{6,7},{7,4},{8,9},{9,10},{10,1... | collective-permute-start | bytes 393224 | tf_op jit(solution)/shard_map/ppermute | solution.py:433
  8.5 5.2 %collective-permute-start.2 = (bf16[8,64,128]{2,1,0:T(8,128)(2,1)S(1)}, bf16[8,64,128]{2,1,0:T(8,128)(2,1)S(1)}, u32[]{:S(2)}, u32[]{:S(2)}) collective-permute-start(bf16[8,64,128]{2,1,0:T(8,128)(2,1)S(1)} %get-tuple-element.34), channel_id=1, source_target_pairs={{0,3},{1,0},{2,1},{3,2},{4,7},{5,4},{6,5},{7,6},{8,11},{9,8},{10,9... | collective-permute-start | bytes 393224 | tf_op jit(solution)/shard_map/ppermute | solution.py:433
  14.5 15.1 %collective-permute-start.3 = (bf16[160,1152]{1,0:T(8,128)(2,1)S(1)}, bf16[160,1152]{1,0:T(8,128)(2,1)S(1)}, u32[]{:S(2)}, u32[]{:S(2)}) collective-permute-start(bf16[160,1152]{1,0:T(8,128)(2,1)S(1)} %far.1), channel_id=1, source_target_pairs={{0,28},{4,8},{8,4},{12,16},{16,12},{20,24},{24,20},{28,0},{1,29},{... | collective-permute-start | bytes 1105928 | tf_op jit(solution)/shard_map/ppermute | solution.py:512
  17.7 11.8 %collective-permute-start.4 = (bf16[160,128]{1,0:T(8,128)(2,1)S(1)}, bf16[160,128]{1,0:T(8,128)(2,1)S(1)}, u32[]{:S(2)}, u32[]{:S(2)}) collective-permute-start(bf16[160,128]{1,0:T(8,128)(2,1)S(1)} %near_sides.1), channel_id=1, source_target_pairs={{0,4},{4,0},{8,12},{12,8},{16,20},{20,16},{24,28},{28,24},{1,5},{5... | collective-permute-start | bytes 122888 | tf_op jit(solution)/shard_map/ppermute | solution.py:517
  26.0 9.7 %collective-permute-start.7 = (f32[4,32,256]{2,1,0:T(8,128)S(1)}, f32[4,32,256]{2,1,0:T(8,128)S(1)}, u32[]{:S(2)}, u32[]{:S(2)}) collective-permute-start(f32[4,32,256]{2,1,0:T(8,128)S(1)} %get-tuple-element.50), channel_id=1, source_target_pairs={{0,32},{32,0},{64,96},{96,64},{1,33},{33,1},{65,97},{97,65},{2,34}... | collective-permute-start | bytes 393224 | tf_op jit(solution)/shard_map/ppermute | solution.py:437
  35.1 1.6 %collective-permute-start.5 = (f32[4,32,256]{2,1,0:T(8,128)S(1)}, f32[4,32,256]{2,1,0:T(8,128)S(1)}, u32[]{:S(2)}, u32[]{:S(2)}) collective-permute-start(f32[4,32,256]{2,1,0:T(8,128)S(1)} %get-tuple-element.48), channel_id=1, source_target_pairs={{0,32},{32,0},{64,96},{96,64},{1,33},{33,1},{65,97},{97,65},{2,34}... | collective-permute-start | bytes 393224 | tf_op jit(solution)/shard_map/ppermute | solution.py:437
  35.7 3.8 %collective-permute-start.8 = (f32[2,32,256]{2,1,0:T(8,128)S(1)}, f32[2,32,256]{2,1,0:T(8,128)S(1)}, u32[]{:S(2)}, u32[]{:S(2)}) collective-permute-start(f32[2,32,256]{2,1,0:T(8,128)S(1)} %slice_add_fusion), channel_id=1, source_target_pairs={{0,64},{32,96},{64,0},{96,32},{1,65},{33,97},{65,1},{97,33},{2,66}... | collective-permute-start | bytes 196616 | tf_op jit(solution)/shard_map/ppermute | solution.py:442
  36.7 4.2 %collective-permute-start.6 = (f32[2,32,256]{2,1,0:T(8,128)S(1)}, f32[2,32,256]{2,1,0:T(8,128)S(1)}, u32[]{:S(2)}, u32[]{:S(2)}) collective-permute-start(f32[2,32,256]{2,1,0:T(8,128)S(1)} %slice_add_fusion.2), channel_id=1, source_target_pairs={{0,64},{32,96},{64,0},{96,32},{1,65},{33,97},{65,1},{97,33},{2,66}... | collective-permute-start | bytes 196616 | tf_op jit(solution)/shard_map/ppermute | solution.py:442

commit v9 on v6

--- a/solution.py
+++ b/solution.py
@@ -29,36 +29,31 @@
     return hi, (value - hi.astype(F32)).astype(BF16)
 
 
-def target_column(shape, first, members, cols):
+def target_column(lane, first, members, cols):
     chunks = LANES // members
     fine = (cols + 2 * HALO) // chunks
-    lane = lax.broadcasted_iota(jnp.int32, shape, 1)
-    return fine * (lane % chunks) + first - HALO, lane // chunks
-
-
-def fill_selectors(to_fields, to_weights, to_sides, back, members, cols):
+    return fine * (lane & (chunks - 1)) + first - HALO, lane >> (chunks.bit_length() - 1)
+
+
+def fill_selectors(wanted, to_fields, to_weights, to_sides, back, members, cols):
     fine = back.shape[0] // LANES
     nowhere = -4 * LANES
 
     def mark(hit):
         return jnp.where(hit, 1.0, 0.0).astype(BF16)
 
-    for first in range(fine):
+    for first in wanted:
         lanes = slice(first * LANES, (first + 1) * LANES)
-        shape = (cols, LANES)
-        column, member = target_column(shape, first, members, cols)
-        row = lax.broadcasted_iota(jnp.int32, shape, 0)
-        here = row == column
+        column, member = target_column(lax.broadcasted_iota(jnp.int32, (1, LANES), 1), first, members, cols)
+        marked = mark(lax.broadcasted_iota(jnp.int32, (cols, LANES), 0) == column)
         for m in range(members):
-            to_fields[m * cols : (m + 1) * cols, lanes] = mark(here & (member == m))
+            to_fields[m * cols : (m + 1) * cols, lanes] = marked * mark(member == m)
         for part in range(2):
-            to_weights[part * cols : (part + 1) * cols, lanes] = mark(here)
+            to_weights[part * cols : (part + 1) * cols, lanes] = marked
         for ref, base, count, offsets in (
             (to_fields, members * cols, LANES, (0,)), (to_sides, 0, 2 * LANES, (0, LANES // 2)),
         ):
-            shape = (count, LANES)
-            column, member = target_column(shape, first, members, cols)
-            row = lax.broadcasted_iota(jnp.int32, shape, 0)
+            row = lax.broadcasted_iota(jnp.int32, (count, LANES), 0)
             after = column - cols + count // 2
             at = jnp.where(column < 0, column + HALO, jnp.where(column >= cols, after, nowhere)) + HALO * member
             hit = row == at
@@ -66,8 +61,7 @@
                 hit = hit | (row == at + offset)
             ref[base : base + count, lanes] = mark(hit)
         shape = (LANES, cols)
-        lane = lax.broadcasted_iota(jnp.int32, shape, 0)
-        column = fine * (lane % (LANES // members)) + first - HALO
+        column, _ = target_column(lax.broadcasted_iota(jnp.int32, shape, 0), first, members, cols)
         back[lanes, :] = mark(lax.broadcasted_iota(jnp.int32, shape, 1) == column)
 
 
@@ -107,7 +101,11 @@
             put(pair, to, rest, HALO)
 
 
-def start_kernel(place, p_hbm, increment_hbm, taper_hbm, to_near, to_left, to_right, p, g, taper, increment, sems):
+def start_kernel(
+    place, p_hbm, increment_hbm, taper_hbm,
+    to_near, to_left, to_right, p, g, to_fields, to_weights, to_sides, back,
+    taper, increment, sems,
+):
     members, levels, rows, cols = p.shape
     copies = []
     for i in (0, rows // HALO - 1, *range(1, rows // HALO - 1)):
@@ -120,6 +118,7 @@
     for _, group in copies:
         for copy in group:
             copy.start()
+    fill_selectors(range(back.shape[0] // LANES), to_fields, to_weights, to_sides, back, members, cols)
 
     def packed(pick, column, shift):
         products = [p[m, :, pick, column].astype(F32) * g[:, pick, column] for m in range(members)]
@@ -232,10 +231,9 @@
     return jnp.dot(a, b, preferred_element_type=F32)
 
 
-def prepare_kernel(p, g, own_values, own_products, to_fields, to_sides, back, fields, weights, to_weights):
+def prepare_kernel(p, g, to_fields, to_weights, own_values, own_products, fields, weights):
     members, levels, rows, cols = p.shape
-    fine = back.shape[0] // LANES
-    fill_selectors(to_fields, to_weights, to_sides, back, members, cols)
+    fine = to_fields.shape[1] // LANES
     for i in range(rows // HALO):
         pick = slice(i * HALO, (i + 1) * HALO)
         out = slice(i * HALO * levels, (i + 1) * HALO * levels)
@@ -478,9 +476,15 @@
         mem // 2,
     ])
 
-    to_near, to_left, to_right, p, g = call(
+    to_near, to_left, to_right, p, g, to_fields, to_weights, to_sides, back = call(
         start_kernel, "start",
-        (strip(0), pack, pack, shape(perturbations.shape, BF16), whole),
+        (
+            strip(0), pack, pack, shape(perturbations.shape, BF16), whole,
+            shape((members * cols + LANES, fine * LANES), BF16),
+            shape((2 * cols, fine * LANES), BF16),
+            shape((2 * LANES, fine * LANES), BF16),
+            shape((fine * LANES, cols), BF16),
+        ),
         (place, *(pltpu.with_memory_space_constraint(a, pltpu.HBM) for a in (perturbations, increment, taper_norm))),
         (pltpu.VMEM(whole.shape, F32), pltpu.VMEM(whole.shape, F32), pltpu.SemaphoreType.DMA((rows // HALO, 3))),
         specs=[smem] + [hbm] * 3,
@@ -490,22 +494,12 @@
     right = shifted(to_left, "lon", -1, True)
 
     values = shape((rows, fine, *tile), F32)
-    own_values, own_products, to_fields, to_sides, back = call(
+    own_values, own_products = call(
         prepare_kernel, "prepare",
-        (
-            values, values,
-            shape((members * cols + LANES, fine * LANES), BF16),
-            shape((2 * LANES, fine * LANES), BF16),
-            shape((fine * LANES, cols), BF16),
-        ),
-        (p, g),
-        (
-            pltpu.VMEM((rows * levels, members * cols), BF16),
-            pltpu.VMEM((rows * levels, 2 * cols), BF16),
-            pltpu.VMEM((2 * cols, fine * LANES), BF16),
-        ),
+        (values, values),
+        (p, g, to_fields, to_weights),
+        (pltpu.VMEM((rows * levels, members * cols), BF16), pltpu.VMEM((rows * levels, 2 * cols), BF16)),
     )
-
     p, g, own_values = lax.optimization_barrier((p, g, own_values))
     (to_far,) = call(far_kernel, "far", (strip(1),), (place, p, g, left, right), specs=[smem] + [vmem] * 4)
     far = lax.ppermute(to_far, "lat", [(i, (i + 1 - 2 * (1 - i % 2)) % count) for i in range(count)])

time: 40.8 us -> 43.1 us (1.056)
  the two profiles are of different devices: /device:TPU:1 before, /device:TPU:84 now
where the time goes in v9:
time: 43.1 us; the launch traced here: 43 us
  Pallas kernels  18.2 us (42%)
  waiting for transfers between devices  13.3 us (31%)
  starting transfers between devices  10.5 us (24%)
  other arithmetic  0.79 us (2%)
    pallas_call x6, Pallas kernels, call(): pl.pallas_call(kernel, out_shape=tuple(outs), in_specs=specs or [vmem] *...  18.2 us
    ppermute x1, waiting for transfers between devices, local(): near = lax.ppermute(to_near, 'lat', [(i, i ^ 1) for i in range(count)])  7.59 us
    ppermute x1, starting transfers between devices, local(): lax.ppermute(to_far, 'lat', [(i, (i + 1 - 2 * (1 - i % 2)) % count) for i...  4.25 us
    ppermute x4, starting transfers between devices, shifted(): return lax.ppermute(value, axis, pairs)  4.18 us
    ppermute x2, waiting for transfers between devices, over_plane(): return here + lax.ppermute(there, 'mem', [(i, i ^ 2) for i in range(4)])  3.53 us
    ppermute x4, waiting for transfers between devices, shifted(): return lax.ppermute(value, axis, pairs)  1.32 us
    ppermute x2, starting transfers between devices, over_plane(): return here + lax.ppermute(there, 'mem', [(i, i ^ 2) for i in range(4)])  1.31 us
    ppermute x2, waiting for transfers between devices, over_core(): got = lax.ppermute(send, 'mem', [(i, i ^ 1) for i in range(4)])  0.88 us
  transfers between devices with their start and end apart: 10, of which 6 were waited for; matrix products, arithmetic and copies ran while one was open for 0% of the time, Pallas kernels for 36%

profile of v9, /device:TPU:84, one launch (start us, length us, event | category | flops | bytes accessed | tf_op | source)
XLA Modules:
  0.0 43.0 jit_solution(2333464162989556381)
XLA Ops:
  0.0 0.1 pad_add_fusion.place
  0.1 2.7 %start.1 = (bf16[160,1024]{1,0:T(8,128)(2,1)S(1)}, bf16[8,64,128]{2,1,0:T(8,128)(2,1)S(1)}, bf16[8,64,128]{2,1,0:T(8,128)(2,1)S(1)}, bf16[4,8,64,256]{3,2,1,0:T(...) custom-call(s32[4]{0:T(128)S(1)} %pad_add_fusion.place, ...), custom_call_target="tpu_custom_call" | custom-call | tf_op jit(solution)/shard_map/start/pallas_call | solution.py:453
  2.8 0.1 collective-permute-start
  2.9 1.3 %collective-permute-start.1 = (bf16[8,64,128]{2,1,0:T(8,128)(2,1)S(1)}, bf16[8,64,128]{2,1,0:T(8,128)(2,1)S(1)}, u32[]{:S(2)}, u32[]{:S(2)}) collective-permute-start(bf16[8,64,128]{2,1,0:T(8,128)(2,1)S(1)} %get-tuple-element.37), channel_id=1, source_target_pairs={{0,1},{1,2},{2,3},{3,0},{4,5},{5,6},{6,7},{7,4},{8,9},{9,10},{10,1... | collective-permute-start | bytes 393224 | tf_op jit(solution)/shard_map/ppermute | solution.py:431
  4.2 0.8 %collective-permute-start.2 = (bf16[8,64,128]{2,1,0:T(8,128)(2,1)S(1)}, bf16[8,64,128]{2,1,0:T(8,128)(2,1)S(1)}, u32[]{:S(2)}, u32[]{:S(2)}) collective-permute-start(bf16[8,64,128]{2,1,0:T(8,128)(2,1)S(1)} %get-tuple-element.38), channel_id=1, source_target_pairs={{0,3},{1,0},{2,1},{3,2},{4,7},{5,4},{6,5},{7,6},{8,11},{9,8},{10,9... | collective-permute-start | bytes 393224 | tf_op jit(solution)/shard_map/ppermute | solution.py:431
  5.0 2.8 %prepare.1 = (f32[64,9,8,128]{3,2,1,0:T(8,128)S(1)}, f32[64,9,8,128]{3,2,1,0:T(8,128)S(1)}) custom-call(bf16[4,8,64,256]{3,2,1,0:T(8,128)(2,1)S(1)} %get-tuple-element.35.p, f32[8,64,256]{2,1,0:T(8,128)S(1)} %get-tuple-element.36.g, bf16[1152,1152]{1,0:T(8,128)(2,1)S(1)} %get-tuple-element.32.to_fields, bf16[512,1152]{1,0:T(8,128)(2,1)S(1)} %get-tuple-element.33.to_weights), custom_call_target="tpu_custom_call" | custom-call | tf_op jit(solution)/shard_map/prepare/pallas_call | solution.py:453
  7.8 0.4 collective-permute-done.1.left
  8.2 0.9 %collective-permute-done.2.right = bf16[8,64,128]{2,1,0:T(8,128)(2,1)S(1)} collective-permute-done((bf16[8,64,128]{2,1,0:T(8,128)(2,1)S(1)}, bf16[8,64,128]{2,1,0:T(8,128)(2,1)S(1)}, u32[]{:S(2)}, u32[]{:S(2)}) %collective-permute-start.2) | collective-permute-done | bytes 131104 | tf_op jit(solution)/shard_map/ppermute | solution.py:431
  9.1 0.8 %far.1 = bf16[160,1152]{1,0:T(8,128)(2,1)S(1)} custom-call(s32[4]{0:T(128)S(1)} %pad_add_fusion.place, bf16[4,8,64,256]{3,2,1,0:T(8,128)(2,1)S(1)} %get-tuple-element.35.p, f32[8,64,256]{2,1,0:T(8,128)S(1)} %get-tuple-element.36.g, bf16[8,64,128]{2,1,0:T(8,128)(2,1)S(1)} %collective-permute-done.1.left, bf16[8,64,128]{2,1,0:T(8,128)(2,1)S(1)} %collective-permute-done.2.right), custom_call_target="tpu_custom_call" | custom-call | tf_op jit(solution)/shard_map/far/pallas_call | solution.py:453
  9.9 4.2 %collective-permute-start.3 = (bf16[160,1152]{1,0:T(8,128)(2,1)S(1)}, bf16[160,1152]{1,0:T(8,128)(2,1)S(1)}, u32[]{:S(2)}, u32[]{:S(2)}) collective-permute-start(bf16[160,1152]{1,0:T(8,128)(2,1)S(1)} %far.1), channel_id=1, source_target_pairs={{0,28},{4,8},{8,4},{12,16},{16,12},{20,24},{24,20},{28,0},{1,29},{... | collective-permute-start | bytes 1105928 | tf_op jit(solution)/shard_map/ppermute | solution.py:505
  14.1 7.6 %collective-permute-done.strip.near = bf16[160,1024]{1,0:T(8,128)(2,1)S(1)} collective-permute-done((bf16[160,1024]{1,0:T(8,128)(2,1)S(1)}, bf16[160,1024]{1,0:T(8,128)(2,1)S(1)}, u32[]{:S(2)}, u32[]{:S(2)}) %collective-permute-start) | collective-permute-done | bytes 327712 | tf_op jit(solution)/shard_map/ppermute | solution.py:492
  21.7 0.2 corners.1
  21.9 0.1 collective-permute-start.5
  22.0 2.0 %collective-permute-start.4 = (bf16[160,128]{1,0:T(8,128)(2,1)S(1)}, bf16[160,128]{1,0:T(8,128)(2,1)S(1)}, u32[]{:S(2)}, u32[]{:S(2)}) collective-permute-start(bf16[160,128]{1,0:T(8,128)(2,1)S(1)} %get-tuple-element.40), channel_id=1, source_target_pairs={{0,1},{1,2},{2,3},{3,0},{4,5},{5,6},{6,7},{7,4},{8,9},{9,10},{10,1... | collective-permute-start | bytes 122888 | tf_op jit(solution)/shard_map/ppermute | solution.py:431
  24.1 6.4 %inner.1 = (f32[4,32,256]{2,1,0:T(8,128)S(1)}, f32[4,32,256]{2,1,0:T(8,128)S(1)}, f32[2,8,4,13,8,128]{5,4,3,2,1,0:T(8,128)S(1)}, f32[2,16,9,8,128]{4,3,2,1,0:T(8,128)S(1)}) custom-call(s32[4]{0:T(128)S(1)} %pad_add_fusion.place, f32[64,9,8,128]{3,2,1,0:T(8,128)S(1)} %get-tuple-element.43.values, f32[64,9,8,128]{3,2,1,0:T(8,128)S(1)} %get-tuple-element.44.own_products, ...), custom_call_target="tpu_custom_call" | custom-call | flops 4000000000 | bytes 1048576 | tf_op jit(solution)/shard_map/inner/pallas_call | solution.py:453
  30.5 0.1 collective-permute-start.8
  30.6 5.4 %outer.1 = (f32[4,32,256]{2,1,0:T(8,128)S(1)}, f32[4,32,256]{2,1,0:T(8,128)S(1)}) custom-call(s32[4]{0:T(128)S(1)} %pad_add_fusion.place, f32[8,64,256]{2,1,0:T(8,128)S(1)} %copy-done, bf16[160,1024]{1,0:T(8,128)(2,1)S(1)} %collective-permute-done.strip.near, bf16[160,1152]{1,0:T(8,128)(2,1)S(1)} %collective-permute-done.3.far, ...), custom_call_target="tpu_custom_call" | custom-call | flops 4000000000 | bytes 1048576 | tf_op jit(solution)/shard_map/outer/pallas_call | solution.py:453
  36.0 0.6 %collective-permute-start.6 = (f32[4,32,256]{2,1,0:T(8,128)S(1)}, f32[4,32,256]{2,1,0:T(8,128)S(1)}, u32[]{:S(2)}, u32[]{:S(2)}) collective-permute-start(f32[4,32,256]{2,1,0:T(8,128)S(1)} %get-tuple-element.50), channel_id=1, source_target_pairs={{0,32},{32,0},{64,96},{96,64},{1,33},{33,1},{65,97},{97,65},{2,34}... | collective-permute-start | bytes 393224 | tf_op jit(solution)/shard_map/ppermute | solution.py:435
  36.5 0.1 collective-permute-start.9
  36.6 0.9 %collective-permute-done.6 = f32[4,32,256]{2,1,0:T(8,128)S(1)} collective-permute-done((f32[4,32,256]{2,1,0:T(8,128)S(1)}, f32[4,32,256]{2,1,0:T(8,128)S(1)}, u32[]{:S(2)}, u32[]{:S(2)}) %collective-permute-start.6) | collective-permute-done | bytes 131104 | tf_op jit(solution)/shard_map/ppermute | solution.py:435
  37.5 1.2 %collective-permute-start.7 = (f32[2,32,256]{2,1,0:T(8,128)S(1)}, f32[2,32,256]{2,1,0:T(8,128)S(1)}, u32[]{:S(2)}, u32[]{:S(2)}) collective-permute-start(f32[2,32,256]{2,1,0:T(8,128)S(1)} %slice_add_fusion.2), channel_id=1, source_target_pairs={{0,64},{32,96},{64,0},{96,32},{1,65},{33,97},{65,1},{97,33},{2,66}... | collective-permute-start | bytes 196616 | tf_op jit(solution)/shard_map/ppermute | solution.py:440
  38.7 2.6 %collective-permute-done.9 = f32[2,32,256]{2,1,0:T(8,128)S(1)} collective-permute-done((f32[2,32,256]{2,1,0:T(8,128)S(1)}, f32[2,32,256]{2,1,0:T(8,128)S(1)}, u32[]{:S(2)}, u32[]{:S(2)}) %collective-permute-start.9) | collective-permute-done | bytes 65568 | tf_op jit(solution)/shard_map/ppermute | solution.py:440
  41.3 1.0 %collective-permute-done.7 = f32[2,32,256]{2,1,0:T(8,128)S(1)} collective-permute-done((f32[2,32,256]{2,1,0:T(8,128)S(1)}, f32[2,32,256]{2,1,0:T(8,128)S(1)}, u32[]{:S(2)}, u32[]{:S(2)}) %collective-permute-start.7) | collective-permute-done | bytes 65568 | tf_op jit(solution)/shard_map/ppermute | solution.py:440
  42.3 0.7 %pad_maximum_fusion = f32[2,64,256]{2,1,0:T(8,128)} fusion(f32[2,16,256]{2,1,0:T(8,128)S(1)} %get-tuple-element.54, f32[2,32,256]{2,1,0:T(8,128)S(1)} %fusion, f32[2,16,256]{2,1,0:T(8,128)S(1)} %get-tuple-element.53), kind=kLoop, calls=%fused_computation | loop fusion | flops 65536 | bytes 262144 | tf_op jit(solution)/shard_map/concatenate | solution.py:544
  (14 shorter events, 0.1 us)
Async XLA Ops:
  2.8 18.9 %collective-permute-start = (bf16[160,1024]{1,0:T(8,128)(2,1)S(1)}, bf16[160,1024]{1,0:T(8,128)(2,1)S(1)}, u32[]{:S(2)}, u32[]{:S(2)}) collective-permute-start(bf16[160,1024]{1,0:T(8,128)(2,1)S(1)} %get-tuple-element.29), channel_id=1, source_target_pairs={{0,4},{4,0},{8,12},{12,8},{16,20},{20,16},{24,28},{28,24},{1,5},{5... | collective-permute-start | bytes 983048 | tf_op jit(solution)/shard_map/ppermute | solution.py:492
  2.9 5.3 %collective-permute-start.1 = (bf16[8,64,128]{2,1,0:T(8,128)(2,1)S(1)}, bf16[8,64,128]{2,1,0:T(8,128)(2,1)S(1)}, u32[]{:S(2)}, u32[]{:S(2)}) collective-permute-start(bf16[8,64,128]{2,1,0:T(8,128)(2,1)S(1)} %get-tuple-element.37), channel_id=1, source_target_pairs={{0,1},{1,2},{2,3},{3,0},{4,5},{5,6},{6,7},{7,4},{8,9},{9,10},{10,1... | collective-permute-start | bytes 393224 | tf_op jit(solution)/shard_map/ppermute | solution.py:431
  4.2 5.0 %collective-permute-start.2 = (bf16[8,64,128]{2,1,0:T(8,128)(2,1)S(1)}, bf16[8,64,128]{2,1,0:T(8,128)(2,1)S(1)}, u32[]{:S(2)}, u32[]{:S(2)}) collective-permute-start(bf16[8,64,128]{2,1,0:T(8,128)(2,1)S(1)} %get-tuple-element.38), channel_id=1, source_target_pairs={{0,3},{1,0},{2,1},{3,2},{4,7},{5,4},{6,5},{7,6},{8,11},{9,8},{10,9... | collective-permute-start | bytes 393224 | tf_op jit(solution)/shard_map/ppermute | solution.py:431
  7.8 16.2 %copy-start.1 = (f32[8]{0:T(128)S(1)}, f32[8]{0:T(128)}, u32[]{:S(2)}) copy-start(f32[8]{0:T(128)} %param.7) | copy-start | bytes 100
  7.8 16.3 %copy-start = (f32[8,64,256]{2,1,0:T(8,128)S(1)}, f32[8,64,256]{2,1,0:T(8,128)}, u32[]{:S(2)}) copy-start(f32[8,64,256]{2,1,0:T(8,128)} %taper.3) | copy-start | bytes 1572868
  9.9 20.7 %collective-permute-start.3 = (bf16[160,1152]{1,0:T(8,128)(2,1)S(1)}, bf16[160,1152]{1,0:T(8,128)(2,1)S(1)}, u32[]{:S(2)}, u32[]{:S(2)}) collective-permute-start(bf16[160,1152]{1,0:T(8,128)(2,1)S(1)} %far.1), channel_id=1, source_target_pairs={{0,28},{4,8},{8,4},{12,16},{16,12},{20,24},{24,20},{28,0},{1,29},{... | collective-permute-start | bytes 1105928 | tf_op jit(solution)/shard_map/ppermute | solution.py:505
  21.9 8.7 %collective-permute-start.5 = (bf16[160,128]{1,0:T(8,128)(2,1)S(1)}, bf16[160,128]{1,0:T(8,128)(2,1)S(1)}, u32[]{:S(2)}, u32[]{:S(2)}) collective-permute-start(bf16[160,128]{1,0:T(8,128)(2,1)S(1)} %get-tuple-element.41), channel_id=1, source_target_pairs={{0,3},{1,0},{2,1},{3,2},{4,7},{5,4},{6,5},{7,6},{8,11},{9,8},{10,9... | collective-permute-start | bytes 122888 | tf_op jit(solution)/shard_map/ppermute | solution.py:431
  22.0 8.6 %collective-permute-start.4 = (bf16[160,128]{1,0:T(8,128)(2,1)S(1)}, bf16[160,128]{1,0:T(8,128)(2,1)S(1)}, u32[]{:S(2)}, u32[]{:S(2)}) collective-permute-start(bf16[160,128]{1,0:T(8,128)(2,1)S(1)} %get-tuple-element.40), channel_id=1, source_target_pairs={{0,1},{1,2},{2,3},{3,0},{4,5},{5,6},{6,7},{7,4},{8,9},{9,10},{10,1... | collective-permute-start | bytes 122888 | tf_op jit(solution)/shard_map/ppermute | solution.py:431
  30.5 6.1 %collective-permute-start.8 = (f32[4,32,256]{2,1,0:T(8,128)S(1)}, f32[4,32,256]{2,1,0:T(8,128)S(1)}, u32[]{:S(2)}, u32[]{:S(2)}) collective-permute-start(f32[4,32,256]{2,1,0:T(8,128)S(1)} %get-tuple-element.52), channel_id=1, source_target_pairs={{0,32},{32,0},{64,96},{96,64},{1,33},{33,1},{65,97},{97,65},{2,34}... | collective-permute-start | bytes 393224 | tf_op jit(solution)/shard_map/ppermute | solution.py:435
  36.0 1.5 %collective-permute-start.6 = (f32[4,32,256]{2,1,0:T(8,128)S(1)}, f32[4,32,256]{2,1,0:T(8,128)S(1)}, u32[]{:S(2)}, u32[]{:S(2)}) collective-permute-start(f32[4,32,256]{2,1,0:T(8,128)S(1)} %get-tuple-element.50), channel_id=1, source_target_pairs={{0,32},{32,0},{64,96},{96,64},{1,33},{33,1},{65,97},{97,65},{2,34}... | collective-permute-start | bytes 393224 | tf_op jit(solution)/shard_map/ppermute | solution.py:435
  36.5 4.8 %collective-permute-start.9 = (f32[2,32,256]{2,1,0:T(8,128)S(1)}, f32[2,32,256]{2,1,0:T(8,128)S(1)}, u32[]{:S(2)}, u32[]{:S(2)}) collective-permute-start(f32[2,32,256]{2,1,0:T(8,128)S(1)} %slice_add_fusion), channel_id=1, source_target_pairs={{0,64},{32,96},{64,0},{96,32},{1,65},{33,97},{65,1},{97,33},{2,66}... | collective-permute-start | bytes 196616 | tf_op jit(solution)/shard_map/ppermute | solution.py:440
  37.5 4.8 %collective-permute-start.7 = (f32[2,32,256]{2,1,0:T(8,128)S(1)}, f32[2,32,256]{2,1,0:T(8,128)S(1)}, u32[]{:S(2)}, u32[]{:S(2)}) collective-permute-start(f32[2,32,256]{2,1,0:T(8,128)S(1)} %slice_add_fusion.2), channel_id=1, source_target_pairs={{0,64},{32,96},{64,0},{96,32},{1,65},{33,97},{65,1},{97,33},{2,66}... | collective-permute-start | bytes 196616 | tf_op jit(solution)/shard_map/ppermute | solution.py:440
